TPU v7x, 256 devices: a whole 4x4x8 slice. The times are simulated.
256 devices in a mesh: contact: 32 (over y, x, core), body: 8 (over z).
Axes of the slice: x: 4, y: 4, z: 8, core: 2. Of those that a mesh axis runs over, the one named last changes fastest.
Arguments:
- jacobian: bfloat16 [4096, 2, 384, 384], P(('contact', 'body')), may hold values from -0.21875 to 0.21875
- tile_block: int32 [4096, 2], P(('contact', 'body')), may hold values from 0 to 31
- tile_count: int32 [256], P(('contact', 'body')), may hold values from 8 to 16, as said below
- vel_free: float32 [256, 384], P('body'), may hold values from -6 to 6
- inv_mass: float32 [256, 384], P('body'), may hold values from 0.25 to 2
- bias: float32 [4096, 384], P(('contact', 'body')), may hold values from -6 to 6
- step_scale: float32 [4096, 384], P(('contact', 'body')), may hold values from 0.05 to 0.5
- friction: float32 [4096, 128], P(('contact', 'body')), may hold values from 0.2 to 1
- impulse_start: float32 [4096, 384], P(('contact', 'body')), may hold values from -6 to 6
Outputs:
- impulse: float32 [4096, 384], P(('contact', 'body'))
- velocity: float32 [256, 384], P('body')
Inputs may be any that keep to these rules, and one draw needn't show every extreme that they name: `tile_count`: some device has all 16 tile slots live in every draw.
All inputs are finite; a program needn't handle non-finite values.
Results may differ from a plain program's by a relative error of at most 0.0062.
Values may be sent and summed in bfloat16 or wider, within the bound.
A program may use at most 64 MiB of HBM per device.

v0:
```python
import jax
import jax.numpy as jnp
from jax import lax
from jax.sharding import PartitionSpec as P

ITERS = 2


def shifted(value, axis, steps):
    count = lax.axis_size(axis)
    pairs = [(source, (source + steps) % count) for source in range(count)]
    return lax.ppermute(value, axis, pairs)


def project(trial, friction, contacts):
    normal = trial[:, :contacts]
    first = trial[:, contacts : 2 * contacts]
    second = trial[:, 2 * contacts :]
    tangent = jnp.sqrt(first * first + second * second)
    inside = tangent <= friction * normal
    below = friction * tangent <= -normal
    moved = (normal + friction * tangent) / (1.0 + friction * friction)
    safe = jnp.where(inside | below, 1.0, tangent)
    factor = jnp.where(inside, 1.0, jnp.where(below, 0.0, friction * moved / safe))
    new_normal = jnp.where(inside, normal, jnp.where(below, 0.0, moved))
    return jnp.concatenate([new_normal, first * factor, second * factor], axis=1)


def per_device(
    jacobian, tile_block, tile_count, vel_free, inv_mass, bias, step_scale, friction, impulse_start
):
    tiles_here = jacobian.shape[0]
    slab_blocks = vel_free.shape[0]
    contacts = friction.shape[1]
    order = jnp.arange(tiles_here, dtype=jnp.int32)
    mask = (order < tile_count[0]).astype(jnp.float32)[:, None]
    span = jnp.arange(slab_blocks, dtype=jnp.int32)
    pick_own = (tile_block[:, 0:1] == span[None, :]).astype(jnp.float32)
    pick_next = (tile_block[:, 1:2] == span[None, :]).astype(jnp.float32)
    pick_own_b = pick_own.astype(jnp.bfloat16)
    pick_next_b = pick_next.astype(jnp.bfloat16)

    def merged_partials(lam):
        lamb = lam.astype(jnp.bfloat16)
        push = jnp.einsum("tkbc,tc->tkb", jacobian, lamb, preferred_element_type=jnp.float32)
        own = jnp.einsum("ts,tb->sb", pick_own, push[:, 0], precision=lax.Precision.HIGHEST)
        later = jnp.einsum("ts,tb->sb", pick_next, push[:, 1], precision=lax.Precision.HIGHEST)
        return own + shifted(later, "body", 1)

    def slab_total(lam):
        return lax.psum(merged_partials(lam), "contact")

    lam = impulse_start * mask
    for sweep in range(ITERS):
        total = slab_total(lam)
        velb = (vel_free + inv_mass * total).astype(jnp.bfloat16)
        velb_next = shifted(velb, "body", -1)
        rows_own = jnp.dot(pick_own_b, velb, preferred_element_type=jnp.float32).astype(
            jnp.bfloat16
        )
        rows_next = jnp.dot(pick_next_b, velb_next, preferred_element_type=jnp.float32).astype(
            jnp.bfloat16
        )
        rows = jnp.stack([rows_own, rows_next], axis=1)
        rel = jnp.einsum("tkbc,tkb->tc", jacobian, rows, preferred_element_type=jnp.float32) + bias
        lam = project(lam - step_scale * rel, friction, contacts) * mask
    total = slab_total(lam)
    velocity = vel_free + inv_mass * total
    return (lam, velocity)


def solution(mesh):
    placed = (
        P(("contact", "body"), None, None, None),
        P(("contact", "body"), None),
        P(("contact", "body")),
        P("body", None),
        P("body", None),
        P(("contact", "body"), None),
        P(("contact", "body"), None),
        P(("contact", "body"), None),
        P(("contact", "body"), None),
    )
    return jax.shard_map(
        per_device,
        mesh=mesh,
        in_specs=placed,
        out_specs=(P(("contact", "body"), None), P("body", None)),
        check_vma=False,
    )
```

profile of v0, /device:TPU:1, one launch (start us, length us, event | category | flops | bytes accessed | tf_op | source)
XLA Modules:
  0.0 433.3 jit_solution(17397203647870327549)
XLA Ops:
  1.3 0.8 slice_bitcast_fusion.1
  2.1 0.8 fusion.35
  2.9 6.2 %fusion.31 = f32[16,1,2,384]{3,1,2,0:T(1,128)S(1)} fusion(bf16[16,2,384,384]{3,2,1,0:T(8,128)(2,1)} %param.9, bf16[16,384,1,1]{1,0,2,3:T(8,128)(2,1)S(1)} %fusion.35), kind=kOutput, calls=%fused_computation.50 | convolution fusion | flops 9437184 | bytes 9498624 | tf_op jit(solution)/shard_map/tkbc,tc->tkb/dot_general | solution.py:45
  9.3 0.3 fusion.18
  9.5 2.5 collective-permute-start
  12.1 5.4 %collective-permute-done = f32[32,384]{1,0:T(8,128)S(1)} collective-permute-done((f32[32,384]{1,0:T(8,128)S(1)}, f32[32,384]{1,0:T(8,128)S(1)}, u32[]{:S(2)}, u32[]{:S(2)}) %collective-permute-start) | collective-permute-done | bytes 49184 | tf_op jit(solution)/shard_map/ppermute | solution.py:12
  17.5 0.3 convolution_add_fusion.2
  17.8 123.4 %psum.21 = f32[32,384]{1,0:T(8,128)S(1)} all-reduce(f32[32,384]{1,0:T(8,128)S(1)} %convolution_add_fusion.2), channel_id=1, replica_groups=mesh['contact'=32,'body'=8] {'contact'}, use_global_device_ids=true, to_apply=%region_0.0 | all-reduce | flops 12288 | bytes 98304 | tf_op jit(solution)/shard_map/psum | solution.py:51
  141.2 1.5 collective-permute-start.1
  142.8 0.2 fusion
  143.0 1.0 collective-permute-done.1
  144.0 0.2 fusion.1
  144.2 5.0 %fusion.6 = f32[16,1,384,1]{2,1,3,0:T(1,128)S(1)} fusion(bf16[16,2,384,384]{3,2,1,0:T(8,128)(2,1)} %param.9, bf16[16,2,384,1]{2,0,1,3:T(8,128)(2,1)S(1)} %maximum_bitcast_fusion), kind=kOutput, calls=%fused_computation.15 | convolution fusion | flops 9437184 | bytes 9486336 | tf_op jit(solution)/shard_map/tkbc,tkb->tc/dot_general | solution.py:65
  149.5 6.2 %fusion.29 = f32[16,1,2,384]{3,1,2,0:T(1,128)S(1)} fusion(bf16[16,2,384,384]{3,2,1,0:T(8,128)(2,1)} %param.9, bf16[16,384,1,1]{1,0,2,3:T(8,128)(2,1)S(1)} %fusion.34), kind=kOutput, calls=%fused_computation.48 | convolution fusion | flops 9437184 | bytes 9498624 | tf_op jit(solution)/shard_map/tkbc,tc->tkb/dot_general | solution.py:45
  155.8 0.3 fusion.13
  156.0 0.1 collective-permute-start.2
  156.1 4.4 %collective-permute-done.2 = f32[32,384]{1,0:T(8,128)S(1)} collective-permute-done((f32[32,384]{1,0:T(8,128)S(1)}, f32[32,384]{1,0:T(8,128)S(1)}, u32[]{:S(2)}, u32[]{:S(2)}) %collective-permute-start.2) | collective-permute-done | bytes 49184 | tf_op jit(solution)/shard_map/ppermute | solution.py:12
  160.6 0.3 convolution_add_fusion.1
  160.9 125.8 %psum.22 = f32[32,384]{1,0:T(8,128)S(1)} all-reduce(f32[32,384]{1,0:T(8,128)S(1)} %convolution_add_fusion.1), channel_id=1, replica_groups=mesh['contact'=32,'body'=8] {'contact'}, use_global_device_ids=true, to_apply=%region_1.2 | all-reduce | flops 12288 | bytes 98304 | tf_op jit(solution)/shard_map/psum | solution.py:51
  286.7 1.5 collective-permute-start.3
  288.2 0.2 fusion.2
  288.4 1.0 collective-permute-done.3
  289.4 0.2 fusion.3
  289.6 5.0 %fusion.4 = f32[16,1,384,1]{2,1,3,0:T(1,128)S(1)} fusion(bf16[16,2,384,384]{3,2,1,0:T(8,128)(2,1)} %param.9, bf16[16,2,384,1]{2,0,1,3:T(8,128)(2,1)S(1)} %maximum_bitcast_fusion.1), kind=kOutput, calls=%fused_computation.12 | convolution fusion | flops 9437184 | bytes 9486336 | tf_op jit(solution)/shard_map/tkbc,tkb->tc/dot_general | solution.py:65
  294.8 0.7 convert_bitcast_fusion
  295.5 6.2 %fusion.27 = f32[16,1,2,384]{3,1,2,0:T(1,128)S(1)} fusion(bf16[16,2,384,384]{3,2,1,0:T(8,128)(2,1)} %param.9, bf16[16,384,1,1]{1,0,2,3:T(8,128)(2,1)S(1)} %get-tuple-element.2), kind=kOutput, calls=%fused_computation.46 | convolution fusion | flops 9437184 | bytes 9498624 | tf_op jit(solution)/shard_map/tkbc,tc->tkb/dot_general | solution.py:45
  301.8 0.3 fusion.8
  302.1 0.1 collective-permute-start.4
  302.2 4.4 %collective-permute-done.4 = f32[32,384]{1,0:T(8,128)S(1)} collective-permute-done((f32[32,384]{1,0:T(8,128)S(1)}, f32[32,384]{1,0:T(8,128)S(1)}, u32[]{:S(2)}, u32[]{:S(2)}) %collective-permute-start.4) | collective-permute-done | bytes 49184 | tf_op jit(solution)/shard_map/ppermute | solution.py:12
  306.6 0.3 convolution_add_fusion
  306.9 125.8 %psum.23 = f32[32,384]{1,0:T(8,128)S(1)} all-reduce(f32[32,384]{1,0:T(8,128)S(1)} %convolution_add_fusion), channel_id=1, replica_groups=mesh['contact'=32,'body'=8] {'contact'}, use_global_device_ids=true, to_apply=%region_2.3 | all-reduce | flops 12288 | bytes 98304 | tf_op jit(solution)/shard_map/psum | solution.py:51
  432.7 0.6 multiply_add_fusion
  (30 shorter events, 0.6 us)
Async XLA Ops:
  0.6 140.6 %copy-start.1 = (f32[32,384]{1,0:T(8,128)S(1)}, f32[32,384]{1,0:T(8,128)}, u32[]{:S(2)}) copy-start(f32[32,384]{1,0:T(8,128)} %param.13) | copy-start | bytes 147460
  0.6 140.6 %copy-start = (f32[32,384]{1,0:T(8,128)S(1)}, f32[32,384]{1,0:T(8,128)}, u32[]{:S(2)}) copy-start(f32[32,384]{1,0:T(8,128)} %param.12) | copy-start | bytes 147460
  2.9 146.4 %copy-start.2 = (f32[16,384]{1,0:T(8,128)S(1)}, f32[16,384]{1,0:T(8,128)}, u32[]{:S(2)}) copy-start(f32[16,384]{1,0:T(8,128)} %param.17) | copy-start | bytes 73732
  2.9 146.4 %copy-start.3 = (f32[16,384]{1,0:T(8,128)S(1)}, f32[16,384]{1,0:T(8,128)}, u32[]{:S(2)}) copy-start(f32[16,384]{1,0:T(8,128)} %param.15) | copy-start | bytes 73732
  2.9 146.4 %copy-start.4 = (f32[16,384]{1,0:T(8,128)S(1)}, f32[16,384]{1,0:T(8,128)}, u32[]{:S(2)}) copy-start(f32[16,384]{1,0:T(8,128)} %param.14) | copy-start | bytes 73732
  2.9 146.4 %copy-start.5 = (f32[16,128]{1,0:T(8,128)S(1)}, f32[16,128]{1,0:T(8,128)}, u32[]{:S(2)}) copy-start(f32[16,128]{1,0:T(8,128)} %param.16) | copy-start | bytes 24580
  9.5 8.0 %collective-permute-start = (f32[32,384]{1,0:T(8,128)S(1)}, f32[32,384]{1,0:T(8,128)S(1)}, u32[]{:S(2)}, u32[]{:S(2)}) collective-permute-start(f32[32,384]{1,0:T(8,128)S(1)} %fusion.18), channel_id=1, source_target_pairs={{0,1},{1,2},{2,3},{3,4},{4,5},{5,6},{6,7},{7,0},{8,9},{9,10},{10,1... | collective-permute-start | bytes 147464 | tf_op jit(solution)/shard_map/ppermute | solution.py:12
  141.2 2.8 collective-permute-start.1
  156.0 4.5 %collective-permute-start.2 = (f32[32,384]{1,0:T(8,128)S(1)}, f32[32,384]{1,0:T(8,128)S(1)}, u32[]{:S(2)}, u32[]{:S(2)}) collective-permute-start(f32[32,384]{1,0:T(8,128)S(1)} %fusion.13), channel_id=1, source_target_pairs={{0,1},{1,2},{2,3},{3,4},{4,5},{5,6},{6,7},{7,0},{8,9},{9,10},{10,1... | collective-permute-start | bytes 147464 | tf_op jit(solution)/shard_map/ppermute | solution.py:12
  286.7 2.8 collective-permute-start.3
  302.1 4.5 %collective-permute-start.4 = (f32[32,384]{1,0:T(8,128)S(1)}, f32[32,384]{1,0:T(8,128)S(1)}, u32[]{:S(2)}, u32[]{:S(2)}) collective-permute-start(f32[32,384]{1,0:T(8,128)S(1)} %fusion.8), channel_id=1, source_target_pairs={{0,1},{1,2},{2,3},{3,4},{4,5},{5,6},{6,7},{7,0},{8,9},{9,10},{10,1... | collective-permute-start | bytes 147464 | tf_op jit(solution)/shard_map/ppermute | solution.py:12
where the time goes:
time: 436 us; the launch traced here: 433 us
  blocking collectives  375 us (86%)
  matrix products  31.2 us (7%)
  waiting for transfers between devices  16.3 us (4%)
  starting transfers between devices  5.78 us (1%)
    psum x3, blocking collectives, slab_total(): return lax.psum(merged_partials(lam), 'contact')  375 us
    dot_general x3, matrix products, merged_partials(): jnp.einsum('tkbc,tc->tkb', jacobian, lamb, preferred_element_type=jnp.flo...  18.7 us
    ppermute x5, waiting for transfers between devices, shifted(): return lax.ppermute(value, axis, pairs)  16.3 us
    dot_general x2, matrix products, per_device(): jnp.einsum('tkbc,tkb->tc', jacobian, rows, preferred_element_type=jnp.flo...  10.1 us
  transfers between devices with their start and end apart: 5, of which 5 were waited for; matrix products, arithmetic and copies ran while one was open for 0% of the time, Pallas kernels for 0%

commit v1 on v0

--- a/solution.py
+++ b/solution.py
@@ -1,15 +1,14 @@
+import functools
+
 import jax
 import jax.numpy as jnp
 from jax import lax
+from jax.experimental import pallas as pl
+from jax.experimental.pallas import tpu as pltpu
 from jax.sharding import PartitionSpec as P
 
 ITERS = 2
-
-
-def shifted(value, axis, steps):
-    count = lax.axis_size(axis)
-    pairs = [(source, (source + steps) % count) for source in range(count)]
-    return lax.ppermute(value, axis, pairs)
+MESH = pl.DeviceIdType.MESH
 
 
 def project(trial, friction, contacts):
@@ -26,8 +25,104 @@
     return jnp.concatenate([new_normal, first * factor, second * factor], axis=1)
 
 
+def exchange_kernel(
+    n_contact, n_body, last,
+    own_ref, later_ref, vfree_ref, imass_ref, *rest,
+):
+    steps = n_contact.bit_length() - 1
+    if last:
+        vel_ref, recv_l, stage, recv_c, send_sem, recv_sem = rest
+    else:
+        velb_ref, velb_next_ref, recv_l, stage, recv_c, recv_v, send_sem, recv_sem = rest
+    c = lax.axis_index("contact")
+    b = lax.axis_index("body")
+    up = lax.rem(b + 1, n_body)
+    down = lax.rem(b + n_body - 1, n_body)
+    partners = []
+    for k in range(steps):
+        width = 1 << k
+        bit = lax.rem(c // width, 2)
+        partners.append(c + (1 - 2 * bit) * width)
+
+    barrier = pltpu.get_barrier_semaphore()
+    for p in partners:
+        pl.semaphore_signal(barrier, inc=1, device_id=(p, b), device_id_type=MESH)
+    for nb in (up, down):
+        pl.semaphore_signal(barrier, inc=1, device_id=(c, nb), device_id_type=MESH)
+    pl.semaphore_wait(barrier, steps + 2)
+
+    shift = pltpu.make_async_remote_copy(
+        src_ref=later_ref, dst_ref=recv_l, send_sem=send_sem.at[0], recv_sem=recv_sem.at[0],
+        device_id=(c, up), device_id_type=MESH,
+    )
+    shift.start()
+    shift.wait()
+    stage[0] = own_ref[...] + recv_l[...]
+    copies = []
+    for k in range(steps):
+        copy = pltpu.make_async_remote_copy(
+            src_ref=stage.at[k], dst_ref=recv_c.at[k],
+            send_sem=send_sem.at[k + 1], recv_sem=recv_sem.at[k + 1],
+            device_id=(partners[k], b), device_id_type=MESH,
+        )
+        copy.start()
+        copy.wait_recv()
+        stage[k + 1] = stage[k] + recv_c[k]
+        copies.append(copy)
+    vel = vfree_ref[...] + imass_ref[...] * stage[steps]
+    if last:
+        vel_ref[...] = vel
+    else:
+        velb_ref[...] = vel.astype(jnp.bfloat16)
+        back = pltpu.make_async_remote_copy(
+            src_ref=velb_ref, dst_ref=recv_v, send_sem=send_sem.at[steps + 1],
+            recv_sem=recv_sem.at[steps + 1], device_id=(c, down), device_id_type=MESH,
+        )
+        back.start()
+        back.wait()
+        velb_next_ref[...] = recv_v[...]
+    for copy in copies:
+        copy.wait_send()
+
+
+def exchange(own, later, vel_free, inv_mass, n_contact, n_body, last):
+    shape = own.shape
+    steps = n_contact.bit_length() - 1
+    vspec = pl.BlockSpec(memory_space=pltpu.VMEM)
+    if last:
+        out_shape = jax.ShapeDtypeStruct(shape, jnp.float32)
+        out_specs = vspec
+        extra = []
+    else:
+        out_shape = (
+            jax.ShapeDtypeStruct(shape, jnp.bfloat16),
+            jax.ShapeDtypeStruct(shape, jnp.bfloat16),
+        )
+        out_specs = (vspec, vspec)
+        extra = [pltpu.VMEM(shape, jnp.bfloat16)]
+    scratch = [
+        pltpu.VMEM(shape, jnp.float32),
+        pltpu.VMEM((steps + 1,) + shape, jnp.float32),
+        pltpu.VMEM((steps,) + shape, jnp.float32),
+        *extra,
+        pltpu.SemaphoreType.DMA((steps + 2,)),
+        pltpu.SemaphoreType.DMA((steps + 2,)),
+    ]
+    return pl.pallas_call(
+        functools.partial(exchange_kernel, n_contact, n_body, last),
+        out_shape=out_shape,
+        in_specs=[vspec] * 4,
+        out_specs=out_specs,
+        scratch_shapes=scratch,
+        compiler_params=pltpu.CompilerParams(
+            collective_id=1 if last else 0, has_side_effects=True
+        ),
+    )(own, later, vel_free, inv_mass)
+
+
 def per_device(
-    jacobian, tile_block, tile_count, vel_free, inv_mass, bias, step_scale, friction, impulse_start
+    n_contact, n_body,
+    jacobian, tile_block, tile_count, vel_free, inv_mass, bias, step_scale, friction, impulse_start,
 ):
     tiles_here = jacobian.shape[0]
     slab_blocks = vel_free.shape[0]
@@ -40,21 +135,17 @@
     pick_own_b = pick_own.astype(jnp.bfloat16)
     pick_next_b = pick_next.astype(jnp.bfloat16)
 
-    def merged_partials(lam):
+    def partials(lam):
         lamb = lam.astype(jnp.bfloat16)
         push = jnp.einsum("tkbc,tc->tkb", jacobian, lamb, preferred_element_type=jnp.float32)
         own = jnp.einsum("ts,tb->sb", pick_own, push[:, 0], precision=lax.Precision.HIGHEST)
         later = jnp.einsum("ts,tb->sb", pick_next, push[:, 1], precision=lax.Precision.HIGHEST)
-        return own + shifted(later, "body", 1)
-
-    def slab_total(lam):
-        return lax.psum(merged_partials(lam), "contact")
+        return own, later
 
     lam = impulse_start * mask
     for sweep in range(ITERS):
-        total = slab_total(lam)
-        velb = (vel_free + inv_mass * total).astype(jnp.bfloat16)
-        velb_next = shifted(velb, "body", -1)
+        own, later = partials(lam)
+        velb, velb_next = exchange(own, later, vel_free, inv_mass, n_contact, n_body, False)
         rows_own = jnp.dot(pick_own_b, velb, preferred_element_type=jnp.float32).astype(
             jnp.bfloat16
         )
@@ -64,12 +155,14 @@
         rows = jnp.stack([rows_own, rows_next], axis=1)
         rel = jnp.einsum("tkbc,tkb->tc", jacobian, rows, preferred_element_type=jnp.float32) + bias
         lam = project(lam - step_scale * rel, friction, contacts) * mask
-    total = slab_total(lam)
-    velocity = vel_free + inv_mass * total
+    own, later = partials(lam)
+    velocity = exchange(own, later, vel_free, inv_mass, n_contact, n_body, True)
     return (lam, velocity)
 
 
 def solution(mesh):
+    n_contact = mesh.shape["contact"]
+    n_body = mesh.shape["body"]
     placed = (
         P(("contact", "body"), None, None, None),
         P(("contact", "body"), None),
@@ -82,7 +175,7 @@
         P(("contact", "body"), None),
     )
     return jax.shard_map(
-        per_device,
+        functools.partial(per_device, n_contact, n_body),
         mesh=mesh,
         in_specs=placed,
         out_specs=(P(("contact", "body"), None), P("body", None)),

time: 436 us -> 122 us (0.28)
  blocking collectives: 375 us -> 0 us
  Pallas kernels: 0 us -> 77.1 us
  waiting for transfers between devices: 16.3 us -> 0 us
  matrix products: 31.2 us -> 37.9 us
  starting transfers between devices: 5.78 us -> 0 us
    psum x3 -> x0, blocking collectives: 375 us -> none  [slab_total(): return lax.psum(merged_partials(lam), 'contact')]
    pallas_call x0 -> x3, Pallas kernels: none -> 77.1 us  [exchange(): pl.pallas_call(functools.partial(exchange_kernel, n_contact, n_body, last...]
    ppermute x5 -> x0, waiting for transfers between devices: 16.3 us -> none  [shifted(): return lax.ppermute(value, axis, pairs)]
    ppermute x5 -> x0, starting transfers between devices: 5.78 us -> none  [shifted(): return lax.ppermute(value, axis, pairs)]
  transfers between devices with their start and end apart: 5 -> 0, of which waited for: 5 -> 0; matrix products, arithmetic and copies ran while one was open for 0% -> 0% of each run, Pallas kernels for 0% -> 0%
where the time goes in v1:
time: 122 us; the launch traced here: 121 us
  Pallas kernels  77.1 us (63%)
  matrix products  37.9 us (31%)
  local copies, waits for them, and re-layouts  2.45 us (2%)
  other arithmetic  1.8 us (1%)
  between operations  1.42 us (1%)
    pallas_call x3, Pallas kernels, exchange(): pl.pallas_call(functools.partial(exchange_kernel, n_contact, n_body, last...  77.1 us
    dot_general x3, matrix products, partials(): jnp.einsum('tkbc,tc->tkb', jacobian, lamb, preferred_element_type=jnp.flo...  18.7 us
    dot_general x2, matrix products, per_device(): jnp.einsum('tkbc,tkb->tc', jacobian, rows, preferred_element_type=jnp.flo...  10.1 us
    dot_general x3, matrix products, partials(): jnp.einsum('ts,tb->sb', pick_own, push[:, 0], precision=lax.Precision.HIG...  2.72 us
    dot_general x3, matrix products, partials(): jnp.einsum('ts,tb->sb', pick_next, push[:, 1], precision=lax.Precision.HI...  2.71 us

profile of v1, /device:TPU:1, one launch (start us, length us, event | category | flops | bytes accessed | tf_op | source)
XLA Modules:
  0.0 120.6 jit_solution(10282621001071934746)
XLA Ops:
  1.3 0.8 slice_bitcast_fusion
  2.0 0.8 fusion.38
  2.9 0.0 copy-start
  2.9 0.0 copy-start.1
  2.9 0.0 copy-start.3
  2.9 6.2 %fusion.34 = f32[16,1,2,384]{3,1,2,0:T(1,128)S(1)} fusion(bf16[16,2,384,384]{3,2,1,0:T(8,128)(2,1)} %param.9, bf16[16,384,1,1]{1,0,2,3:T(8,128)(2,1)S(1)} %fusion.38), kind=kOutput, calls=%fused_computation.47 | convolution fusion | flops 9437184 | bytes 9498624 | tf_op jit(solution)/shard_map/tkbc,tc->tkb/dot_general | solution.py:140
  9.2 0.9 fusion.20.later_ref
  10.1 0.9 fusion.23.own_ref
  11.0 29.0 %shard_map.104 = (bf16[32,384]{1,0:T(8,128)(2,1)}, bf16[32,384]{1,0:T(8,128)(2,1)}) custom-call(f32[32,384]{1,0:T(8,128)} %fusion.23.own_ref, f32[32,384]{1,0:T(8,128)} %fusion.20.later_ref, f32[32,384]{1,0:T(8,128)} %vfree_ref.5, f32[32,384]{1,0:T(8,128)} %imass_ref.5), custom_call_target="tpu_custom_call" | custom-call | tf_op jit(solution)/shard_map/pallas_call | solution.py:111
  40.1 0.9 fusion
  41.0 0.9 fusion.1
  41.9 5.1 %fusion.6 = f32[16,1,384,1]{2,1,3,0:T(1,128)S(1)} fusion(bf16[16,2,384,384]{3,2,1,0:T(8,128)(2,1)} %param.9, bf16[16,2,384,1]{2,0,1,3:T(8,128)(2,1)S(1)} %maximum_bitcast_fusion), kind=kOutput, calls=%fused_computation.12 | convolution fusion | flops 9437184 | bytes 9486336 | tf_op jit(solution)/shard_map/tkbc,tkb->tc/dot_general | solution.py:156
  47.0 0.0 copy-done
  47.0 0.0 copy-done.1
  47.0 0.0 copy-done.2
  47.0 0.1 fusion.29
  47.1 0.0 copy-done.3
  47.1 0.1 fusion.37
  47.2 6.2 %fusion.32 = f32[16,1,2,384]{3,1,2,0:T(1,128)S(1)} fusion(bf16[16,2,384,384]{3,2,1,0:T(8,128)(2,1)} %param.9, bf16[16,384,1,1]{1,0,2,3:T(8,128)(2,1)S(1)} %fusion.37), kind=kOutput, calls=%fused_computation.45 | convolution fusion | flops 9437184 | bytes 9498624 | tf_op jit(solution)/shard_map/tkbc,tc->tkb/dot_general | solution.py:140
  53.5 0.9 fusion.14.later_ref
  54.4 0.9 fusion.17.own_ref
  55.3 24.2 %shard_map.105 = (bf16[32,384]{1,0:T(8,128)(2,1)}, bf16[32,384]{1,0:T(8,128)(2,1)}) custom-call(f32[32,384]{1,0:T(8,128)} %fusion.17.own_ref, f32[32,384]{1,0:T(8,128)} %fusion.14.later_ref, f32[32,384]{1,0:T(8,128)} %vfree_ref.5, f32[32,384]{1,0:T(8,128)} %imass_ref.5), custom_call_target="tpu_custom_call" | custom-call | tf_op jit(solution)/shard_map/pallas_call | solution.py:111
  79.5 0.9 fusion.2
  80.4 0.9 fusion.3
  81.3 5.1 %fusion.4 = f32[16,1,384,1]{2,1,3,0:T(1,128)S(1)} fusion(bf16[16,2,384,384]{3,2,1,0:T(8,128)(2,1)} %param.9, bf16[16,2,384,1]{2,0,1,3:T(8,128)(2,1)S(1)} %maximum_bitcast_fusion.1), kind=kOutput, calls=%fused_computation.9 | convolution fusion | flops 9437184 | bytes 9486336 | tf_op jit(solution)/shard_map/tkbc,tkb->tc/dot_general | solution.py:156
  86.4 0.1 fusion.27
  86.5 0.7 convert_bitcast_fusion
  87.2 6.2 %fusion.30 = f32[16,1,2,384]{3,1,2,0:T(1,128)S(1)} fusion(bf16[16,2,384,384]{3,2,1,0:T(8,128)(2,1)} %param.9, bf16[16,384,1,1]{1,0,2,3:T(8,128)(2,1)S(1)} %get-tuple-element.10), kind=kOutput, calls=%fused_computation.43 | convolution fusion | flops 9437184 | bytes 9498624 | tf_op jit(solution)/shard_map/tkbc,tc->tkb/dot_general | solution.py:140
  93.5 0.9 fusion.8.later_ref
  94.4 0.9 fusion.11.own_ref
  95.3 23.9 %shard_map.106 = f32[32,384]{1,0:T(8,128)} custom-call(f32[32,384]{1,0:T(8,128)} %fusion.11.own_ref, f32[32,384]{1,0:T(8,128)} %fusion.8.later_ref, f32[32,384]{1,0:T(8,128)} %vfree_ref.5, f32[32,384]{1,0:T(8,128)} %imass_ref.5), custom_call_target="tpu_custom_call" | custom-call | tf_op jit(solution)/shard_map/pallas_call | solution.py:111
  119.2 1.4 %copy.71 = f32[32,384]{1,0:T(8,128)} copy(f32[32,384]{1,0:T(8,128)} %shard_map.106) | data formatting | bytes 98304
  (14 shorter events, 0.3 us)
Async XLA Ops:
  2.9 44.1 %copy-start = (f32[16,384]{1,0:T(8,128)S(1)}, f32[16,384]{1,0:T(8,128)}, u32[]{:S(2)}) copy-start(f32[16,384]{1,0:T(8,128)} %param.17) | copy-start | bytes 73732
  2.9 44.1 %copy-start.1 = (f32[16,384]{1,0:T(8,128)S(1)}, f32[16,384]{1,0:T(8,128)}, u32[]{:S(2)}) copy-start(f32[16,384]{1,0:T(8,128)} %param.15) | copy-start | bytes 73732
  2.9 44.1 %copy-start.2 = (f32[16,384]{1,0:T(8,128)S(1)}, f32[16,384]{1,0:T(8,128)}, u32[]{:S(2)}) copy-start(f32[16,384]{1,0:T(8,128)} %param.14) | copy-start | bytes 73732
  2.9 44.2 %copy-start.3 = (f32[16,128]{1,0:T(8,128)S(1)}, f32[16,128]{1,0:T(8,128)}, u32[]{:S(2)}) copy-start(f32[16,128]{1,0:T(8,128)} %param.16) | copy-start | bytes 24580

commit v2 on v0

v2 whole, which is shorter than its diff:
```python
import functools
import math

import jax
import jax.numpy as jnp
from jax import lax
from jax.experimental import pallas as pl
from jax.experimental.pallas import tpu as pltpu
from jax.sharding import PartitionSpec as P

ITERS = 2
MESH = pl.DeviceIdType.MESH


def project(trial, friction, contacts):
    normal = trial[:, :contacts]
    first = trial[:, contacts : 2 * contacts]
    second = trial[:, 2 * contacts :]
    tangent = jnp.sqrt(first * first + second * second)
    inside = tangent <= friction * normal
    below = friction * tangent <= -normal
    moved = (normal + friction * tangent) / (1.0 + friction * friction)
    safe = jnp.where(inside | below, 1.0, tangent)
    factor = jnp.where(inside, 1.0, jnp.where(below, 0.0, friction * moved / safe))
    new_normal = jnp.where(inside, normal, jnp.where(below, 0.0, moved))
    return jnp.concatenate([new_normal, first * factor, second * factor], axis=1)


def contact_groups(n_contact):
    rest = n_contact // 2
    gy = 1
    for d in range(1, int(math.isqrt(rest)) + 1):
        if rest % d == 0:
            gy = d
    return rest // gy, gy


def scatter_rows(pick_t_ref, push):
    tiles = push.shape[0]
    acc = None
    for t in range(tiles):
        term = pick_t_ref[:, t : t + 1] * push[t : t + 1, :]
        acc = term if acc is None else acc + term
    return acc


def gather_rows(pick_ref, vel_ref):
    blocks = vel_ref.shape[0]
    acc = None
    for s in range(blocks):
        term = pick_ref[:, s : s + 1] * vel_ref[s : s + 1, :].astype(jnp.float32)
        acc = term if acc is None else acc + term
    return acc


def sweep_kernel(n_contact, n_body, last, *refs):
    gx, gy = contact_groups(n_contact)
    if last:
        (push_ref, pto_ref, ptn_ref, vfree_ref, imass_ref,
         vel_out,
         later_buf, recv_l, p_buf, recv_core, xbuf, ybuf, vel_buf,
         s_sem, r_sem, sx_sem, rx_sem, sy_sem, ry_sem) = refs
    else:
        (push_ref, pto_ref, ptn_ref, vfree_ref, imass_ref, po_ref, pn_ref,
         rows_out,
         later_buf, recv_l, p_buf, recv_core, xbuf, ybuf, vel_buf, vel_next,
         s_sem, r_sem, sx_sem, rx_sem, sy_sem, ry_sem) = refs
    half = p_buf.shape[0] // 2
    c = lax.axis_index("contact")
    b = lax.axis_index("body")
    core = lax.rem(c, 2)
    x = lax.rem(c // 2, gx)
    y = c // (2 * gx)
    mate = c + 1 - 2 * core
    up = lax.rem(b + 1, n_body)
    down = lax.rem(b + n_body - 1, n_body)
    x_peers = [(y * gx + lax.rem(x + j, gx)) * 2 + core for j in range(1, gx)]
    y_peers = [(lax.rem(y + j, gy) * gx + x) * 2 + core for j in range(1, gy)]

    greet = [(c, up), (c, down), (mate, b)]
    greet += [(p, b) for p in x_peers] + [(p, b) for p in y_peers]
    if not last:
        greet += [(mate, up), (mate, down)]
    barrier = pltpu.get_barrier_semaphore()
    for dev in greet:
        pl.semaphore_signal(barrier, inc=1, device_id=dev, device_id_type=MESH)
    pl.semaphore_wait(barrier, len(greet))

    def remote(src, dst, send, recv, dev):
        return pltpu.make_async_remote_copy(
            src_ref=src, dst_ref=dst, send_sem=send, recv_sem=recv,
            device_id=dev, device_id_type=MESH,
        )

    sent = []
    later_buf[...] = scatter_rows(ptn_ref, push_ref[1])
    shift = remote(later_buf, recv_l, s_sem.at[0], r_sem.at[0], (c, up))
    shift.start()
    own = scatter_rows(pto_ref, push_ref[0])
    shift.wait_recv()
    sent.append(shift)
    p_buf[...] = own + recv_l[...]

    mine = pl.ds(pl.multiple_of(core * half, half), half)
    theirs = pl.ds(pl.multiple_of((1 - core) * half, half), half)
    rs = remote(p_buf.at[theirs], recv_core, s_sem.at[1], r_sem.at[1], (mate, b))
    rs.start()
    rs.wait_recv()
    sent.append(rs)
    part = p_buf[mine] + recv_core[...]

    for buf, pos, peers, size, ssem, rsem in (
        (xbuf, x, x_peers, gx, sx_sem, rx_sem),
        (ybuf, y, y_peers, gy, sy_sem, ry_sem),
    ):
        if size == 1:
            continue
        buf[pos] = part
        for j, p in enumerate(peers):
            cp = remote(buf.at[pos], buf.at[pos], ssem.at[j], rsem.at[pos], (p, b))
            cp.start()
            sent.append(cp)
        for j in range(1, size):
            src_pos = lax.rem(pos + size - j, size)
            remote(buf.at[src_pos], buf.at[src_pos], ssem.at[0], rsem.at[src_pos], (peers[-j], b)).wait_recv()
        part = buf[0]
        for g in range(1, size):
            part = part + buf[g]

    vel = vfree_ref[mine] + imass_ref[mine] * part
    if last:
        vel_buf[mine] = vel
        cp = remote(vel_buf.at[mine], vel_buf.at[mine], s_sem.at[2], r_sem.at[2], (mate, b))
        cp.start()
        sent.append(cp)
        remote(vel_buf.at[theirs], vel_buf.at[theirs], s_sem.at[2], r_sem.at[2], (mate, b)).wait_recv()
        vel_out[...] = vel_buf[...]
    else:
        vel_buf[mine] = vel.astype(jnp.bfloat16)
        src = vel_buf.at[mine]
        for k, (dst, dev) in enumerate((
            (vel_buf.at[mine], (mate, b)),
            (vel_next.at[mine], (c, down)),
            (vel_next.at[mine], (mate, down)),
        )):
            cp = remote(src, dst, s_sem.at[2 + k], r_sem.at[2 + k], dev)
            cp.start()
            sent.append(cp)
        for k, (dst, dev) in enumerate((
            (vel_buf.at[theirs], (mate, b)),
            (vel_next.at[mine], (c, up)),
            (vel_next.at[theirs], (mate, up)),
        )):
            remote(src, dst, s_sem.at[2 + k], r_sem.at[2 + k], dev).wait_recv()
        rows_out[0] = gather_rows(po_ref, vel_buf).astype(jnp.bfloat16)
        rows_out[1] = gather_rows(pn_ref, vel_next).astype(jnp.bfloat16)
    for cp in sent:
        cp.wait_send()


def sweep_exchange(push, pick_t_own, pick_t_next, vel_free, inv_mass, pick_own, pick_next,
                   n_contact, n_body, last):
    gx, gy = contact_groups(n_contact)
    blocks, width = vel_free.shape
    half = blocks // 2
    vspec = pl.BlockSpec(memory_space=pltpu.VMEM)
    args = [push, pick_t_own, pick_t_next, vel_free, inv_mass]
    if last:
        out_shape = jax.ShapeDtypeStruct((blocks, width), jnp.float32)
        vel_scratch = [pltpu.VMEM((blocks, width), jnp.float32)]
    else:
        args += [pick_own, pick_next]
        out_shape = jax.ShapeDtypeStruct(push.shape, jnp.bfloat16)
        vel_scratch = [pltpu.VMEM((blocks, width), jnp.bfloat16)] * 2
    scratch = [
        pltpu.VMEM((blocks, width), jnp.float32),
        pltpu.VMEM((blocks, width), jnp.float32),
        pltpu.VMEM((blocks, width), jnp.float32),
        pltpu.VMEM((half, width), jnp.float32),
        pltpu.VMEM((gx, half, width), jnp.float32),
        pltpu.VMEM((gy, half, width), jnp.float32),
        *vel_scratch,
        pltpu.SemaphoreType.DMA((5,)),
        pltpu.SemaphoreType.DMA((5,)),
        pltpu.SemaphoreType.DMA((max(gx - 1, 1),)),
        pltpu.SemaphoreType.DMA((gx,)),
        pltpu.SemaphoreType.DMA((max(gy - 1, 1),)),
        pltpu.SemaphoreType.DMA((gy,)),
    ]
    return pl.pallas_call(
        functools.partial(sweep_kernel, n_contact, n_body, last),
        out_shape=out_shape,
        in_specs=[vspec] * len(args),
        out_specs=vspec,
        scratch_shapes=scratch,
        compiler_params=pltpu.CompilerParams(
            collective_id=1 if last else 0, has_side_effects=True
        ),
    )(*args)


def per_device(
    n_contact, n_body,
    jacobian, tile_block, tile_count, vel_free, inv_mass, bias, step_scale, friction, impulse_start,
):
    tiles_here = jacobian.shape[0]
    slab_blocks = vel_free.shape[0]
    contacts = friction.shape[1]
    order = jnp.arange(tiles_here, dtype=jnp.int32)
    mask = (order < tile_count[0]).astype(jnp.float32)[:, None]
    span = jnp.arange(slab_blocks, dtype=jnp.int32)
    pick_own = (tile_block[:, 0:1] == span[None, :]).astype(jnp.float32)
    pick_next = (tile_block[:, 1:2] == span[None, :]).astype(jnp.float32)
    pick_t_own = pick_own.T
    pick_t_next = pick_next.T

    def pushes(lam):
        lamb = lam.astype(jnp.bfloat16)
        return jnp.einsum("tkbc,tc->ktb", jacobian, lamb, preferred_element_type=jnp.float32)

    lam = impulse_start * mask
    for sweep in range(ITERS):
        rows = sweep_exchange(
            pushes(lam), pick_t_own, pick_t_next, vel_free, inv_mass, pick_own, pick_next,
            n_contact, n_body, False,
        )
        rel = jnp.einsum("tkbc,ktb->tc", jacobian, rows, preferred_element_type=jnp.float32) + bias
        lam = project(lam - step_scale * rel, friction, contacts) * mask
    velocity = sweep_exchange(
        pushes(lam), pick_t_own, pick_t_next, vel_free, inv_mass, pick_own, pick_next,
        n_contact, n_body, True,
    )
    return (lam, velocity)


def solution(mesh):
    n_contact = mesh.shape["contact"]
    n_body = mesh.shape["body"]
    placed = (
        P(("contact", "body"), None, None, None),
        P(("contact", "body"), None),
        P(("contact", "body")),
        P("body", None),
        P("body", None),
        P(("contact", "body"), None),
        P(("contact", "body"), None),
        P(("contact", "body"), None),
        P(("contact", "body"), None),
    )
    return jax.shard_map(
        functools.partial(per_device, n_contact, n_body),
        mesh=mesh,
        in_specs=placed,
        out_specs=(P(("contact", "body"), None), P("body", None)),
        check_vma=False,
    )
```

time: 436 us -> 99.3 us (0.23)
  blocking collectives: 375 us -> 0 us
  Pallas kernels: 0 us -> 61.4 us
  waiting for transfers between devices: 16.3 us -> 0 us
  starting transfers between devices: 5.78 us -> 0 us
    psum x3 -> x0, blocking collectives: 375 us -> none  [slab_total(): return lax.psum(merged_partials(lam), 'contact')]
    pallas_call x0 -> x3, Pallas kernels: none -> 61.4 us  [sweep_exchange(): pl.pallas_call(functools.partial(sweep_kernel, n_contact, n_body, last),...]
    ppermute x5 -> x0, waiting for transfers between devices: 16.3 us -> none  [shifted(): return lax.ppermute(value, axis, pairs)]
    ppermute x5 -> x0, starting transfers between devices: 5.78 us -> none  [shifted(): return lax.ppermute(value, axis, pairs)]
    dot_general x15 -> x5, matrix products: 31.2 us -> 28.8 us  [the longest x3 18.6 us: pushes(): jnp.einsum('tkbc,tc->ktb', jacobian, lamb, preferred_element_type=jnp.flo...]
  transfers between devices with their start and end apart: 5 -> 0, of which waited for: 5 -> 0; matrix products, arithmetic and copies ran while one was open for 0% -> 0% of each run, Pallas kernels for 0% -> 0%
where the time goes in v2:
time: 99.3 us; the launch traced here: 98.8 us
  Pallas kernels  61.4 us (62%)
  matrix products  28.8 us (29%)
  local copies, waits for them, and re-layouts  4.13 us (4%)
  other arithmetic  3.07 us (3%)
  between operations  1.36 us (1%)
    pallas_call x3, Pallas kernels, sweep_exchange(): pl.pallas_call(functools.partial(sweep_kernel, n_contact, n_body, last),...  61.4 us
    dot_general x3, matrix products, pushes(): jnp.einsum('tkbc,tc->ktb', jacobian, lamb, preferred_element_type=jnp.flo...  18.6 us
    dot_general x2, matrix products, per_device(): jnp.einsum('tkbc,ktb->tc', jacobian, rows, preferred_element_type=jnp.flo...  10.1 us

profile of v2, /device:TPU:1, one launch (start us, length us, event | category | flops | bytes accessed | tf_op | source)
XLA Modules:
  0.0 98.8 jit_solution(7406966779414229101)
XLA Ops:
  1.3 0.8 slice_bitcast_fusion
  2.0 0.8 fusion.18
  2.9 0.7 fusion.20
  3.5 0.6 fusion.14
  4.1 0.0 copy-start
  4.1 0.0 copy-start.1
  4.2 0.0 copy-start.2
  4.2 0.0 copy-start.3
  4.2 6.2 %fusion.12 = f32[16,1,2,384]{3,1,2,0:T(1,128)S(1)} fusion(bf16[16,2,384,384]{3,2,1,0:T(8,128)(2,1)} %param.9, bf16[16,384,1,1]{1,0,2,3:T(8,128)(2,1)S(1)} %fusion.18), kind=kOutput, calls=%fused_computation.19 | convolution fusion | flops 9437184 | bytes 9498624 | tf_op jit(solution)/shard_map/tkbc,tc->ktb/dot_general | solution.py:219
  10.4 0.6 copy.38
  11.0 25.5 %shard_map.104 = bf16[2,16,384]{2,1,0:T(8,128)(2,1)} custom-call(f32[2,16,384]{2,1,0:T(8,128)} %bitcast.50, f32[32,16]{1,0:T(8,128)} %get-tuple-element.12.refs_1_, f32[32,16]{1,0:T(8,128)} %get-tuple-element.13.refs_2_, f32[32,384]{1,0:T(8,128)} %refs_3_.5, f32[32,384]{1,0:T(8,128)} %refs_4_.5, f32[16,32]{1,0:T(8,128)} %get-tuple-element.14.refs_5_, ...), custom_call_target="tpu_custom_call" | custom-call | tf_op jit(solution)/shard_map/pallas_call | solution.py:190
  36.5 5.1 %fusion.2 = f32[16,1,384,1]{2,1,3,0:T(1,128)S(1)} fusion(bf16[16,2,384,384]{3,2,1,0:T(8,128)(2,1)} %param.9, bf16[2,16,384,1]{2,1,0,3:T(8,128)(2,1)} %bitcast.47), kind=kOutput, calls=%fused_computation.4 | convolution fusion | flops 9437184 | bytes 9486336 | tf_op jit(solution)/shard_map/tkbc,ktb->tc/dot_general | solution.py:227
  41.6 0.0 copy-done
  41.6 0.0 copy-done.1
  41.6 0.0 copy-done.2
  41.6 0.1 fusion.7
  41.7 0.0 copy-done.3
  41.7 0.1 fusion.17
  41.8 6.2 %fusion.10 = f32[16,1,2,384]{3,1,2,0:T(1,128)S(1)} fusion(bf16[16,2,384,384]{3,2,1,0:T(8,128)(2,1)} %param.9, bf16[16,384,1,1]{1,0,2,3:T(8,128)(2,1)S(1)} %fusion.17), kind=kOutput, calls=%fused_computation.17 | convolution fusion | flops 9437184 | bytes 9498624 | tf_op jit(solution)/shard_map/tkbc,tc->ktb/dot_general | solution.py:219
  48.0 0.6 copy.37
  48.6 18.3 %shard_map.105 = bf16[2,16,384]{2,1,0:T(8,128)(2,1)} custom-call(f32[2,16,384]{2,1,0:T(8,128)} %bitcast.48, f32[32,16]{1,0:T(8,128)} %get-tuple-element.12.refs_1_, f32[32,16]{1,0:T(8,128)} %get-tuple-element.13.refs_2_, f32[32,384]{1,0:T(8,128)} %refs_3_.5, f32[32,384]{1,0:T(8,128)} %refs_4_.5, f32[16,32]{1,0:T(8,128)} %get-tuple-element.14.refs_5_, ...), custom_call_target="tpu_custom_call" | custom-call | tf_op jit(solution)/shard_map/pallas_call | solution.py:190
  66.9 5.1 %fusion = f32[16,1,384,1]{2,1,3,0:T(1,128)S(1)} fusion(bf16[16,2,384,384]{3,2,1,0:T(8,128)(2,1)} %param.9, bf16[2,16,384,1]{2,1,0,3:T(8,128)(2,1)} %bitcast.46), kind=kOutput, calls=%fused_computation.1 | convolution fusion | flops 9437184 | bytes 9486336 | tf_op jit(solution)/shard_map/tkbc,ktb->tc/dot_general | solution.py:227
  72.0 0.1 fusion.5
  72.1 0.7 convert_bitcast_fusion
  72.8 6.2 %fusion.8 = f32[16,1,2,384]{3,1,2,0:T(1,128)S(1)} fusion(bf16[16,2,384,384]{3,2,1,0:T(8,128)(2,1)} %param.9, bf16[16,384,1,1]{1,0,2,3:T(8,128)(2,1)S(1)} %get-tuple-element.2), kind=kOutput, calls=%fused_computation.15 | convolution fusion | flops 9437184 | bytes 9498624 | tf_op jit(solution)/shard_map/tkbc,tc->ktb/dot_general | solution.py:219
  79.0 0.6 copy.36
  79.7 17.7 %shard_map.106 = f32[32,384]{1,0:T(8,128)} custom-call(f32[2,16,384]{2,1,0:T(8,128)} %bitcast.49, f32[32,16]{1,0:T(8,128)} %get-tuple-element.12.refs_1_, f32[32,16]{1,0:T(8,128)} %get-tuple-element.13.refs_2_, f32[32,384]{1,0:T(8,128)} %refs_3_.5, f32[32,384]{1,0:T(8,128)} %refs_4_.5), custom_call_target="tpu_custom_call" | custom-call | tf_op jit(solution)/shard_map/pallas_call | solution.py:190
  97.3 1.4 %copy.41 = f32[32,384]{1,0:T(8,128)} copy(f32[32,384]{1,0:T(8,128)} %shard_map.106) | data formatting | bytes 98304
  (5 shorter events, 0.1 us)
Async XLA Ops:
  4.1 37.4 %copy-start = (f32[16,384]{1,0:T(8,128)S(1)}, f32[16,384]{1,0:T(8,128)}, u32[]{:S(2)}) copy-start(f32[16,384]{1,0:T(8,128)} %param.17) | copy-start | bytes 73732
  4.1 37.4 %copy-start.1 = (f32[16,384]{1,0:T(8,128)S(1)}, f32[16,384]{1,0:T(8,128)}, u32[]{:S(2)}) copy-start(f32[16,384]{1,0:T(8,128)} %param.15) | copy-start | bytes 73732
  4.2 37.4 %copy-start.2 = (f32[16,384]{1,0:T(8,128)S(1)}, f32[16,384]{1,0:T(8,128)}, u32[]{:S(2)}) copy-start(f32[16,384]{1,0:T(8,128)} %param.14) | copy-start | bytes 73732
  4.2 37.5 %copy-start.3 = (f32[16,128]{1,0:T(8,128)S(1)}, f32[16,128]{1,0:T(8,128)}, u32[]{:S(2)}) copy-start(f32[16,128]{1,0:T(8,128)} %param.16) | copy-start | bytes 24580

commit v3 on v2

v3 whole, which is shorter than its diff:
```python
import functools
import math

import jax
import jax.numpy as jnp
from jax import lax
from jax.experimental import pallas as pl
from jax.experimental.pallas import tpu as pltpu
from jax.sharding import PartitionSpec as P

ITERS = 2
MESH = pl.DeviceIdType.MESH


def project(trial, friction, contacts):
    normal = trial[:, :contacts]
    first = trial[:, contacts : 2 * contacts]
    second = trial[:, 2 * contacts :]
    tangent = jnp.sqrt(first * first + second * second)
    inside = tangent <= friction * normal
    below = friction * tangent <= -normal
    moved = (normal + friction * tangent) / (1.0 + friction * friction)
    safe = jnp.where(inside | below, 1.0, tangent)
    factor = jnp.where(inside, 1.0, jnp.where(below, 0.0, friction * moved / safe))
    new_normal = jnp.where(inside, normal, jnp.where(below, 0.0, moved))
    return jnp.concatenate([new_normal, first * factor, second * factor], axis=1)


def contact_groups(n_contact):
    rest = n_contact // 2
    gy = 1
    for d in range(1, int(math.isqrt(rest)) + 1):
        if rest % d == 0:
            gy = d
    return rest // gy, gy


def scatter_rows(tb_ref, column, push_ref, blocks):
    tiles = push_ref.shape[1]
    width = push_ref.shape[2]
    slot = lax.broadcasted_iota(jnp.int32, (blocks, width), 0)
    acc = None
    for t in range(tiles):
        row = push_ref[column, t : t + 1, :]
        term = jnp.where(slot == tb_ref[t, column], row, 0.0)
        acc = term if acc is None else acc + term
    return acc


def sweep_kernel(n_contact, n_body, last, *refs):
    gx, gy = contact_groups(n_contact)
    if last:
        (tb_ref, push_ref,
         tot_out,
         own_buf, later_buf, recv3, xbuf, ybuf, tot_buf,
         s_sem, r_sem, sx_sem, rx_sem, sy_sem, ry_sem) = refs
    else:
        (tb_ref, push_ref, vfree_ref, imass_ref,
         rows_out,
         own_buf, later_buf, recv3, xbuf, ybuf, vel_buf, vel_next, velf, rows_buf,
         s_sem, r_sem, sx_sem, rx_sem, sy_sem, ry_sem) = refs
    blocks = own_buf.shape[0]
    width = own_buf.shape[1]
    half = blocks // 2
    c = lax.axis_index("contact")
    b = lax.axis_index("body")
    core = lax.rem(c, 2)
    x = lax.rem(c // 2, gx)
    y = c // (2 * gx)
    mate = c + 1 - 2 * core
    up = lax.rem(b + 1, n_body)
    down = lax.rem(b + n_body - 1, n_body)
    x_peers = [(y * gx + lax.rem(x + j, gx)) * 2 + core for j in range(1, gx)]
    y_peers = [(lax.rem(y + j, gy) * gx + x) * 2 + core for j in range(1, gy)]

    greet = [(mate, b), (c, up), (mate, up), (c, down), (mate, down)]
    greet += [(p, b) for p in x_peers] + [(p, b) for p in y_peers]
    barrier = pltpu.get_barrier_semaphore()
    for dev in greet:
        pl.semaphore_signal(barrier, inc=1, device_id=dev, device_id_type=MESH)
    pl.semaphore_wait(barrier, len(greet))

    def remote(src, dst, send, recv, dev):
        return pltpu.make_async_remote_copy(
            src_ref=src, dst_ref=dst, send_sem=send, recv_sem=recv,
            device_id=dev, device_id_type=MESH,
        )

    mine = pl.ds(pl.multiple_of(core * half, half), half)
    theirs = pl.ds(pl.multiple_of((1 - core) * half, half), half)
    sent = []
    later_buf[...] = scatter_rows(tb_ref, 1, push_ref, blocks)
    for k, (src, dev) in enumerate(((later_buf.at[mine], (c, up)), (later_buf.at[theirs], (mate, up)))):
        cp = remote(src, recv3.at[1 + k], s_sem.at[1 + k], r_sem.at[1 + k], dev)
        cp.start()
        sent.append(cp)
    own_buf[...] = scatter_rows(tb_ref, 0, push_ref, blocks)
    cp = remote(own_buf.at[theirs], recv3.at[0], s_sem.at[0], r_sem.at[0], (mate, b))
    cp.start()
    sent.append(cp)
    for k, dev in enumerate(((mate, b), (c, down), (mate, down))):
        remote(own_buf.at[mine], recv3.at[k], s_sem.at[k], r_sem.at[k], dev).wait_recv()
    part = own_buf[mine] + recv3[0] + recv3[1] + recv3[2]

    for buf, pos, peers, size, ssem, rsem in (
        (xbuf, x, x_peers, gx, sx_sem, rx_sem),
        (ybuf, y, y_peers, gy, sy_sem, ry_sem),
    ):
        if size == 1:
            continue
        buf[pos] = part
        for j, p in enumerate(peers):
            cp = remote(buf.at[pos], buf.at[pos], ssem.at[j], rsem.at[pos], (p, b))
            cp.start()
            sent.append(cp)
        for j in range(1, size):
            src_pos = lax.rem(pos + size - j, size)
            remote(buf.at[src_pos], buf.at[src_pos], ssem.at[0], rsem.at[src_pos], (peers[-j], b)).wait_recv()
        part = buf[0]
        for g in range(1, size):
            part = part + buf[g]

    if last:
        tot_buf[mine] = part
        cp = remote(tot_buf.at[mine], tot_buf.at[mine], s_sem.at[3], r_sem.at[3], (mate, b))
        cp.start()
        sent.append(cp)
        remote(tot_buf.at[theirs], tot_buf.at[theirs], s_sem.at[3], r_sem.at[3], (mate, b)).wait_recv()
        tot_out[...] = tot_buf[...]
    else:
        vel = vfree_ref[mine] + imass_ref[mine] * part
        vel_buf[mine] = vel.astype(jnp.bfloat16)
        src = vel_buf.at[mine]
        for k, (dst, dev) in enumerate((
            (vel_buf.at[mine], (mate, b)),
            (vel_next.at[mine], (c, down)),
            (vel_next.at[mine], (mate, down)),
        )):
            cp = remote(src, dst, s_sem.at[3 + k], r_sem.at[3 + k], dev)
            cp.start()
            sent.append(cp)
        for k, (dst, dev) in enumerate((
            (vel_buf.at[theirs], (mate, b)),
            (vel_next.at[mine], (c, up)),
            (vel_next.at[theirs], (mate, up)),
        )):
            remote(src, dst, s_sem.at[3 + k], r_sem.at[3 + k], dev).wait_recv()
        velf[0] = vel_buf[...].astype(jnp.float32)
        velf[1] = vel_next[...].astype(jnp.float32)
        tiles = rows_buf.shape[1]
        for column in range(2):
            for t in range(tiles):
                rows_buf[column, pl.ds(t, 1), :] = velf[column, pl.ds(tb_ref[t, column], 1), :]
            rows_out[column] = rows_buf[column].astype(jnp.bfloat16)
    for cp in sent:
        cp.wait_send()


def sweep_exchange(tile_block, push, vel_free, inv_mass, n_contact, n_body, last):
    gx, gy = contact_groups(n_contact)
    blocks, width = vel_free.shape
    tiles = push.shape[1]
    half = blocks // 2
    vspec = pl.BlockSpec(memory_space=pltpu.VMEM)
    sspec = pl.BlockSpec(memory_space=pltpu.SMEM)
    if last:
        args = [tile_block, push]
        out_shape = jax.ShapeDtypeStruct((blocks, width), jnp.float32)
        tail = [pltpu.VMEM((blocks, width), jnp.float32)]
    else:
        args = [tile_block, push, vel_free, inv_mass]
        out_shape = jax.ShapeDtypeStruct((2, tiles, width), jnp.bfloat16)
        tail = [
            pltpu.VMEM((blocks, width), jnp.bfloat16),
            pltpu.VMEM((blocks, width), jnp.bfloat16),
            pltpu.VMEM((2, blocks, width), jnp.float32),
            pltpu.VMEM((2, tiles, width), jnp.float32),
        ]
    scratch = [
        pltpu.VMEM((blocks, width), jnp.float32),
        pltpu.VMEM((blocks, width), jnp.float32),
        pltpu.VMEM((3, half, width), jnp.float32),
        pltpu.VMEM((gx, half, width), jnp.float32),
        pltpu.VMEM((gy, half, width), jnp.float32),
        *tail,
        pltpu.SemaphoreType.DMA((6,)),
        pltpu.SemaphoreType.DMA((6,)),
        pltpu.SemaphoreType.DMA((max(gx - 1, 1),)),
        pltpu.SemaphoreType.DMA((gx,)),
        pltpu.SemaphoreType.DMA((max(gy - 1, 1),)),
        pltpu.SemaphoreType.DMA((gy,)),
    ]
    return pl.pallas_call(
        functools.partial(sweep_kernel, n_contact, n_body, last),
        out_shape=out_shape,
        in_specs=[sspec] + [vspec] * (len(args) - 1),
        out_specs=vspec,
        scratch_shapes=scratch,
        compiler_params=pltpu.CompilerParams(
            collective_id=1 if last else 0, has_side_effects=True
        ),
    )(*args)


def per_device(
    n_contact, n_body,
    jacobian, tile_block, tile_count, vel_free, inv_mass, bias, step_scale, friction, impulse_start,
):
    tiles_here = jacobian.shape[0]
    contacts = friction.shape[1]
    order = jnp.arange(tiles_here, dtype=jnp.int32)
    mask = (order < tile_count[0]).astype(jnp.float32)[:, None]

    def pushes(lam):
        lamb = lam.astype(jnp.bfloat16)
        return jnp.einsum("tkbc,tc->ktb", jacobian, lamb, preferred_element_type=jnp.float32)

    lam = impulse_start * mask
    for sweep in range(ITERS):
        rows = sweep_exchange(tile_block, pushes(lam), vel_free, inv_mass, n_contact, n_body, False)
        rel = jnp.einsum("tkbc,ktb->tc", jacobian, rows, preferred_element_type=jnp.float32) + bias
        lam = project(lam - step_scale * rel, friction, contacts) * mask
    total = sweep_exchange(tile_block, pushes(lam), vel_free, inv_mass, n_contact, n_body, True)
    velocity = vel_free + inv_mass * total
    return (lam, velocity)


def solution(mesh):
    n_contact = mesh.shape["contact"]
    n_body = mesh.shape["body"]
    placed = (
        P(("contact", "body"), None, None, None),
        P(("contact", "body"), None),
        P(("contact", "body")),
        P("body", None),
        P("body", None),
        P(("contact", "body"), None),
        P(("contact", "body"), None),
        P(("contact", "body"), None),
        P(("contact", "body"), None),
    )
    return jax.shard_map(
        functools.partial(per_device, n_contact, n_body),
        mesh=mesh,
        in_specs=placed,
        out_specs=(P(("contact", "body"), None), P("body", None)),
        check_vma=False,
    )
```

time: 99.3 us -> 97 us (0.977)
  Pallas kernels: 61.4 us -> 59.8 us
    pallas_call x3, Pallas kernels: 61.4 us -> 59.8 us  [sweep_exchange(): pl.pallas_call(functools.partial(sweep_kernel, n_contact, n_body, last),...]
    add x0 -> x1, other arithmetic: none -> 1.43 us  [per_device(): velocity = vel_free + inv_mass * total]
    convert_element_type x2 -> x0, other arithmetic: 1.29 us -> none  [per_device(): pick_own = (tile_block[:, 0:1] == span[None, :]).astype(jnp.float32)]
where the time goes in v3:
time: 97 us; the launch traced here: 96.5 us
  Pallas kernels  59.8 us (62%)
  matrix products  28.8 us (30%)
  local copies, waits for them, and re-layouts  3.31 us (3%)
  other arithmetic  3.21 us (3%)
  between operations  1.4 us (1%)
    pallas_call x3, Pallas kernels, sweep_exchange(): pl.pallas_call(functools.partial(sweep_kernel, n_contact, n_body, last),...  59.8 us
    dot_general x3, matrix products, pushes(): jnp.einsum('tkbc,tc->ktb', jacobian, lamb, preferred_element_type=jnp.flo...  18.7 us
    dot_general x2, matrix products, per_device(): jnp.einsum('tkbc,ktb->tc', jacobian, rows, preferred_element_type=jnp.flo...  10.2 us

profile of v3, /device:TPU:1, one launch (start us, length us, event | category | flops | bytes accessed | tf_op | source)
XLA Modules:
  0.0 96.5 jit_solution(5220118489896020138)
XLA Ops:
  1.3 1.3 %copy.11.refs_0_ = s32[16,2]{1,0:T(8,128)} copy(s32[16,2]{0,1:T(2,128)} %param.10) | data formatting | bytes 256 | tf_op args[1]
  2.6 0.8 fusion.16
  3.4 0.0 copy-start.2
  3.4 0.0 copy-start.3
  3.4 0.0 copy-start.4
  3.5 0.0 copy-start.5
  3.5 6.2 %fusion.12 = f32[16,1,2,384]{3,1,2,0:T(1,128)S(1)} fusion(bf16[16,2,384,384]{3,2,1,0:T(8,128)(2,1)} %param.9, bf16[16,384,1,1]{1,0,2,3:T(8,128)(2,1)S(1)} %fusion.16), kind=kOutput, calls=%fused_computation.20 | convolution fusion | flops 9437184 | bytes 9498624 | tf_op jit(solution)/shard_map/tkbc,tc->ktb/dot_general | solution.py:216
  9.7 0.6 copy.41
  10.4 24.8 %shard_map.104 = bf16[2,16,384]{2,1,0:T(8,128)(2,1)} custom-call(s32[16,2]{1,0:T(8,128)} %copy.11.refs_0_, f32[2,16,384]{2,1,0:T(8,128)} %bitcast.45, f32[32,384]{1,0:T(8,128)} %refs_2_.3, f32[32,384]{1,0:T(8,128)} %refs_3_.3), custom_call_target="tpu_custom_call" | custom-call | tf_op jit(solution)/shard_map/pallas_call | solution.py:193
  35.2 5.1 %fusion.2 = f32[16,1,384,1]{2,1,3,0:T(1,128)S(1)} fusion(bf16[16,2,384,384]{3,2,1,0:T(8,128)(2,1)} %param.9, bf16[2,16,384,1]{2,1,0,3:T(8,128)(2,1)} %bitcast.42), kind=kOutput, calls=%fused_computation.4 | convolution fusion | flops 9437184 | bytes 9486336 | tf_op jit(solution)/shard_map/tkbc,ktb->tc/dot_general | solution.py:221
  40.2 0.0 copy-done.2
  40.2 0.0 copy-done.3
  40.3 0.0 copy-done.4
  40.3 0.1 fusion.7
  40.3 0.0 copy-done.5
  40.4 0.1 fusion.15
  40.5 6.2 %fusion.10 = f32[16,1,2,384]{3,1,2,0:T(1,128)S(1)} fusion(bf16[16,2,384,384]{3,2,1,0:T(8,128)(2,1)} %param.9, bf16[16,384,1,1]{1,0,2,3:T(8,128)(2,1)S(1)} %fusion.15), kind=kOutput, calls=%fused_computation.18 | convolution fusion | flops 9437184 | bytes 9498624 | tf_op jit(solution)/shard_map/tkbc,tc->ktb/dot_general | solution.py:216
  46.7 0.6 copy.40
  47.3 17.7 %shard_map.105 = bf16[2,16,384]{2,1,0:T(8,128)(2,1)} custom-call(s32[16,2]{1,0:T(8,128)} %copy.11.refs_0_, f32[2,16,384]{2,1,0:T(8,128)} %bitcast.46, f32[32,384]{1,0:T(8,128)} %refs_2_.3, f32[32,384]{1,0:T(8,128)} %refs_3_.3), custom_call_target="tpu_custom_call" | custom-call | tf_op jit(solution)/shard_map/pallas_call | solution.py:193
  65.0 0.0 copy-start
  65.0 0.0 copy-start.1
  65.0 5.1 %fusion = f32[16,1,384,1]{2,1,3,0:T(1,128)S(1)} fusion(bf16[16,2,384,384]{3,2,1,0:T(8,128)(2,1)} %param.9, bf16[2,16,384,1]{2,1,0,3:T(8,128)(2,1)} %bitcast.43), kind=kOutput, calls=%fused_computation.1 | convolution fusion | flops 9437184 | bytes 9486336 | tf_op jit(solution)/shard_map/tkbc,ktb->tc/dot_general | solution.py:221
  70.1 0.1 fusion.5
  70.2 0.7 convert_bitcast_fusion
  70.9 6.2 %fusion.8 = f32[16,1,2,384]{3,1,2,0:T(1,128)S(1)} fusion(bf16[16,2,384,384]{3,2,1,0:T(8,128)(2,1)} %param.9, bf16[16,384,1,1]{1,0,2,3:T(8,128)(2,1)S(1)} %get-tuple-element.2), kind=kOutput, calls=%fused_computation.16 | convolution fusion | flops 9437184 | bytes 9498624 | tf_op jit(solution)/shard_map/tkbc,tc->ktb/dot_general | solution.py:216
  77.1 0.6 copy.39
  77.8 17.3 %shard_map.106 = f32[32,384]{1,0:T(8,128)} custom-call(s32[16,2]{1,0:T(8,128)} %copy.11.refs_0_, f32[2,16,384]{2,1,0:T(8,128)} %bitcast.44), custom_call_target="tpu_custom_call" | custom-call | tf_op jit(solution)/shard_map/pallas_call | solution.py:193
  95.1 0.0 copy-done
  95.1 0.0 copy-done.1
  95.1 1.4 %multiply_add_fusion = f32[32,384]{1,0:T(8,128)} fusion(f32[32,384]{1,0:T(8,128)S(1)} %copy-done, f32[32,384]{1,0:T(8,128)S(1)} %copy-done.1, f32[32,384]{1,0:T(8,128)} %shard_map.106), kind=kLoop, calls=%fused_computation.7 | loop fusion | flops 24576 | bytes 196608 | tf_op jit(solution)/shard_map/add | solution.py:224
  (5 shorter events, 0.1 us)
Async XLA Ops:
  3.4 36.8 %copy-start.2 = (f32[16,384]{1,0:T(8,128)S(1)}, f32[16,384]{1,0:T(8,128)}, u32[]{:S(2)}) copy-start(f32[16,384]{1,0:T(8,128)} %param.17) | copy-start | bytes 73732
  3.4 36.8 %copy-start.3 = (f32[16,384]{1,0:T(8,128)S(1)}, f32[16,384]{1,0:T(8,128)}, u32[]{:S(2)}) copy-start(f32[16,384]{1,0:T(8,128)} %param.15) | copy-start | bytes 73732
  3.4 36.8 %copy-start.4 = (f32[16,384]{1,0:T(8,128)S(1)}, f32[16,384]{1,0:T(8,128)}, u32[]{:S(2)}) copy-start(f32[16,384]{1,0:T(8,128)} %param.14) | copy-start | bytes 73732
  3.5 36.9 %copy-start.5 = (f32[16,128]{1,0:T(8,128)S(1)}, f32[16,128]{1,0:T(8,128)}, u32[]{:S(2)}) copy-start(f32[16,128]{1,0:T(8,128)} %param.16) | copy-start | bytes 24580
  65.0 30.0 %copy-start = (f32[32,384]{1,0:T(8,128)S(1)}, f32[32,384]{1,0:T(8,128)}, u32[]{:S(2)}) copy-start(f32[32,384]{1,0:T(8,128)} %refs_2_.3) | copy-start | bytes 147460
  65.0 30.0 %copy-start.1 = (f32[32,384]{1,0:T(8,128)S(1)}, f32[32,384]{1,0:T(8,128)}, u32[]{:S(2)}) copy-start(f32[32,384]{1,0:T(8,128)} %refs_3_.3) | copy-start | bytes 147460

commit v4 on v3

--- a/solution.py
+++ b/solution.py
@@ -42,7 +42,7 @@
     acc = None
     for t in range(tiles):
         row = push_ref[column, t : t + 1, :]
-        term = jnp.where(slot == tb_ref[t, column], row, 0.0)
+        term = jnp.where(slot == tb_ref[column, t], row, 0.0)
         acc = term if acc is None else acc + term
     return acc
 
@@ -52,13 +52,13 @@
     if last:
         (tb_ref, push_ref,
          tot_out,
-         own_buf, later_buf, recv3, xbuf, ybuf, tot_buf,
-         s_sem, r_sem, sx_sem, rx_sem, sy_sem, ry_sem) = refs
+         own_buf, later_buf, recv3, gbuf, tot_buf,
+         s_sem, r_sem, gs_sem, gr_sem) = refs
     else:
         (tb_ref, push_ref, vfree_ref, imass_ref,
          rows_out,
-         own_buf, later_buf, recv3, xbuf, ybuf, vel_buf, vel_next, velf, rows_buf,
-         s_sem, r_sem, sx_sem, rx_sem, sy_sem, ry_sem) = refs
+         own_buf, later_buf, recv3, gbuf, vel_buf, vel_next, velf, rows_buf,
+         s_sem, r_sem, gs_sem, gr_sem) = refs
     blocks = own_buf.shape[0]
     width = own_buf.shape[1]
     half = blocks // 2
@@ -70,11 +70,12 @@
     mate = c + 1 - 2 * core
     up = lax.rem(b + 1, n_body)
     down = lax.rem(b + n_body - 1, n_body)
-    x_peers = [(y * gx + lax.rem(x + j, gx)) * 2 + core for j in range(1, gx)]
-    y_peers = [(lax.rem(y + j, gy) * gx + x) * 2 + core for j in range(1, gy)]
+    group = gx * gy
+    q = c // 2
+    peers = [lax.rem(q + j, group) * 2 + core for j in range(1, group)]
 
     greet = [(mate, b), (c, up), (mate, up), (c, down), (mate, down)]
-    greet += [(p, b) for p in x_peers] + [(p, b) for p in y_peers]
+    greet += [(p, b) for p in peers]
     barrier = pltpu.get_barrier_semaphore()
     for dev in greet:
         pl.semaphore_signal(barrier, inc=1, device_id=dev, device_id_type=MESH)
@@ -102,23 +103,18 @@
         remote(own_buf.at[mine], recv3.at[k], s_sem.at[k], r_sem.at[k], dev).wait_recv()
     part = own_buf[mine] + recv3[0] + recv3[1] + recv3[2]
 
-    for buf, pos, peers, size, ssem, rsem in (
-        (xbuf, x, x_peers, gx, sx_sem, rx_sem),
-        (ybuf, y, y_peers, gy, sy_sem, ry_sem),
-    ):
-        if size == 1:
-            continue
-        buf[pos] = part
+    if group > 1:
+        gbuf[q] = part
         for j, p in enumerate(peers):
-            cp = remote(buf.at[pos], buf.at[pos], ssem.at[j], rsem.at[pos], (p, b))
+            cp = remote(gbuf.at[q], gbuf.at[q], gs_sem.at[j], gr_sem.at[q], (p, b))
             cp.start()
             sent.append(cp)
-        for j in range(1, size):
-            src_pos = lax.rem(pos + size - j, size)
-            remote(buf.at[src_pos], buf.at[src_pos], ssem.at[0], rsem.at[src_pos], (peers[-j], b)).wait_recv()
-        part = buf[0]
-        for g in range(1, size):
-            part = part + buf[g]
+        for j in range(1, group):
+            src_q = lax.rem(q + group - j, group)
+            remote(gbuf.at[src_q], gbuf.at[src_q], gs_sem.at[0], gr_sem.at[src_q], (peers[-j], b)).wait_recv()
+        part = gbuf[0]
+        for g in range(1, group):
+            part = part + gbuf[g]
 
     if last:
         tot_buf[mine] = part
@@ -150,7 +146,7 @@
         tiles = rows_buf.shape[1]
         for column in range(2):
             for t in range(tiles):
-                rows_buf[column, pl.ds(t, 1), :] = velf[column, pl.ds(tb_ref[t, column], 1), :]
+                rows_buf[column, pl.ds(t, 1), :] = velf[column, pl.ds(tb_ref[column, t], 1), :]
             rows_out[column] = rows_buf[column].astype(jnp.bfloat16)
     for cp in sent:
         cp.wait_send()
@@ -180,15 +176,12 @@
         pltpu.VMEM((blocks, width), jnp.float32),
         pltpu.VMEM((blocks, width), jnp.float32),
         pltpu.VMEM((3, half, width), jnp.float32),
-        pltpu.VMEM((gx, half, width), jnp.float32),
-        pltpu.VMEM((gy, half, width), jnp.float32),
+        pltpu.VMEM((gx * gy, half, width), jnp.float32),
         *tail,
         pltpu.SemaphoreType.DMA((6,)),
         pltpu.SemaphoreType.DMA((6,)),
-        pltpu.SemaphoreType.DMA((max(gx - 1, 1),)),
-        pltpu.SemaphoreType.DMA((gx,)),
-        pltpu.SemaphoreType.DMA((max(gy - 1, 1),)),
-        pltpu.SemaphoreType.DMA((gy,)),
+        pltpu.SemaphoreType.DMA((max(gx * gy - 1, 1),)),
+        pltpu.SemaphoreType.DMA((gx * gy,)),
     ]
     return pl.pallas_call(
         functools.partial(sweep_kernel, n_contact, n_body, last),
@@ -217,10 +210,10 @@
 
     lam = impulse_start * mask
     for sweep in range(ITERS):
-        rows = sweep_exchange(tile_block, pushes(lam), vel_free, inv_mass, n_contact, n_body, False)
+        rows = sweep_exchange(tile_block.T, pushes(lam), vel_free, inv_mass, n_contact, n_body, False)
         rel = jnp.einsum("tkbc,ktb->tc", jacobian, rows, preferred_element_type=jnp.float32) + bias
         lam = project(lam - step_scale * rel, friction, contacts) * mask
-    total = sweep_exchange(tile_block, pushes(lam), vel_free, inv_mass, n_contact, n_body, True)
+    total = sweep_exchange(tile_block.T, pushes(lam), vel_free, inv_mass, n_contact, n_body, True)
     velocity = vel_free + inv_mass * total
     return (lam, velocity)
 

time: 97 us -> 99.6 us (1.027)
  Pallas kernels: 59.8 us -> 63.7 us
  local copies, waits for them, and re-layouts: 3.31 us -> 1.97 us
    pallas_call x3, Pallas kernels: 59.8 us -> 63.7 us  [sweep_exchange(): pl.pallas_call(functools.partial(sweep_kernel, n_contact, n_body, last),...]
    unnamed x13 -> x12, local copies, waits for them, and re-layouts: 1.38 us -> 0.03 us
where the time goes in v4:
time: 99.6 us; the launch traced here: 99.1 us
  Pallas kernels  63.7 us (64%)
  matrix products  28.8 us (29%)
  other arithmetic  3.21 us (3%)
  local copies, waits for them, and re-layouts  1.97 us (2%)
  between operations  1.4 us (1%)
    pallas_call x3, Pallas kernels, sweep_exchange(): pl.pallas_call(functools.partial(sweep_kernel, n_contact, n_body, last),...  63.7 us
    dot_general x3, matrix products, pushes(): jnp.einsum('tkbc,tc->ktb', jacobian, lamb, preferred_element_type=jnp.flo...  18.7 us
    dot_general x2, matrix products, per_device(): jnp.einsum('tkbc,ktb->tc', jacobian, rows, preferred_element_type=jnp.flo...  10.2 us

profile of v4, /device:TPU:1, one launch (start us, length us, event | category | flops | bytes accessed | tf_op | source)
XLA Modules:
  0.0 99.1 jit_solution(5767640604344414451)
XLA Ops:
  1.3 0.8 fusion.16
  2.1 0.0 copy-start.2
  2.1 0.0 copy-start.3
  2.1 0.0 copy-start.4
  2.1 0.0 copy-start.5
  2.1 6.2 %fusion.12 = f32[16,1,2,384]{3,1,2,0:T(1,128)S(1)} fusion(bf16[16,2,384,384]{3,2,1,0:T(8,128)(2,1)} %param.9, bf16[16,384,1,1]{1,0,2,3:T(8,128)(2,1)S(1)} %fusion.16), kind=kOutput, calls=%fused_computation.20 | convolution fusion | flops 9437184 | bytes 9498624 | tf_op jit(solution)/shard_map/tkbc,tc->ktb/dot_general | solution.py:209
  8.4 0.6 copy.38
  9.0 24.2 %shard_map.104 = bf16[2,16,384]{2,1,0:T(8,128)(2,1)} custom-call(s32[2,16]{1,0:T(2,128)} %bitcast.48, f32[2,16,384]{2,1,0:T(8,128)} %bitcast.46, f32[32,384]{1,0:T(8,128)} %refs_2_.3, f32[32,384]{1,0:T(8,128)} %refs_3_.3), custom_call_target="tpu_custom_call" | custom-call | tf_op jit(solution)/shard_map/pallas_call | solution.py:186
  33.2 5.1 %fusion.2 = f32[16,1,384,1]{2,1,3,0:T(1,128)S(1)} fusion(bf16[16,2,384,384]{3,2,1,0:T(8,128)(2,1)} %param.9, bf16[2,16,384,1]{2,1,0,3:T(8,128)(2,1)} %bitcast.43), kind=kOutput, calls=%fused_computation.4 | convolution fusion | flops 9437184 | bytes 9486336 | tf_op jit(solution)/shard_map/tkbc,ktb->tc/dot_general | solution.py:214
  38.3 0.0 copy-done.2
  38.3 0.0 copy-done.3
  38.3 0.0 copy-done.4
  38.3 0.1 fusion.7
  38.4 0.0 copy-done.5
  38.4 0.1 fusion.15
  38.5 6.2 %fusion.10 = f32[16,1,2,384]{3,1,2,0:T(1,128)S(1)} fusion(bf16[16,2,384,384]{3,2,1,0:T(8,128)(2,1)} %param.9, bf16[16,384,1,1]{1,0,2,3:T(8,128)(2,1)S(1)} %fusion.15), kind=kOutput, calls=%fused_computation.18 | convolution fusion | flops 9437184 | bytes 9498624 | tf_op jit(solution)/shard_map/tkbc,tc->ktb/dot_general | solution.py:209
  44.7 0.6 copy.37
  45.4 19.9 %shard_map.105 = bf16[2,16,384]{2,1,0:T(8,128)(2,1)} custom-call(s32[2,16]{1,0:T(2,128)} %bitcast.49, f32[2,16,384]{2,1,0:T(8,128)} %bitcast.47, f32[32,384]{1,0:T(8,128)} %refs_2_.3, f32[32,384]{1,0:T(8,128)} %refs_3_.3), custom_call_target="tpu_custom_call" | custom-call | tf_op jit(solution)/shard_map/pallas_call | solution.py:186
  65.3 0.0 copy-start
  65.3 0.0 copy-start.1
  65.3 5.1 %fusion = f32[16,1,384,1]{2,1,3,0:T(1,128)S(1)} fusion(bf16[16,2,384,384]{3,2,1,0:T(8,128)(2,1)} %param.9, bf16[2,16,384,1]{2,1,0,3:T(8,128)(2,1)} %bitcast.44), kind=kOutput, calls=%fused_computation.1 | convolution fusion | flops 9437184 | bytes 9486336 | tf_op jit(solution)/shard_map/tkbc,ktb->tc/dot_general | solution.py:214
  70.4 0.1 fusion.5
  70.5 0.7 convert_bitcast_fusion
  71.2 6.2 %fusion.8 = f32[16,1,2,384]{3,1,2,0:T(1,128)S(1)} fusion(bf16[16,2,384,384]{3,2,1,0:T(8,128)(2,1)} %param.9, bf16[16,384,1,1]{1,0,2,3:T(8,128)(2,1)S(1)} %get-tuple-element.2), kind=kOutput, calls=%fused_computation.16 | convolution fusion | flops 9437184 | bytes 9498624 | tf_op jit(solution)/shard_map/tkbc,tc->ktb/dot_general | solution.py:209
  77.4 0.6 copy.36
  78.0 19.6 %shard_map.106 = f32[32,384]{1,0:T(8,128)} custom-call(s32[2,16]{1,0:T(2,128)} %bitcast.50, f32[2,16,384]{2,1,0:T(8,128)} %bitcast.45), custom_call_target="tpu_custom_call" | custom-call | tf_op jit(solution)/shard_map/pallas_call | solution.py:186
  97.7 0.0 copy-done
  97.7 0.0 copy-done.1
  97.7 1.4 %multiply_add_fusion = f32[32,384]{1,0:T(8,128)} fusion(f32[32,384]{1,0:T(8,128)S(1)} %copy-done, f32[32,384]{1,0:T(8,128)S(1)} %copy-done.1, f32[32,384]{1,0:T(8,128)} %shard_map.106), kind=kLoop, calls=%fused_computation.7 | loop fusion | flops 24576 | bytes 196608 | tf_op jit(solution)/shard_map/add | solution.py:217
  (5 shorter events, 0.1 us)
Async XLA Ops:
  2.1 36.2 %copy-start.2 = (f32[16,384]{1,0:T(8,128)S(1)}, f32[16,384]{1,0:T(8,128)}, u32[]{:S(2)}) copy-start(f32[16,384]{1,0:T(8,128)} %param.17) | copy-start | bytes 73732
  2.1 36.2 %copy-start.3 = (f32[16,384]{1,0:T(8,128)S(1)}, f32[16,384]{1,0:T(8,128)}, u32[]{:S(2)}) copy-start(f32[16,384]{1,0:T(8,128)} %param.15) | copy-start | bytes 73732
  2.1 36.2 %copy-start.4 = (f32[16,384]{1,0:T(8,128)S(1)}, f32[16,384]{1,0:T(8,128)}, u32[]{:S(2)}) copy-start(f32[16,384]{1,0:T(8,128)} %param.14) | copy-start | bytes 73732
  2.1 36.3 %copy-start.5 = (f32[16,128]{1,0:T(8,128)S(1)}, f32[16,128]{1,0:T(8,128)}, u32[]{:S(2)}) copy-start(f32[16,128]{1,0:T(8,128)} %param.16) | copy-start | bytes 24580
  65.3 32.4 %copy-start = (f32[32,384]{1,0:T(8,128)S(1)}, f32[32,384]{1,0:T(8,128)}, u32[]{:S(2)}) copy-start(f32[32,384]{1,0:T(8,128)} %refs_2_.3) | copy-start | bytes 147460
  65.3 32.4 %copy-start.1 = (f32[32,384]{1,0:T(8,128)S(1)}, f32[32,384]{1,0:T(8,128)}, u32[]{:S(2)}) copy-start(f32[32,384]{1,0:T(8,128)} %refs_3_.3) | copy-start | bytes 147460

commit v5 on v3

--- a/solution.py
+++ b/solution.py
@@ -42,7 +42,7 @@
     acc = None
     for t in range(tiles):
         row = push_ref[column, t : t + 1, :]
-        term = jnp.where(slot == tb_ref[t, column], row, 0.0)
+        term = jnp.where(slot == tb_ref[column, t], row, 0.0)
         acc = term if acc is None else acc + term
     return acc
 
@@ -150,7 +150,7 @@
         tiles = rows_buf.shape[1]
         for column in range(2):
             for t in range(tiles):
-                rows_buf[column, pl.ds(t, 1), :] = velf[column, pl.ds(tb_ref[t, column], 1), :]
+                rows_buf[column, pl.ds(t, 1), :] = velf[column, pl.ds(tb_ref[column, t], 1), :]
             rows_out[column] = rows_buf[column].astype(jnp.bfloat16)
     for cp in sent:
         cp.wait_send()
@@ -217,10 +217,10 @@
 
     lam = impulse_start * mask
     for sweep in range(ITERS):
-        rows = sweep_exchange(tile_block, pushes(lam), vel_free, inv_mass, n_contact, n_body, False)
+        rows = sweep_exchange(tile_block.T, pushes(lam), vel_free, inv_mass, n_contact, n_body, False)
         rel = jnp.einsum("tkbc,ktb->tc", jacobian, rows, preferred_element_type=jnp.float32) + bias
         lam = project(lam - step_scale * rel, friction, contacts) * mask
-    total = sweep_exchange(tile_block, pushes(lam), vel_free, inv_mass, n_contact, n_body, True)
+    total = sweep_exchange(tile_block.T, pushes(lam), vel_free, inv_mass, n_contact, n_body, True)
     velocity = vel_free + inv_mass * total
     return (lam, velocity)
 

time: 97 us -> 95.5 us (0.985)
  local copies, waits for them, and re-layouts: 3.31 us -> 1.97 us
    unnamed x13 -> x12, local copies, waits for them, and re-layouts: 1.38 us -> 0.03 us
where the time goes in v5:
time: 95.5 us; the launch traced here: 95 us
  Pallas kernels  59.6 us (62%)
  matrix products  28.8 us (30%)
  other arithmetic  3.21 us (3%)
  local copies, waits for them, and re-layouts  1.97 us (2%)
  between operations  1.4 us (1%)
    pallas_call x3, Pallas kernels, sweep_exchange(): pl.pallas_call(functools.partial(sweep_kernel, n_contact, n_body, last),...  59.6 us
    dot_general x3, matrix products, pushes(): jnp.einsum('tkbc,tc->ktb', jacobian, lamb, preferred_element_type=jnp.flo...  18.7 us
    dot_general x2, matrix products, per_device(): jnp.einsum('tkbc,ktb->tc', jacobian, rows, preferred_element_type=jnp.flo...  10.2 us
    dot_general x3, local copies, waits for them, and re-layouts, pushes(): jnp.einsum('tkbc,tc->ktb', jacobian, lamb, preferred_element_type=jnp.flo...  1.94 us

profile of v5, /device:TPU:1, one launch (start us, length us, event | category | flops | bytes accessed | tf_op | source)
XLA Modules:
  0.0 95.0 jit_solution(6187646901382377161)
XLA Ops:
  1.3 0.8 fusion.16
  2.1 0.0 copy-start.2
  2.1 0.0 copy-start.3
  2.1 0.0 copy-start.4
  2.1 0.0 copy-start.5
  2.1 6.2 %fusion.12 = f32[16,1,2,384]{3,1,2,0:T(1,128)S(1)} fusion(bf16[16,2,384,384]{3,2,1,0:T(8,128)(2,1)} %param.9, bf16[16,384,1,1]{1,0,2,3:T(8,128)(2,1)S(1)} %fusion.16), kind=kOutput, calls=%fused_computation.20 | convolution fusion | flops 9437184 | bytes 9498624 | tf_op jit(solution)/shard_map/tkbc,tc->ktb/dot_general | solution.py:216
  8.4 0.6 copy.38
  9.0 24.7 %shard_map.104 = bf16[2,16,384]{2,1,0:T(8,128)(2,1)} custom-call(s32[2,16]{1,0:T(2,128)} %bitcast.48, f32[2,16,384]{2,1,0:T(8,128)} %bitcast.46, f32[32,384]{1,0:T(8,128)} %refs_2_.3, f32[32,384]{1,0:T(8,128)} %refs_3_.3), custom_call_target="tpu_custom_call" | custom-call | tf_op jit(solution)/shard_map/pallas_call | solution.py:193
  33.8 5.1 %fusion.2 = f32[16,1,384,1]{2,1,3,0:T(1,128)S(1)} fusion(bf16[16,2,384,384]{3,2,1,0:T(8,128)(2,1)} %param.9, bf16[2,16,384,1]{2,1,0,3:T(8,128)(2,1)} %bitcast.43), kind=kOutput, calls=%fused_computation.4 | convolution fusion | flops 9437184 | bytes 9486336 | tf_op jit(solution)/shard_map/tkbc,ktb->tc/dot_general | solution.py:221
  38.8 0.0 copy-done.2
  38.8 0.0 copy-done.3
  38.8 0.0 copy-done.4
  38.8 0.1 fusion.7
  38.9 0.0 copy-done.5
  39.0 0.1 fusion.15
  39.0 6.2 %fusion.10 = f32[16,1,2,384]{3,1,2,0:T(1,128)S(1)} fusion(bf16[16,2,384,384]{3,2,1,0:T(8,128)(2,1)} %param.9, bf16[16,384,1,1]{1,0,2,3:T(8,128)(2,1)S(1)} %fusion.15), kind=kOutput, calls=%fused_computation.18 | convolution fusion | flops 9437184 | bytes 9498624 | tf_op jit(solution)/shard_map/tkbc,tc->ktb/dot_general | solution.py:216
  45.2 0.6 copy.37
  45.9 17.6 %shard_map.105 = bf16[2,16,384]{2,1,0:T(8,128)(2,1)} custom-call(s32[2,16]{1,0:T(2,128)} %bitcast.49, f32[2,16,384]{2,1,0:T(8,128)} %bitcast.47, f32[32,384]{1,0:T(8,128)} %refs_2_.3, f32[32,384]{1,0:T(8,128)} %refs_3_.3), custom_call_target="tpu_custom_call" | custom-call | tf_op jit(solution)/shard_map/pallas_call | solution.py:193
  63.5 0.0 copy-start
  63.5 0.0 copy-start.1
  63.5 5.1 %fusion = f32[16,1,384,1]{2,1,3,0:T(1,128)S(1)} fusion(bf16[16,2,384,384]{3,2,1,0:T(8,128)(2,1)} %param.9, bf16[2,16,384,1]{2,1,0,3:T(8,128)(2,1)} %bitcast.44), kind=kOutput, calls=%fused_computation.1 | convolution fusion | flops 9437184 | bytes 9486336 | tf_op jit(solution)/shard_map/tkbc,ktb->tc/dot_general | solution.py:221
  68.6 0.1 fusion.5
  68.8 0.7 convert_bitcast_fusion
  69.4 6.2 %fusion.8 = f32[16,1,2,384]{3,1,2,0:T(1,128)S(1)} fusion(bf16[16,2,384,384]{3,2,1,0:T(8,128)(2,1)} %param.9, bf16[16,384,1,1]{1,0,2,3:T(8,128)(2,1)S(1)} %get-tuple-element.2), kind=kOutput, calls=%fused_computation.16 | convolution fusion | flops 9437184 | bytes 9498624 | tf_op jit(solution)/shard_map/tkbc,tc->ktb/dot_general | solution.py:216
  75.6 0.6 copy.36
  76.3 17.3 %shard_map.106 = f32[32,384]{1,0:T(8,128)} custom-call(s32[2,16]{1,0:T(2,128)} %bitcast.50, f32[2,16,384]{2,1,0:T(8,128)} %bitcast.45), custom_call_target="tpu_custom_call" | custom-call | tf_op jit(solution)/shard_map/pallas_call | solution.py:193
  93.6 0.0 copy-done
  93.6 0.0 copy-done.1
  93.6 1.4 %multiply_add_fusion = f32[32,384]{1,0:T(8,128)} fusion(f32[32,384]{1,0:T(8,128)S(1)} %copy-done, f32[32,384]{1,0:T(8,128)S(1)} %copy-done.1, f32[32,384]{1,0:T(8,128)} %shard_map.106), kind=kLoop, calls=%fused_computation.7 | loop fusion | flops 24576 | bytes 196608 | tf_op jit(solution)/shard_map/add | solution.py:224
  (5 shorter events, 0.1 us)
Async XLA Ops:
  2.1 36.7 %copy-start.2 = (f32[16,384]{1,0:T(8,128)S(1)}, f32[16,384]{1,0:T(8,128)}, u32[]{:S(2)}) copy-start(f32[16,384]{1,0:T(8,128)} %param.17) | copy-start | bytes 73732
  2.1 36.7 %copy-start.3 = (f32[16,384]{1,0:T(8,128)S(1)}, f32[16,384]{1,0:T(8,128)}, u32[]{:S(2)}) copy-start(f32[16,384]{1,0:T(8,128)} %param.15) | copy-start | bytes 73732
  2.1 36.7 %copy-start.4 = (f32[16,384]{1,0:T(8,128)S(1)}, f32[16,384]{1,0:T(8,128)}, u32[]{:S(2)}) copy-start(f32[16,384]{1,0:T(8,128)} %param.14) | copy-start | bytes 73732
  2.1 36.8 %copy-start.5 = (f32[16,128]{1,0:T(8,128)S(1)}, f32[16,128]{1,0:T(8,128)}, u32[]{:S(2)}) copy-start(f32[16,128]{1,0:T(8,128)} %param.16) | copy-start | bytes 24580
  63.5 30.0 %copy-start = (f32[32,384]{1,0:T(8,128)S(1)}, f32[32,384]{1,0:T(8,128)}, u32[]{:S(2)}) copy-start(f32[32,384]{1,0:T(8,128)} %refs_2_.3) | copy-start | bytes 147460
  63.5 30.0 %copy-start.1 = (f32[32,384]{1,0:T(8,128)S(1)}, f32[32,384]{1,0:T(8,128)}, u32[]{:S(2)}) copy-start(f32[32,384]{1,0:T(8,128)} %refs_3_.3) | copy-start | bytes 147460

commit v6 on v5

--- a/solution.py
+++ b/solution.py
@@ -202,6 +202,139 @@
     )(*args)
 
 
+def dual_kernel(n_contact, n_body, *refs):
+    gx, gy = contact_groups(n_contact)
+    (tb_ref, push_ref, vfree_ref, imass_ref, vnext_ref,
+     rows_out,
+     own_buf, later_buf, recv6, xbuf, ybuf, vel_buf, velf, rows_buf,
+     s_sem, r_sem, sx_sem, rx_sem, sy_sem, ry_sem) = refs
+    blocks = own_buf.shape[0]
+    width = own_buf.shape[1]
+    half = blocks // 2
+    c = lax.axis_index("contact")
+    b = lax.axis_index("body")
+    core = lax.rem(c, 2)
+    x = lax.rem(c // 2, gx)
+    y = c // (2 * gx)
+    mate = c + 1 - 2 * core
+    up = lax.rem(b + 1, n_body)
+    down = lax.rem(b + n_body - 1, n_body)
+    x_peers = [(y * gx + lax.rem(x + j, gx)) * 2 + core for j in range(1, gx)]
+    y_peers = [(lax.rem(y + j, gy) * gx + x) * 2 + core for j in range(1, gy)]
+
+    greet = [(mate, b), (c, up), (mate, up), (c, down), (mate, down)]
+    greet += [(p, b) for p in x_peers] + [(p, b) for p in y_peers]
+    barrier = pltpu.get_barrier_semaphore()
+    for dev in greet:
+        pl.semaphore_signal(barrier, inc=1, device_id=dev, device_id_type=MESH)
+    pl.semaphore_wait(barrier, len(greet))
+
+    def remote(src, dst, send, recv, dev):
+        return pltpu.make_async_remote_copy(
+            src_ref=src, dst_ref=dst, send_sem=send, recv_sem=recv,
+            device_id=dev, device_id_type=MESH,
+        )
+
+    mine = pl.ds(pl.multiple_of(core * half, half), half)
+    theirs = pl.ds(pl.multiple_of((1 - core) * half, half), half)
+    sent = []
+    later_buf[...] = scatter_rows(tb_ref, 1, push_ref, blocks)
+    plan = (
+        (later_buf.at[mine], (c, up)),
+        (later_buf.at[theirs], (mate, up)),
+        (later_buf.at[theirs], (mate, b)),
+    )
+    for k, (src, dev) in enumerate(plan):
+        cp = remote(src, recv6.at[k], s_sem.at[k], r_sem.at[k], dev)
+        cp.start()
+        sent.append(cp)
+    own_buf[...] = scatter_rows(tb_ref, 0, push_ref, blocks)
+    plan = (
+        (own_buf.at[mine], (c, down)),
+        (own_buf.at[theirs], (mate, down)),
+        (own_buf.at[theirs], (mate, b)),
+    )
+    for k, (src, dev) in enumerate(plan):
+        cp = remote(src, recv6.at[3 + k], s_sem.at[3 + k], r_sem.at[3 + k], dev)
+        cp.start()
+        sent.append(cp)
+    senders = ((c, down), (mate, down), (mate, b), (c, up), (mate, up), (mate, b))
+    for k, dev in enumerate(senders):
+        remote(own_buf.at[mine], recv6.at[k], s_sem.at[k], r_sem.at[k], dev).wait_recv()
+    part = jnp.concatenate([
+        own_buf[mine] + recv6[5] + recv6[0] + recv6[1],
+        later_buf[mine] + recv6[2] + recv6[3] + recv6[4],
+    ], axis=0)
+
+    for buf, pos, peers, size, ssem, rsem in (
+        (xbuf, x, x_peers, gx, sx_sem, rx_sem),
+        (ybuf, y, y_peers, gy, sy_sem, ry_sem),
+    ):
+        if size == 1:
+            continue
+        buf[pos] = part
+        for j, p in enumerate(peers):
+            cp = remote(buf.at[pos], buf.at[pos], ssem.at[j], rsem.at[pos], (p, b))
+            cp.start()
+            sent.append(cp)
+        for j in range(1, size):
+            src_pos = lax.rem(pos + size - j, size)
+            remote(buf.at[src_pos], buf.at[src_pos], ssem.at[0], rsem.at[src_pos], (peers[-j], b)).wait_recv()
+        part = buf[0]
+        for g in range(1, size):
+            part = part + buf[g]
+
+    vel_buf[0, mine] = (vfree_ref[mine] + imass_ref[mine] * part[:half]).astype(jnp.bfloat16)
+    vel_buf[1, mine] = (vnext_ref[0, mine] + vnext_ref[1, mine] * part[half:]).astype(jnp.bfloat16)
+    for k in range(2):
+        cp = remote(vel_buf.at[k, mine], vel_buf.at[k, mine], s_sem.at[6 + k], r_sem.at[6 + k], (mate, b))
+        cp.start()
+        sent.append(cp)
+    for k in range(2):
+        remote(vel_buf.at[k, theirs], vel_buf.at[k, theirs], s_sem.at[6 + k], r_sem.at[6 + k], (mate, b)).wait_recv()
+    velf[...] = vel_buf[...].astype(jnp.float32)
+    tiles = rows_buf.shape[1]
+    for column in range(2):
+        for t in range(tiles):
+            rows_buf[column, pl.ds(t, 1), :] = velf[column, pl.ds(tb_ref[column, t], 1), :]
+        rows_out[column] = rows_buf[column].astype(jnp.bfloat16)
+    for cp in sent:
+        cp.wait_send()
+
+
+def dual_exchange(tile_block, push, vel_free, inv_mass, vnext, n_contact, n_body):
+    gx, gy = contact_groups(n_contact)
+    blocks, width = vel_free.shape
+    tiles = push.shape[1]
+    half = blocks // 2
+    vspec = pl.BlockSpec(memory_space=pltpu.VMEM)
+    sspec = pl.BlockSpec(memory_space=pltpu.SMEM)
+    scratch = [
+        pltpu.VMEM((blocks, width), jnp.float32),
+        pltpu.VMEM((blocks, width), jnp.float32),
+        pltpu.VMEM((6, half, width), jnp.float32),
+        pltpu.VMEM((gx, blocks, width), jnp.float32),
+        pltpu.VMEM((gy, blocks, width), jnp.float32),
+        pltpu.VMEM((2, blocks, width), jnp.bfloat16),
+        pltpu.VMEM((2, blocks, width), jnp.float32),
+        pltpu.VMEM((2, tiles, width), jnp.float32),
+        pltpu.SemaphoreType.DMA((8,)),
+        pltpu.SemaphoreType.DMA((8,)),
+        pltpu.SemaphoreType.DMA((max(gx - 1, 1),)),
+        pltpu.SemaphoreType.DMA((gx,)),
+        pltpu.SemaphoreType.DMA((max(gy - 1, 1),)),
+        pltpu.SemaphoreType.DMA((gy,)),
+    ]
+    return pl.pallas_call(
+        functools.partial(dual_kernel, n_contact, n_body),
+        out_shape=jax.ShapeDtypeStruct((2, tiles, width), jnp.bfloat16),
+        in_specs=[sspec] + [vspec] * 4,
+        out_specs=vspec,
+        scratch_shapes=scratch,
+        compiler_params=pltpu.CompilerParams(collective_id=2, has_side_effects=True),
+    )(tile_block, push, vel_free, inv_mass, vnext)
+
+
 def per_device(
     n_contact, n_body,
     jacobian, tile_block, tile_count, vel_free, inv_mass, bias, step_scale, friction, impulse_start,
@@ -215,9 +348,14 @@
         lamb = lam.astype(jnp.bfloat16)
         return jnp.einsum("tkbc,tc->ktb", jacobian, lamb, preferred_element_type=jnp.float32)
 
+    count = lax.axis_size("body")
+    vnext = lax.ppermute(
+        jnp.stack([vel_free, inv_mass]), "body",
+        [(source, (source + count - 1) % count) for source in range(count)],
+    )
     lam = impulse_start * mask
     for sweep in range(ITERS):
-        rows = sweep_exchange(tile_block.T, pushes(lam), vel_free, inv_mass, n_contact, n_body, False)
+        rows = dual_exchange(tile_block.T, pushes(lam), vel_free, inv_mass, vnext, n_contact, n_body)
         rel = jnp.einsum("tkbc,ktb->tc", jacobian, rows, preferred_element_type=jnp.float32) + bias
         lam = project(lam - step_scale * rel, friction, contacts) * mask
     total = sweep_exchange(tile_block.T, pushes(lam), vel_free, inv_mass, n_contact, n_body, True)

time: 95.5 us -> 97.7 us (1.023)
  starting transfers between devices: 0 us -> 6.47 us
  Pallas kernels: 59.6 us -> 53.8 us
    pallas_call x3 -> x1, Pallas kernels: 59.6 us -> 15.4 us  [sweep_exchange(): pl.pallas_call(functools.partial(sweep_kernel, n_contact, n_body, last),...]
    pallas_call x0 -> x2, Pallas kernels: none -> 38.4 us  [dual_exchange(): pl.pallas_call(functools.partial(dual_kernel, n_contact, n_body), out_sha...]
    ppermute x0 -> x1, starting transfers between devices: none -> 6.47 us  [per_device(): lax.ppermute(jnp.stack([vel_free, inv_mass]), 'body', [(source, (source +...]
  transfers between devices with their start and end apart: 0 -> 1, of which waited for: 0 -> 0; matrix products, arithmetic and copies ran while one was open for 0% -> 8% of each run, Pallas kernels for 0% -> 0%
where the time goes in v6:
time: 97.7 us; the launch traced here: 97.1 us
  Pallas kernels  53.8 us (55%)
  matrix products  28.8 us (29%)
  starting transfers between devices  6.47 us (7%)
  other arithmetic  4.05 us (4%)
  local copies, waits for them, and re-layouts  2.6 us (3%)
  between operations  1.41 us (1%)
    pallas_call x2, Pallas kernels, dual_exchange(): pl.pallas_call(functools.partial(dual_kernel, n_contact, n_body), out_sha...  38.4 us
    dot_general x3, matrix products, pushes(): jnp.einsum('tkbc,tc->ktb', jacobian, lamb, preferred_element_type=jnp.flo...  18.7 us
    pallas_call x1, Pallas kernels, sweep_exchange(): pl.pallas_call(functools.partial(sweep_kernel, n_contact, n_body, last),...  15.4 us
    dot_general x2, matrix products, per_device(): jnp.einsum('tkbc,ktb->tc', jacobian, rows, preferred_element_type=jnp.flo...  10.2 us
    ppermute x1, starting transfers between devices, per_device(): lax.ppermute(jnp.stack([vel_free, inv_mass]), 'body', [(source, (source +...  6.47 us
  transfers between devices with their start and end apart: 1, of which 0 were waited for; matrix products, arithmetic and copies ran while one was open for 8% of the time, Pallas kernels for 0%

profile of v6, /device:TPU:1, one launch (start us, length us, event | category | flops | bytes accessed | tf_op | source)
XLA Modules:
  0.0 97.1 jit_solution(1845446032340069873)
XLA Ops:
  0.6 0.8 pad_maximum_fusion
  1.5 6.5 %collective-permute-start = (f32[2,32,384]{2,1,0:T(8,128)S(1)}, f32[2,32,384]{2,1,0:T(8,128)S(1)}, u32[]{:S(2)}, u32[]{:S(2)}) collective-permute-start(f32[2,32,384]{2,1,0:T(8,128)S(1)} %pad_maximum_fusion), channel_id=1, source_target_pairs={{0,7},{1,0},{2,1},{3,2},{4,3},{5,4},{6,5},{7,6},{8,15},{9,8},{10,9... | collective-permute-start | bytes 294920 | tf_op jit(solution)/shard_map/ppermute | solution.py:352
  8.6 0.8 fusion.16
  9.4 0.0 copy-start.3
  9.4 0.0 copy-start.4
  9.4 0.0 copy-start.6
  9.4 6.2 %fusion.12 = f32[16,1,2,384]{3,1,2,0:T(1,128)S(1)} fusion(bf16[16,2,384,384]{3,2,1,0:T(8,128)(2,1)} %param.9, bf16[16,384,1,1]{1,0,2,3:T(8,128)(2,1)S(1)} %fusion.16), kind=kOutput, calls=%fused_computation.21 | convolution fusion | flops 9437184 | bytes 9498624 | tf_op jit(solution)/shard_map/tkbc,tc->ktb/dot_general | solution.py:349
  15.7 0.6 copy.38
  16.3 0.0 collective-permute-done.refs_4_
  16.3 0.6 copy-done.2
  17.0 20.7 %shard_map.104 = bf16[2,16,384]{2,1,0:T(8,128)(2,1)} custom-call(s32[2,16]{1,0:T(2,128)} %bitcast.52, f32[2,16,384]{2,1,0:T(8,128)} %bitcast.50, f32[32,384]{1,0:T(8,128)} %refs_2_.3, f32[32,384]{1,0:T(8,128)} %refs_3_.3, f32[2,32,384]{2,1,0:T(8,128)} %copy-done.2), custom_call_target="tpu_custom_call" | custom-call | tf_op jit(solution)/shard_map/pallas_call | solution.py:328
  37.7 5.1 %fusion.2 = f32[16,1,384,1]{2,1,3,0:T(1,128)S(1)} fusion(bf16[16,2,384,384]{3,2,1,0:T(8,128)(2,1)} %param.9, bf16[2,16,384,1]{2,1,0,3:T(8,128)(2,1)} %bitcast.48), kind=kOutput, calls=%fused_computation.5 | convolution fusion | flops 9437184 | bytes 9486336 | tf_op jit(solution)/shard_map/tkbc,ktb->tc/dot_general | solution.py:359
  42.7 0.0 copy-done.3
  42.7 0.0 copy-done.4
  42.7 0.0 copy-done.5
  42.8 0.1 fusion.7
  42.8 0.0 copy-done.6
  42.9 0.1 fusion.15
  43.0 6.2 %fusion.10 = f32[16,1,2,384]{3,1,2,0:T(1,128)S(1)} fusion(bf16[16,2,384,384]{3,2,1,0:T(8,128)(2,1)} %param.9, bf16[16,384,1,1]{1,0,2,3:T(8,128)(2,1)S(1)} %fusion.15), kind=kOutput, calls=%fused_computation.19 | convolution fusion | flops 9437184 | bytes 9498624 | tf_op jit(solution)/shard_map/tkbc,tc->ktb/dot_general | solution.py:349
  49.2 0.6 copy.37
  49.8 17.7 %shard_map.105 = bf16[2,16,384]{2,1,0:T(8,128)(2,1)} custom-call(s32[2,16]{1,0:T(2,128)} %bitcast.53, f32[2,16,384]{2,1,0:T(8,128)} %bitcast.51, f32[32,384]{1,0:T(8,128)} %refs_2_.3, f32[32,384]{1,0:T(8,128)} %refs_3_.3, f32[2,32,384]{2,1,0:T(8,128)} %copy-done.2), custom_call_target="tpu_custom_call" | custom-call | tf_op jit(solution)/shard_map/pallas_call | solution.py:328
  67.5 0.0 copy-start
  67.5 0.0 copy-start.1
  67.5 5.1 %fusion = f32[16,1,384,1]{2,1,3,0:T(1,128)S(1)} fusion(bf16[16,2,384,384]{3,2,1,0:T(8,128)(2,1)} %param.9, bf16[2,16,384,1]{2,1,0,3:T(8,128)(2,1)} %bitcast.47), kind=kOutput, calls=%fused_computation.2 | convolution fusion | flops 9437184 | bytes 9486336 | tf_op jit(solution)/shard_map/tkbc,ktb->tc/dot_general | solution.py:359
  72.6 0.1 fusion.5
  72.7 0.7 convert_bitcast_fusion
  73.4 6.2 %fusion.8 = f32[16,1,2,384]{3,1,2,0:T(1,128)S(1)} fusion(bf16[16,2,384,384]{3,2,1,0:T(8,128)(2,1)} %param.9, bf16[16,384,1,1]{1,0,2,3:T(8,128)(2,1)S(1)} %get-tuple-element.2), kind=kOutput, calls=%fused_computation.17 | convolution fusion | flops 9437184 | bytes 9498624 | tf_op jit(solution)/shard_map/tkbc,tc->ktb/dot_general | solution.py:349
  79.6 0.6 copy.36
  80.2 15.4 %shard_map.106 = f32[32,384]{1,0:T(8,128)} custom-call(s32[2,16]{1,0:T(2,128)} %bitcast.54, f32[2,16,384]{2,1,0:T(8,128)} %bitcast.49), custom_call_target="tpu_custom_call" | custom-call | tf_op jit(solution)/shard_map/pallas_call | solution.py:193
  95.7 0.0 copy-done
  95.7 0.0 copy-done.1
  95.7 1.4 %multiply_add_fusion = f32[32,384]{1,0:T(8,128)} fusion(f32[32,384]{1,0:T(8,128)S(1)} %copy-done, f32[32,384]{1,0:T(8,128)S(1)} %copy-done.1, f32[32,384]{1,0:T(8,128)} %shard_map.106), kind=kLoop, calls=%fused_computation.8 | loop fusion | flops 24576 | bytes 196608 | tf_op jit(solution)/shard_map/add | solution.py:362
  (7 shorter events, 0.1 us)
Async XLA Ops:
  1.5 14.9 %collective-permute-start = (f32[2,32,384]{2,1,0:T(8,128)S(1)}, f32[2,32,384]{2,1,0:T(8,128)S(1)}, u32[]{:S(2)}, u32[]{:S(2)}) collective-permute-start(f32[2,32,384]{2,1,0:T(8,128)S(1)} %pad_maximum_fusion), channel_id=1, source_target_pairs={{0,7},{1,0},{2,1},{3,2},{4,3},{5,4},{6,5},{7,6},{8,15},{9,8},{10,9... | collective-permute-start | bytes 294920 | tf_op jit(solution)/shard_map/ppermute | solution.py:352
  9.4 33.3 %copy-start.3 = (f32[16,384]{1,0:T(8,128)S(1)}, f32[16,384]{1,0:T(8,128)}, u32[]{:S(2)}) copy-start(f32[16,384]{1,0:T(8,128)} %param.17) | copy-start | bytes 73732
  9.4 33.3 %copy-start.4 = (f32[16,384]{1,0:T(8,128)S(1)}, f32[16,384]{1,0:T(8,128)}, u32[]{:S(2)}) copy-start(f32[16,384]{1,0:T(8,128)} %param.15) | copy-start | bytes 73732
  9.4 33.3 %copy-start.5 = (f32[16,384]{1,0:T(8,128)S(1)}, f32[16,384]{1,0:T(8,128)}, u32[]{:S(2)}) copy-start(f32[16,384]{1,0:T(8,128)} %param.14) | copy-start | bytes 73732
  9.4 33.4 %copy-start.6 = (f32[16,128]{1,0:T(8,128)S(1)}, f32[16,128]{1,0:T(8,128)}, u32[]{:S(2)}) copy-start(f32[16,128]{1,0:T(8,128)} %param.16) | copy-start | bytes 24580
  16.3 0.6 copy-start.2
  67.5 28.2 %copy-start = (f32[32,384]{1,0:T(8,128)S(1)}, f32[32,384]{1,0:T(8,128)}, u32[]{:S(2)}) copy-start(f32[32,384]{1,0:T(8,128)} %refs_2_.3) | copy-start | bytes 147460
  67.5 28.2 %copy-start.1 = (f32[32,384]{1,0:T(8,128)S(1)}, f32[32,384]{1,0:T(8,128)}, u32[]{:S(2)}) copy-start(f32[32,384]{1,0:T(8,128)} %refs_3_.3) | copy-start | bytes 147460

commit v7 on v5

--- a/solution.py
+++ b/solution.py
@@ -78,6 +78,8 @@
     barrier = pltpu.get_barrier_semaphore()
     for dev in greet:
         pl.semaphore_signal(barrier, inc=1, device_id=dev, device_id_type=MESH)
+    later_buf[...] = scatter_rows(tb_ref, 1, push_ref, blocks)
+    own_buf[...] = scatter_rows(tb_ref, 0, push_ref, blocks)
     pl.semaphore_wait(barrier, len(greet))
 
     def remote(src, dst, send, recv, dev):
@@ -89,12 +91,10 @@
     mine = pl.ds(pl.multiple_of(core * half, half), half)
     theirs = pl.ds(pl.multiple_of((1 - core) * half, half), half)
     sent = []
-    later_buf[...] = scatter_rows(tb_ref, 1, push_ref, blocks)
     for k, (src, dev) in enumerate(((later_buf.at[mine], (c, up)), (later_buf.at[theirs], (mate, up)))):
         cp = remote(src, recv3.at[1 + k], s_sem.at[1 + k], r_sem.at[1 + k], dev)
         cp.start()
         sent.append(cp)
-    own_buf[...] = scatter_rows(tb_ref, 0, push_ref, blocks)
     cp = remote(own_buf.at[theirs], recv3.at[0], s_sem.at[0], r_sem.at[0], (mate, b))
     cp.start()
     sent.append(cp)

time: 95.5 us -> 95.3 us (level)
  no operation moved by 1% of the time
where the time goes in v7:
time: 95.3 us; the launch traced here: 94.8 us
  Pallas kernels  59.4 us (62%)
  matrix products  28.8 us (30%)
  other arithmetic  3.21 us (3%)
  local copies, waits for them, and re-layouts  1.97 us (2%)
  between operations  1.4 us (1%)
    pallas_call x3, Pallas kernels, sweep_exchange(): pl.pallas_call(functools.partial(sweep_kernel, n_contact, n_body, last),...  59.4 us
    dot_general x3, matrix products, pushes(): jnp.einsum('tkbc,tc->ktb', jacobian, lamb, preferred_element_type=jnp.flo...  18.7 us
    dot_general x2, matrix products, per_device(): jnp.einsum('tkbc,ktb->tc', jacobian, rows, preferred_element_type=jnp.flo...  10.2 us
    dot_general x3, local copies, waits for them, and re-layouts, pushes(): jnp.einsum('tkbc,tc->ktb', jacobian, lamb, preferred_element_type=jnp.flo...  1.94 us

profile of v7, /device:TPU:1, one launch (start us, length us, event | category | flops | bytes accessed | tf_op | source)
XLA Modules:
  0.0 94.8 jit_solution(7949898387973728414)
XLA Ops:
  1.3 0.8 fusion.16
  2.1 0.0 copy-start.2
  2.1 0.0 copy-start.3
  2.1 0.0 copy-start.4
  2.1 0.0 copy-start.5
  2.1 6.2 %fusion.12 = f32[16,1,2,384]{3,1,2,0:T(1,128)S(1)} fusion(bf16[16,2,384,384]{3,2,1,0:T(8,128)(2,1)} %param.9, bf16[16,384,1,1]{1,0,2,3:T(8,128)(2,1)S(1)} %fusion.16), kind=kOutput, calls=%fused_computation.20 | convolution fusion | flops 9437184 | bytes 9498624 | tf_op jit(solution)/shard_map/tkbc,tc->ktb/dot_general | solution.py:216
  8.4 0.6 copy.38
  9.0 24.7 %shard_map.104 = bf16[2,16,384]{2,1,0:T(8,128)(2,1)} custom-call(s32[2,16]{1,0:T(2,128)} %bitcast.48, f32[2,16,384]{2,1,0:T(8,128)} %bitcast.46, f32[32,384]{1,0:T(8,128)} %refs_2_.3, f32[32,384]{1,0:T(8,128)} %refs_3_.3), custom_call_target="tpu_custom_call" | custom-call | tf_op jit(solution)/shard_map/pallas_call | solution.py:193
  33.7 5.1 %fusion.2 = f32[16,1,384,1]{2,1,3,0:T(1,128)S(1)} fusion(bf16[16,2,384,384]{3,2,1,0:T(8,128)(2,1)} %param.9, bf16[2,16,384,1]{2,1,0,3:T(8,128)(2,1)} %bitcast.43), kind=kOutput, calls=%fused_computation.4 | convolution fusion | flops 9437184 | bytes 9486336 | tf_op jit(solution)/shard_map/tkbc,ktb->tc/dot_general | solution.py:221
  38.7 0.0 copy-done.2
  38.7 0.0 copy-done.3
  38.8 0.0 copy-done.4
  38.8 0.1 fusion.7
  38.8 0.0 copy-done.5
  38.9 0.1 fusion.15
  39.0 6.2 %fusion.10 = f32[16,1,2,384]{3,1,2,0:T(1,128)S(1)} fusion(bf16[16,2,384,384]{3,2,1,0:T(8,128)(2,1)} %param.9, bf16[16,384,1,1]{1,0,2,3:T(8,128)(2,1)S(1)} %fusion.15), kind=kOutput, calls=%fused_computation.18 | convolution fusion | flops 9437184 | bytes 9498624 | tf_op jit(solution)/shard_map/tkbc,tc->ktb/dot_general | solution.py:216
  45.2 0.6 copy.37
  45.8 17.5 %shard_map.105 = bf16[2,16,384]{2,1,0:T(8,128)(2,1)} custom-call(s32[2,16]{1,0:T(2,128)} %bitcast.49, f32[2,16,384]{2,1,0:T(8,128)} %bitcast.47, f32[32,384]{1,0:T(8,128)} %refs_2_.3, f32[32,384]{1,0:T(8,128)} %refs_3_.3), custom_call_target="tpu_custom_call" | custom-call | tf_op jit(solution)/shard_map/pallas_call | solution.py:193
  63.3 0.0 copy-start
  63.4 0.0 copy-start.1
  63.4 5.1 %fusion = f32[16,1,384,1]{2,1,3,0:T(1,128)S(1)} fusion(bf16[16,2,384,384]{3,2,1,0:T(8,128)(2,1)} %param.9, bf16[2,16,384,1]{2,1,0,3:T(8,128)(2,1)} %bitcast.44), kind=kOutput, calls=%fused_computation.1 | convolution fusion | flops 9437184 | bytes 9486336 | tf_op jit(solution)/shard_map/tkbc,ktb->tc/dot_general | solution.py:221
  68.5 0.1 fusion.5
  68.6 0.7 convert_bitcast_fusion
  69.3 6.2 %fusion.8 = f32[16,1,2,384]{3,1,2,0:T(1,128)S(1)} fusion(bf16[16,2,384,384]{3,2,1,0:T(8,128)(2,1)} %param.9, bf16[16,384,1,1]{1,0,2,3:T(8,128)(2,1)S(1)} %get-tuple-element.2), kind=kOutput, calls=%fused_computation.16 | convolution fusion | flops 9437184 | bytes 9498624 | tf_op jit(solution)/shard_map/tkbc,tc->ktb/dot_general | solution.py:216
  75.5 0.6 copy.36
  76.1 17.2 %shard_map.106 = f32[32,384]{1,0:T(8,128)} custom-call(s32[2,16]{1,0:T(2,128)} %bitcast.50, f32[2,16,384]{2,1,0:T(8,128)} %bitcast.45), custom_call_target="tpu_custom_call" | custom-call | tf_op jit(solution)/shard_map/pallas_call | solution.py:193
  93.3 0.0 copy-done
  93.3 0.0 copy-done.1
  93.3 1.4 %multiply_add_fusion = f32[32,384]{1,0:T(8,128)} fusion(f32[32,384]{1,0:T(8,128)S(1)} %copy-done, f32[32,384]{1,0:T(8,128)S(1)} %copy-done.1, f32[32,384]{1,0:T(8,128)} %shard_map.106), kind=kLoop, calls=%fused_computation.7 | loop fusion | flops 24576 | bytes 196608 | tf_op jit(solution)/shard_map/add | solution.py:224
  (5 shorter events, 0.1 us)
Async XLA Ops:
  2.1 36.6 %copy-start.2 = (f32[16,384]{1,0:T(8,128)S(1)}, f32[16,384]{1,0:T(8,128)}, u32[]{:S(2)}) copy-start(f32[16,384]{1,0:T(8,128)} %param.17) | copy-start | bytes 73732
  2.1 36.6 %copy-start.3 = (f32[16,384]{1,0:T(8,128)S(1)}, f32[16,384]{1,0:T(8,128)}, u32[]{:S(2)}) copy-start(f32[16,384]{1,0:T(8,128)} %param.15) | copy-start | bytes 73732
  2.1 36.6 %copy-start.4 = (f32[16,384]{1,0:T(8,128)S(1)}, f32[16,384]{1,0:T(8,128)}, u32[]{:S(2)}) copy-start(f32[16,384]{1,0:T(8,128)} %param.14) | copy-start | bytes 73732
  2.1 36.7 %copy-start.5 = (f32[16,128]{1,0:T(8,128)S(1)}, f32[16,128]{1,0:T(8,128)}, u32[]{:S(2)}) copy-start(f32[16,128]{1,0:T(8,128)} %param.16) | copy-start | bytes 24580
  63.3 30.0 %copy-start = (f32[32,384]{1,0:T(8,128)S(1)}, f32[32,384]{1,0:T(8,128)}, u32[]{:S(2)}) copy-start(f32[32,384]{1,0:T(8,128)} %refs_2_.3) | copy-start | bytes 147460
  63.4 30.0 %copy-start.1 = (f32[32,384]{1,0:T(8,128)S(1)}, f32[32,384]{1,0:T(8,128)}, u32[]{:S(2)}) copy-start(f32[32,384]{1,0:T(8,128)} %refs_3_.3) | copy-start | bytes 147460

commit v8 on v7

--- a/solution.py
+++ b/solution.py
@@ -102,10 +102,13 @@
         remote(own_buf.at[mine], recv3.at[k], s_sem.at[k], r_sem.at[k], dev).wait_recv()
     part = own_buf[mine] + recv3[0] + recv3[1] + recv3[2]
 
-    for buf, pos, peers, size, ssem, rsem in (
-        (xbuf, x, x_peers, gx, sx_sem, rx_sem),
-        (ybuf, y, y_peers, gy, sy_sem, ry_sem),
-    ):
+    rounds = [(xbuf, x, x_peers, gx, sx_sem, rx_sem), (ybuf, y, y_peers, gy, sy_sem, ry_sem)]
+    if gx == gy:
+        first = [xv * (1 - core) + yv * core for xv, yv in zip([x] + x_peers, [y] + y_peers)]
+        second = [xv * core + yv * (1 - core) for xv, yv in zip([x] + x_peers, [y] + y_peers)]
+        rounds = [(xbuf, first[0], first[1:], gx, sx_sem, rx_sem),
+                  (ybuf, second[0], second[1:], gy, sy_sem, ry_sem)]
+    for buf, pos, peers, size, ssem, rsem in rounds:
         if size == 1:
             continue
         buf[pos] = part

time: 95.3 us -> 95.3 us (level)
  no operation moved by 1% of the time
where the time goes in v8:
time: 95.3 us; the launch traced here: 94.7 us
  Pallas kernels  59.4 us (62%)
  matrix products  28.8 us (30%)
  other arithmetic  3.21 us (3%)
  local copies, waits for them, and re-layouts  1.97 us (2%)
  between operations  1.4 us (1%)
    pallas_call x3, Pallas kernels, sweep_exchange(): pl.pallas_call(functools.partial(sweep_kernel, n_contact, n_body, last),...  59.4 us
    dot_general x3, matrix products, pushes(): jnp.einsum('tkbc,tc->ktb', jacobian, lamb, preferred_element_type=jnp.flo...  18.7 us
    dot_general x2, matrix products, per_device(): jnp.einsum('tkbc,ktb->tc', jacobian, rows, preferred_element_type=jnp.flo...  10.2 us
    dot_general x3, local copies, waits for them, and re-layouts, pushes(): jnp.einsum('tkbc,tc->ktb', jacobian, lamb, preferred_element_type=jnp.flo...  1.94 us

profile of v8, /device:TPU:1, one launch (start us, length us, event | category | flops | bytes accessed | tf_op | source)
XLA Modules:
  0.0 94.7 jit_solution(17624935984589149527)
XLA Ops:
  1.3 0.8 fusion.16
  2.1 0.0 copy-start.2
  2.1 0.0 copy-start.3
  2.1 0.0 copy-start.4
  2.1 0.0 copy-start.5
  2.1 6.2 %fusion.12 = f32[16,1,2,384]{3,1,2,0:T(1,128)S(1)} fusion(bf16[16,2,384,384]{3,2,1,0:T(8,128)(2,1)} %param.9, bf16[16,384,1,1]{1,0,2,3:T(8,128)(2,1)S(1)} %fusion.16), kind=kOutput, calls=%fused_computation.20 | convolution fusion | flops 9437184 | bytes 9498624 | tf_op jit(solution)/shard_map/tkbc,tc->ktb/dot_general | solution.py:219
  8.4 0.6 copy.38
  9.0 24.7 %shard_map.104 = bf16[2,16,384]{2,1,0:T(8,128)(2,1)} custom-call(s32[2,16]{1,0:T(2,128)} %bitcast.48, f32[2,16,384]{2,1,0:T(8,128)} %bitcast.46, f32[32,384]{1,0:T(8,128)} %refs_2_.3, f32[32,384]{1,0:T(8,128)} %refs_3_.3), custom_call_target="tpu_custom_call" | custom-call | tf_op jit(solution)/shard_map/pallas_call | solution.py:196
  33.7 5.1 %fusion.2 = f32[16,1,384,1]{2,1,3,0:T(1,128)S(1)} fusion(bf16[16,2,384,384]{3,2,1,0:T(8,128)(2,1)} %param.9, bf16[2,16,384,1]{2,1,0,3:T(8,128)(2,1)} %bitcast.43), kind=kOutput, calls=%fused_computation.4 | convolution fusion | flops 9437184 | bytes 9486336 | tf_op jit(solution)/shard_map/tkbc,ktb->tc/dot_general | solution.py:224
  38.7 0.0 copy-done.2
  38.7 0.0 copy-done.3
  38.7 0.0 copy-done.4
  38.8 0.1 fusion.7
  38.8 0.0 copy-done.5
  38.9 0.1 fusion.15
  39.0 6.2 %fusion.10 = f32[16,1,2,384]{3,1,2,0:T(1,128)S(1)} fusion(bf16[16,2,384,384]{3,2,1,0:T(8,128)(2,1)} %param.9, bf16[16,384,1,1]{1,0,2,3:T(8,128)(2,1)S(1)} %fusion.15), kind=kOutput, calls=%fused_computation.18 | convolution fusion | flops 9437184 | bytes 9498624 | tf_op jit(solution)/shard_map/tkbc,tc->ktb/dot_general | solution.py:219
  45.2 0.6 copy.37
  45.8 17.5 %shard_map.105 = bf16[2,16,384]{2,1,0:T(8,128)(2,1)} custom-call(s32[2,16]{1,0:T(2,128)} %bitcast.49, f32[2,16,384]{2,1,0:T(8,128)} %bitcast.47, f32[32,384]{1,0:T(8,128)} %refs_2_.3, f32[32,384]{1,0:T(8,128)} %refs_3_.3), custom_call_target="tpu_custom_call" | custom-call | tf_op jit(solution)/shard_map/pallas_call | solution.py:196
  63.3 0.0 copy-start
  63.4 0.0 copy-start.1
  63.4 5.1 %fusion = f32[16,1,384,1]{2,1,3,0:T(1,128)S(1)} fusion(bf16[16,2,384,384]{3,2,1,0:T(8,128)(2,1)} %param.9, bf16[2,16,384,1]{2,1,0,3:T(8,128)(2,1)} %bitcast.44), kind=kOutput, calls=%fused_computation.1 | convolution fusion | flops 9437184 | bytes 9486336 | tf_op jit(solution)/shard_map/tkbc,ktb->tc/dot_general | solution.py:224
  68.5 0.1 fusion.5
  68.6 0.7 convert_bitcast_fusion
  69.3 6.2 %fusion.8 = f32[16,1,2,384]{3,1,2,0:T(1,128)S(1)} fusion(bf16[16,2,384,384]{3,2,1,0:T(8,128)(2,1)} %param.9, bf16[16,384,1,1]{1,0,2,3:T(8,128)(2,1)S(1)} %get-tuple-element.2), kind=kOutput, calls=%fused_computation.16 | convolution fusion | flops 9437184 | bytes 9498624 | tf_op jit(solution)/shard_map/tkbc,tc->ktb/dot_general | solution.py:219
  75.5 0.6 copy.36
  76.1 17.2 %shard_map.106 = f32[32,384]{1,0:T(8,128)} custom-call(s32[2,16]{1,0:T(2,128)} %bitcast.50, f32[2,16,384]{2,1,0:T(8,128)} %bitcast.45), custom_call_target="tpu_custom_call" | custom-call | tf_op jit(solution)/shard_map/pallas_call | solution.py:196
  93.3 0.0 copy-done
  93.3 0.0 copy-done.1
  93.3 1.4 %multiply_add_fusion = f32[32,384]{1,0:T(8,128)} fusion(f32[32,384]{1,0:T(8,128)S(1)} %copy-done, f32[32,384]{1,0:T(8,128)S(1)} %copy-done.1, f32[32,384]{1,0:T(8,128)} %shard_map.106), kind=kLoop, calls=%fused_computation.7 | loop fusion | flops 24576 | bytes 196608 | tf_op jit(solution)/shard_map/add | solution.py:227
  (5 shorter events, 0.1 us)
Async XLA Ops:
  2.1 36.6 %copy-start.2 = (f32[16,384]{1,0:T(8,128)S(1)}, f32[16,384]{1,0:T(8,128)}, u32[]{:S(2)}) copy-start(f32[16,384]{1,0:T(8,128)} %param.17) | copy-start | bytes 73732
  2.1 36.6 %copy-start.3 = (f32[16,384]{1,0:T(8,128)S(1)}, f32[16,384]{1,0:T(8,128)}, u32[]{:S(2)}) copy-start(f32[16,384]{1,0:T(8,128)} %param.15) | copy-start | bytes 73732
  2.1 36.6 %copy-start.4 = (f32[16,384]{1,0:T(8,128)S(1)}, f32[16,384]{1,0:T(8,128)}, u32[]{:S(2)}) copy-start(f32[16,384]{1,0:T(8,128)} %param.14) | copy-start | bytes 73732
  2.1 36.7 %copy-start.5 = (f32[16,128]{1,0:T(8,128)S(1)}, f32[16,128]{1,0:T(8,128)}, u32[]{:S(2)}) copy-start(f32[16,128]{1,0:T(8,128)} %param.16) | copy-start | bytes 24580
  63.3 30.0 %copy-start = (f32[32,384]{1,0:T(8,128)S(1)}, f32[32,384]{1,0:T(8,128)}, u32[]{:S(2)}) copy-start(f32[32,384]{1,0:T(8,128)} %refs_2_.3) | copy-start | bytes 147460
  63.4 30.0 %copy-start.1 = (f32[32,384]{1,0:T(8,128)S(1)}, f32[32,384]{1,0:T(8,128)}, u32[]{:S(2)}) copy-start(f32[32,384]{1,0:T(8,128)} %refs_3_.3) | copy-start | bytes 147460

commit v9 on v6

--- a/solution.py
+++ b/solution.py
@@ -78,6 +78,8 @@
     barrier = pltpu.get_barrier_semaphore()
     for dev in greet:
         pl.semaphore_signal(barrier, inc=1, device_id=dev, device_id_type=MESH)
+    later_buf[...] = scatter_rows(tb_ref, 1, push_ref, blocks)
+    own_buf[...] = scatter_rows(tb_ref, 0, push_ref, blocks)
     pl.semaphore_wait(barrier, len(greet))
 
     def remote(src, dst, send, recv, dev):
@@ -89,12 +91,10 @@
     mine = pl.ds(pl.multiple_of(core * half, half), half)
     theirs = pl.ds(pl.multiple_of((1 - core) * half, half), half)
     sent = []
-    later_buf[...] = scatter_rows(tb_ref, 1, push_ref, blocks)
     for k, (src, dev) in enumerate(((later_buf.at[mine], (c, up)), (later_buf.at[theirs], (mate, up)))):
         cp = remote(src, recv3.at[1 + k], s_sem.at[1 + k], r_sem.at[1 + k], dev)
         cp.start()
         sent.append(cp)
-    own_buf[...] = scatter_rows(tb_ref, 0, push_ref, blocks)
     cp = remote(own_buf.at[theirs], recv3.at[0], s_sem.at[0], r_sem.at[0], (mate, b))
     cp.start()
     sent.append(cp)
@@ -102,10 +102,13 @@
         remote(own_buf.at[mine], recv3.at[k], s_sem.at[k], r_sem.at[k], dev).wait_recv()
     part = own_buf[mine] + recv3[0] + recv3[1] + recv3[2]
 
-    for buf, pos, peers, size, ssem, rsem in (
-        (xbuf, x, x_peers, gx, sx_sem, rx_sem),
-        (ybuf, y, y_peers, gy, sy_sem, ry_sem),
-    ):
+    rounds = [(xbuf, x, x_peers, gx, sx_sem, rx_sem), (ybuf, y, y_peers, gy, sy_sem, ry_sem)]
+    if gx == gy:
+        first = [xv * (1 - core) + yv * core for xv, yv in zip([x] + x_peers, [y] + y_peers)]
+        second = [xv * core + yv * (1 - core) for xv, yv in zip([x] + x_peers, [y] + y_peers)]
+        rounds = [(xbuf, first[0], first[1:], gx, sx_sem, rx_sem),
+                  (ybuf, second[0], second[1:], gy, sy_sem, ry_sem)]
+    for buf, pos, peers, size, ssem, rsem in rounds:
         if size == 1:
             continue
         buf[pos] = part
@@ -204,9 +207,9 @@
 
 def dual_kernel(n_contact, n_body, *refs):
     gx, gy = contact_groups(n_contact)
-    (tb_ref, push_ref, vfree_ref, imass_ref, vnext_ref,
+    (tb_ref, push_ref, vfree_ref, imass_ref,
      rows_out,
-     own_buf, later_buf, recv6, xbuf, ybuf, vel_buf, velf, rows_buf,
+     own_buf, later_buf, recv6, xbuf, ybuf, vel_buf, velf, rows_buf, vn_send, vnext_ref,
      s_sem, r_sem, sx_sem, rx_sem, sy_sem, ry_sem) = refs
     blocks = own_buf.shape[0]
     width = own_buf.shape[1]
@@ -258,6 +261,11 @@
         cp = remote(src, recv6.at[3 + k], s_sem.at[3 + k], r_sem.at[3 + k], dev)
         cp.start()
         sent.append(cp)
+    vn_send[0] = vfree_ref[mine]
+    vn_send[1] = imass_ref[mine]
+    vcp = remote(vn_send, vnext_ref, s_sem.at[8], r_sem.at[8], (c, down))
+    vcp.start()
+    sent.append(vcp)
     senders = ((c, down), (mate, down), (mate, b), (c, up), (mate, up), (mate, b))
     for k, dev in enumerate(senders):
         remote(own_buf.at[mine], recv6.at[k], s_sem.at[k], r_sem.at[k], dev).wait_recv()
@@ -266,10 +274,13 @@
         later_buf[mine] + recv6[2] + recv6[3] + recv6[4],
     ], axis=0)
 
-    for buf, pos, peers, size, ssem, rsem in (
-        (xbuf, x, x_peers, gx, sx_sem, rx_sem),
-        (ybuf, y, y_peers, gy, sy_sem, ry_sem),
-    ):
+    rounds = [(xbuf, x, x_peers, gx, sx_sem, rx_sem), (ybuf, y, y_peers, gy, sy_sem, ry_sem)]
+    if gx == gy:
+        first = [xv * (1 - core) + yv * core for xv, yv in zip([x] + x_peers, [y] + y_peers)]
+        second = [xv * core + yv * (1 - core) for xv, yv in zip([x] + x_peers, [y] + y_peers)]
+        rounds = [(xbuf, first[0], first[1:], gx, sx_sem, rx_sem),
+                  (ybuf, second[0], second[1:], gy, sy_sem, ry_sem)]
+    for buf, pos, peers, size, ssem, rsem in rounds:
         if size == 1:
             continue
         buf[pos] = part
@@ -285,7 +296,8 @@
             part = part + buf[g]
 
     vel_buf[0, mine] = (vfree_ref[mine] + imass_ref[mine] * part[:half]).astype(jnp.bfloat16)
-    vel_buf[1, mine] = (vnext_ref[0, mine] + vnext_ref[1, mine] * part[half:]).astype(jnp.bfloat16)
+    remote(vn_send, vnext_ref, s_sem.at[8], r_sem.at[8], (c, up)).wait_recv()
+    vel_buf[1, mine] = (vnext_ref[0] + vnext_ref[1] * part[half:]).astype(jnp.bfloat16)
     for k in range(2):
         cp = remote(vel_buf.at[k, mine], vel_buf.at[k, mine], s_sem.at[6 + k], r_sem.at[6 + k], (mate, b))
         cp.start()
@@ -302,7 +314,7 @@
         cp.wait_send()
 
 
-def dual_exchange(tile_block, push, vel_free, inv_mass, vnext, n_contact, n_body):
+def dual_exchange(tile_block, push, vel_free, inv_mass, n_contact, n_body):
     gx, gy = contact_groups(n_contact)
     blocks, width = vel_free.shape
     tiles = push.shape[1]
@@ -318,8 +330,10 @@
         pltpu.VMEM((2, blocks, width), jnp.bfloat16),
         pltpu.VMEM((2, blocks, width), jnp.float32),
         pltpu.VMEM((2, tiles, width), jnp.float32),
-        pltpu.SemaphoreType.DMA((8,)),
-        pltpu.SemaphoreType.DMA((8,)),
+        pltpu.VMEM((2, half, width), jnp.float32),
+        pltpu.VMEM((2, half, width), jnp.float32),
+        pltpu.SemaphoreType.DMA((9,)),
+        pltpu.SemaphoreType.DMA((9,)),
         pltpu.SemaphoreType.DMA((max(gx - 1, 1),)),
         pltpu.SemaphoreType.DMA((gx,)),
         pltpu.SemaphoreType.DMA((max(gy - 1, 1),)),
@@ -328,11 +342,11 @@
     return pl.pallas_call(
         functools.partial(dual_kernel, n_contact, n_body),
         out_shape=jax.ShapeDtypeStruct((2, tiles, width), jnp.bfloat16),
-        in_specs=[sspec] + [vspec] * 4,
+        in_specs=[sspec] + [vspec] * 3,
         out_specs=vspec,
         scratch_shapes=scratch,
         compiler_params=pltpu.CompilerParams(collective_id=2, has_side_effects=True),
-    )(tile_block, push, vel_free, inv_mass, vnext)
+    )(tile_block, push, vel_free, inv_mass)
 
 
 def per_device(
@@ -348,14 +362,9 @@
         lamb = lam.astype(jnp.bfloat16)
         return jnp.einsum("tkbc,tc->ktb", jacobian, lamb, preferred_element_type=jnp.float32)
 
-    count = lax.axis_size("body")
-    vnext = lax.ppermute(
-        jnp.stack([vel_free, inv_mass]), "body",
-        [(source, (source + count - 1) % count) for source in range(count)],
-    )
     lam = impulse_start * mask
     for sweep in range(ITERS):
-        rows = dual_exchange(tile_block.T, pushes(lam), vel_free, inv_mass, vnext, n_contact, n_body)
+        rows = dual_exchange(tile_block.T, pushes(lam), vel_free, inv_mass, n_contact, n_body)
         rel = jnp.einsum("tkbc,ktb->tc", jacobian, rows, preferred_element_type=jnp.float32) + bias
         lam = project(lam - step_scale * rel, friction, contacts) * mask
     total = sweep_exchange(tile_block.T, pushes(lam), vel_free, inv_mass, n_contact, n_body, True)

time: 97.7 us -> 93 us (0.952)
  starting transfers between devices: 6.47 us -> 0 us
  Pallas kernels: 53.8 us -> 57 us
    ppermute x1 -> x0, starting transfers between devices: 6.47 us -> none  [per_device(): lax.ppermute(jnp.stack([vel_free, inv_mass]), 'body', [(source, (source +...]
    pallas_call x2, Pallas kernels: 38.4 us -> 41.4 us  [dual_exchange(): pl.pallas_call(functools.partial(dual_kernel, n_contact, n_body), out_sha...]
  transfers between devices with their start and end apart: 1 -> 0, of which waited for: 0 -> 0; matrix products, arithmetic and copies ran while one was open for 8% -> 0% of each run, Pallas kernels for 0% -> 0%
where the time goes in v9:
time: 93 us; the launch traced here: 92.4 us
  Pallas kernels  57 us (61%)
  matrix products  28.8 us (31%)
  other arithmetic  3.21 us (3%)
  local copies, waits for them, and re-layouts  1.97 us (2%)
  between operations  1.4 us (2%)
    pallas_call x2, Pallas kernels, dual_exchange(): pl.pallas_call(functools.partial(dual_kernel, n_contact, n_body), out_sha...  41.4 us
    dot_general x3, matrix products, pushes(): jnp.einsum('tkbc,tc->ktb', jacobian, lamb, preferred_element_type=jnp.flo...  18.7 us
    pallas_call x1, Pallas kernels, sweep_exchange(): pl.pallas_call(functools.partial(sweep_kernel, n_contact, n_body, last),...  15.6 us
    dot_general x2, matrix products, per_device(): jnp.einsum('tkbc,ktb->tc', jacobian, rows, preferred_element_type=jnp.flo...  10.2 us
    dot_general x3, local copies, waits for them, and re-layouts, pushes(): jnp.einsum('tkbc,tc->ktb', jacobian, lamb, preferred_element_type=jnp.flo...  1.94 us

profile of v9, /device:TPU:1, one launch (start us, length us, event | category | flops | bytes accessed | tf_op | source)
XLA Modules:
  0.0 92.4 jit_solution(9525786248972425363)
XLA Ops:
  1.3 0.8 fusion.16
  2.1 0.0 copy-start.2
  2.1 0.0 copy-start.3
  2.1 0.0 copy-start.4
  2.1 0.0 copy-start.5
  2.1 6.2 %fusion.12 = f32[16,1,2,384]{3,1,2,0:T(1,128)S(1)} fusion(bf16[16,2,384,384]{3,2,1,0:T(8,128)(2,1)} %param.9, bf16[16,384,1,1]{1,0,2,3:T(8,128)(2,1)S(1)} %fusion.16), kind=kOutput, calls=%fused_computation.20 | convolution fusion | flops 9437184 | bytes 9498624 | tf_op jit(solution)/shard_map/tkbc,tc->ktb/dot_general | solution.py:363
  8.4 0.6 copy.38
  9.0 24.6 %shard_map.104 = bf16[2,16,384]{2,1,0:T(8,128)(2,1)} custom-call(s32[2,16]{1,0:T(2,128)} %bitcast.48, f32[2,16,384]{2,1,0:T(8,128)} %bitcast.46, f32[32,384]{1,0:T(8,128)} %refs_2_.3, f32[32,384]{1,0:T(8,128)} %refs_3_.3), custom_call_target="tpu_custom_call" | custom-call | tf_op jit(solution)/shard_map/pallas_call | solution.py:342
  33.6 5.1 %fusion.2 = f32[16,1,384,1]{2,1,3,0:T(1,128)S(1)} fusion(bf16[16,2,384,384]{3,2,1,0:T(8,128)(2,1)} %param.9, bf16[2,16,384,1]{2,1,0,3:T(8,128)(2,1)} %bitcast.43), kind=kOutput, calls=%fused_computation.4 | convolution fusion | flops 9437184 | bytes 9486336 | tf_op jit(solution)/shard_map/tkbc,ktb->tc/dot_general | solution.py:368
  38.7 0.0 copy-done.2
  38.7 0.0 copy-done.3
  38.7 0.0 copy-done.4
  38.7 0.1 fusion.7
  38.8 0.0 copy-done.5
  38.8 0.1 fusion.15
  38.9 6.2 %fusion.10 = f32[16,1,2,384]{3,1,2,0:T(1,128)S(1)} fusion(bf16[16,2,384,384]{3,2,1,0:T(8,128)(2,1)} %param.9, bf16[16,384,1,1]{1,0,2,3:T(8,128)(2,1)S(1)} %fusion.15), kind=kOutput, calls=%fused_computation.18 | convolution fusion | flops 9437184 | bytes 9498624 | tf_op jit(solution)/shard_map/tkbc,tc->ktb/dot_general | solution.py:363
  45.1 0.6 copy.37
  45.8 16.8 %shard_map.105 = bf16[2,16,384]{2,1,0:T(8,128)(2,1)} custom-call(s32[2,16]{1,0:T(2,128)} %bitcast.49, f32[2,16,384]{2,1,0:T(8,128)} %bitcast.47, f32[32,384]{1,0:T(8,128)} %refs_2_.3, f32[32,384]{1,0:T(8,128)} %refs_3_.3), custom_call_target="tpu_custom_call" | custom-call | tf_op jit(solution)/shard_map/pallas_call | solution.py:342
  62.6 0.0 copy-start
  62.6 0.0 copy-start.1
  62.6 5.1 %fusion = f32[16,1,384,1]{2,1,3,0:T(1,128)S(1)} fusion(bf16[16,2,384,384]{3,2,1,0:T(8,128)(2,1)} %param.9, bf16[2,16,384,1]{2,1,0,3:T(8,128)(2,1)} %bitcast.44), kind=kOutput, calls=%fused_computation.1 | convolution fusion | flops 9437184 | bytes 9486336 | tf_op jit(solution)/shard_map/tkbc,ktb->tc/dot_general | solution.py:368
  67.7 0.1 fusion.5
  67.8 0.7 convert_bitcast_fusion
  68.5 6.2 %fusion.8 = f32[16,1,2,384]{3,1,2,0:T(1,128)S(1)} fusion(bf16[16,2,384,384]{3,2,1,0:T(8,128)(2,1)} %param.9, bf16[16,384,1,1]{1,0,2,3:T(8,128)(2,1)S(1)} %get-tuple-element.2), kind=kOutput, calls=%fused_computation.16 | convolution fusion | flops 9437184 | bytes 9498624 | tf_op jit(solution)/shard_map/tkbc,tc->ktb/dot_general | solution.py:363
  74.7 0.6 copy.36
  75.3 15.6 %shard_map.106 = f32[32,384]{1,0:T(8,128)} custom-call(s32[2,16]{1,0:T(2,128)} %bitcast.50, f32[2,16,384]{2,1,0:T(8,128)} %bitcast.45), custom_call_target="tpu_custom_call" | custom-call | tf_op jit(solution)/shard_map/pallas_call | solution.py:196
  91.0 0.0 copy-done
  91.0 0.0 copy-done.1
  91.0 1.4 %multiply_add_fusion = f32[32,384]{1,0:T(8,128)} fusion(f32[32,384]{1,0:T(8,128)S(1)} %copy-done, f32[32,384]{1,0:T(8,128)S(1)} %copy-done.1, f32[32,384]{1,0:T(8,128)} %shard_map.106), kind=kLoop, calls=%fused_computation.7 | loop fusion | flops 24576 | bytes 196608 | tf_op jit(solution)/shard_map/add | solution.py:371
  (5 shorter events, 0.1 us)
Async XLA Ops:
  2.1 36.6 %copy-start.2 = (f32[16,384]{1,0:T(8,128)S(1)}, f32[16,384]{1,0:T(8,128)}, u32[]{:S(2)}) copy-start(f32[16,384]{1,0:T(8,128)} %param.17) | copy-start | bytes 73732
  2.1 36.6 %copy-start.3 = (f32[16,384]{1,0:T(8,128)S(1)}, f32[16,384]{1,0:T(8,128)}, u32[]{:S(2)}) copy-start(f32[16,384]{1,0:T(8,128)} %param.15) | copy-start | bytes 73732
  2.1 36.6 %copy-start.4 = (f32[16,384]{1,0:T(8,128)S(1)}, f32[16,384]{1,0:T(8,128)}, u32[]{:S(2)}) copy-start(f32[16,384]{1,0:T(8,128)} %param.14) | copy-start | bytes 73732
  2.1 36.7 %copy-start.5 = (f32[16,128]{1,0:T(8,128)S(1)}, f32[16,128]{1,0:T(8,128)}, u32[]{:S(2)}) copy-start(f32[16,128]{1,0:T(8,128)} %param.16) | copy-start | bytes 24580
  62.6 28.4 %copy-start = (f32[32,384]{1,0:T(8,128)S(1)}, f32[32,384]{1,0:T(8,128)}, u32[]{:S(2)}) copy-start(f32[32,384]{1,0:T(8,128)} %refs_2_.3) | copy-start | bytes 147460
  62.6 28.4 %copy-start.1 = (f32[32,384]{1,0:T(8,128)S(1)}, f32[32,384]{1,0:T(8,128)}, u32[]{:S(2)}) copy-start(f32[32,384]{1,0:T(8,128)} %refs_3_.3) | copy-start | bytes 147460

commit v10 on v9

--- a/solution.py
+++ b/solution.py
@@ -36,12 +36,12 @@
 
 
 def scatter_rows(tb_ref, column, push_ref, blocks):
-    tiles = push_ref.shape[1]
+    tiles = push_ref.shape[0]
     width = push_ref.shape[2]
     slot = lax.broadcasted_iota(jnp.int32, (blocks, width), 0)
     acc = None
     for t in range(tiles):
-        row = push_ref[column, t : t + 1, :]
+        row = push_ref[t, column : column + 1, :]
         term = jnp.where(slot == tb_ref[column, t], row, 0.0)
         acc = term if acc is None else acc + term
     return acc
@@ -162,7 +162,7 @@
 def sweep_exchange(tile_block, push, vel_free, inv_mass, n_contact, n_body, last):
     gx, gy = contact_groups(n_contact)
     blocks, width = vel_free.shape
-    tiles = push.shape[1]
+    tiles = push.shape[0]
     half = blocks // 2
     vspec = pl.BlockSpec(memory_space=pltpu.VMEM)
     sspec = pl.BlockSpec(memory_space=pltpu.SMEM)
@@ -317,7 +317,7 @@
 def dual_exchange(tile_block, push, vel_free, inv_mass, n_contact, n_body):
     gx, gy = contact_groups(n_contact)
     blocks, width = vel_free.shape
-    tiles = push.shape[1]
+    tiles = push.shape[0]
     half = blocks // 2
     vspec = pl.BlockSpec(memory_space=pltpu.VMEM)
     sspec = pl.BlockSpec(memory_space=pltpu.SMEM)
@@ -360,7 +360,8 @@
 
     def pushes(lam):
         lamb = lam.astype(jnp.bfloat16)
-        return jnp.einsum("tkbc,tc->ktb", jacobian, lamb, preferred_element_type=jnp.float32)
+        product = jacobian.astype(jnp.float32) * lamb.astype(jnp.float32)[:, None, None, :]
+        return jnp.sum(product, axis=-1)
 
     lam = impulse_start * mask
     for sweep in range(ITERS):

time: 93 us -> 91.3 us (0.982)
  other arithmetic: 3.21 us -> 22.1 us
  matrix products: 28.8 us -> 10.2 us
  local copies, waits for them, and re-layouts: 1.97 us -> 0.03 us
    reduce_sum x0 -> x3, other arithmetic: none -> 18.9 us  [pushes(): return jnp.sum(product, axis=-1)]
    dot_general x3 -> x0, matrix products: 18.7 us -> none  [pushes(): jnp.einsum('tkbc,tc->ktb', jacobian, lamb, preferred_element_type=jnp.flo...]
    dot_general x3 -> x0, local copies, waits for them, and re-layouts: 1.94 us -> none  [pushes(): jnp.einsum('tkbc,tc->ktb', jacobian, lamb, preferred_element_type=jnp.flo...]
where the time goes in v10:
time: 91.3 us; the launch traced here: 90.8 us
  Pallas kernels  57.1 us (63%)
  other arithmetic  22.1 us (24%)
  matrix products  10.2 us (11%)
  between operations  1.4 us (2%)
    pallas_call x2, Pallas kernels, dual_exchange(): pl.pallas_call(functools.partial(dual_kernel, n_contact, n_body), out_sha...  41.4 us
    reduce_sum x3, other arithmetic, pushes(): return jnp.sum(product, axis=-1)  18.9 us
    pallas_call x1, Pallas kernels, sweep_exchange(): pl.pallas_call(functools.partial(sweep_kernel, n_contact, n_body, last),...  15.7 us
    dot_general x2, matrix products, per_device(): jnp.einsum('tkbc,ktb->tc', jacobian, rows, preferred_element_type=jnp.flo...  10.2 us

profile of v10, /device:TPU:1, one launch (start us, length us, event | category | flops | bytes accessed | tf_op | source)
XLA Modules:
  0.0 90.8 jit_solution(620970950153456546)
XLA Ops:
  1.3 0.8 fusion.13
  2.1 0.0 copy-start.2
  2.1 0.0 copy-start.3
  2.1 0.0 copy-start.4
  2.1 0.0 copy-start.5
  2.1 6.3 %fusion.refs_1_ = f32[16,2,384]{2,1,0:T(2,128)} fusion(bf16[16,2,384,384]{3,2,1,0:T(8,128)(2,1)} %param.9, f32[16,384]{1,0:T(8,128)S(1)} %fusion.13), kind=kLoop, calls=%fused_computation.3 | loop fusion | flops 14143488 | bytes 9510912 | tf_op jit(solution)/shard_map/reduce_sum | solution.py:364
  8.4 24.6 %shard_map.104 = bf16[2,16,384]{2,1,0:T(8,128)(2,1)} custom-call(s32[2,16]{1,0:T(2,128)} %bitcast.21, f32[16,2,384]{2,1,0:T(2,128)} %fusion.refs_1_, f32[32,384]{1,0:T(8,128)} %refs_2_.3, f32[32,384]{1,0:T(8,128)} %refs_3_.3), custom_call_target="tpu_custom_call" | custom-call | tf_op jit(solution)/shard_map/pallas_call | solution.py:342
  33.1 5.1 %fusion.5 = f32[16,1,384,1]{2,1,3,0:T(1,128)S(1)} fusion(bf16[16,2,384,384]{3,2,1,0:T(8,128)(2,1)} %param.9, bf16[2,16,384,1]{2,1,0,3:T(8,128)(2,1)} %bitcast.19), kind=kOutput, calls=%fused_computation.8 | convolution fusion | flops 9437184 | bytes 9486336 | tf_op jit(solution)/shard_map/tkbc,ktb->tc/dot_general | solution.py:369
  38.1 0.0 copy-done.2
  38.1 0.0 copy-done.3
  38.1 0.0 copy-done.4
  38.1 0.1 fusion.10
  38.2 0.0 copy-done.5
  38.3 0.1 fusion.12
  38.3 6.3 %fusion.1.refs_1_ = f32[16,2,384]{2,1,0:T(2,128)} fusion(bf16[16,2,384,384]{3,2,1,0:T(8,128)(2,1)} %param.9, f32[16,384]{1,0:T(8,128)S(1)} %fusion.12), kind=kLoop, calls=%fused_computation.4 | loop fusion | flops 14143488 | bytes 9510912 | tf_op jit(solution)/shard_map/reduce_sum | solution.py:364
  44.6 16.8 %shard_map.105 = bf16[2,16,384]{2,1,0:T(8,128)(2,1)} custom-call(s32[2,16]{1,0:T(2,128)} %bitcast.22, f32[16,2,384]{2,1,0:T(2,128)} %fusion.1.refs_1_, f32[32,384]{1,0:T(8,128)} %refs_2_.3, f32[32,384]{1,0:T(8,128)} %refs_3_.3), custom_call_target="tpu_custom_call" | custom-call | tf_op jit(solution)/shard_map/pallas_call | solution.py:342
  61.4 0.0 copy-start
  61.4 0.0 copy-start.1
  61.5 5.1 %fusion.3 = f32[16,1,384,1]{2,1,3,0:T(1,128)S(1)} fusion(bf16[16,2,384,384]{3,2,1,0:T(8,128)(2,1)} %param.9, bf16[2,16,384,1]{2,1,0,3:T(8,128)(2,1)} %bitcast.20), kind=kOutput, calls=%fused_computation.6 | convolution fusion | flops 9437184 | bytes 9486336 | tf_op jit(solution)/shard_map/tkbc,ktb->tc/dot_general | solution.py:369
  66.5 0.1 fusion.8
  66.7 0.7 convert_convert_fusion
  67.4 6.3 %fusion.2.refs_1_ = f32[16,2,384]{2,1,0:T(2,128)} fusion(bf16[16,2,384,384]{3,2,1,0:T(8,128)(2,1)} %param.9, f32[16,384]{1,0:T(8,128)S(1)} %get-tuple-element.2), kind=kLoop, calls=%fused_computation.5 | loop fusion | flops 14143488 | bytes 9510912 | tf_op jit(solution)/shard_map/reduce_sum | solution.py:364
  73.6 15.7 %shard_map.106 = f32[32,384]{1,0:T(8,128)} custom-call(s32[2,16]{1,0:T(2,128)} %bitcast.23, f32[16,2,384]{2,1,0:T(2,128)} %fusion.2.refs_1_), custom_call_target="tpu_custom_call" | custom-call | tf_op jit(solution)/shard_map/pallas_call | solution.py:196
  89.3 0.0 copy-done
  89.3 0.0 copy-done.1
  89.3 1.4 %multiply_add_fusion = f32[32,384]{1,0:T(8,128)} fusion(f32[32,384]{1,0:T(8,128)S(1)} %copy-done, f32[32,384]{1,0:T(8,128)S(1)} %copy-done.1, f32[32,384]{1,0:T(8,128)} %shard_map.106), kind=kLoop, calls=%fused_computation.10 | loop fusion | flops 24576 | bytes 196608 | tf_op jit(solution)/shard_map/add | solution.py:372
  (5 shorter events, 0.1 us)
Async XLA Ops:
  2.1 36.0 %copy-start.2 = (f32[16,384]{1,0:T(8,128)S(1)}, f32[16,384]{1,0:T(8,128)}, u32[]{:S(2)}) copy-start(f32[16,384]{1,0:T(8,128)} %param.17) | copy-start | bytes 73732
  2.1 36.0 %copy-start.3 = (f32[16,384]{1,0:T(8,128)S(1)}, f32[16,384]{1,0:T(8,128)}, u32[]{:S(2)}) copy-start(f32[16,384]{1,0:T(8,128)} %param.15) | copy-start | bytes 73732
  2.1 36.0 %copy-start.4 = (f32[16,384]{1,0:T(8,128)S(1)}, f32[16,384]{1,0:T(8,128)}, u32[]{:S(2)}) copy-start(f32[16,384]{1,0:T(8,128)} %param.14) | copy-start | bytes 73732
  2.1 36.1 %copy-start.5 = (f32[16,128]{1,0:T(8,128)S(1)}, f32[16,128]{1,0:T(8,128)}, u32[]{:S(2)}) copy-start(f32[16,128]{1,0:T(8,128)} %param.16) | copy-start | bytes 24580
  61.4 27.9 %copy-start = (f32[32,384]{1,0:T(8,128)S(1)}, f32[32,384]{1,0:T(8,128)}, u32[]{:S(2)}) copy-start(f32[32,384]{1,0:T(8,128)} %refs_2_.3) | copy-start | bytes 147460
  61.4 27.9 %copy-start.1 = (f32[32,384]{1,0:T(8,128)S(1)}, f32[32,384]{1,0:T(8,128)}, u32[]{:S(2)}) copy-start(f32[32,384]{1,0:T(8,128)} %refs_3_.3) | copy-start | bytes 147460

commit v11 on v9

--- a/solution.py
+++ b/solution.py
@@ -227,9 +227,15 @@
 
     greet = [(mate, b), (c, up), (mate, up), (c, down), (mate, down)]
     greet += [(p, b) for p in x_peers] + [(p, b) for p in y_peers]
+    mine = pl.ds(pl.multiple_of(core * half, half), half)
+    theirs = pl.ds(pl.multiple_of((1 - core) * half, half), half)
     barrier = pltpu.get_barrier_semaphore()
     for dev in greet:
         pl.semaphore_signal(barrier, inc=1, device_id=dev, device_id_type=MESH)
+    later_buf[...] = scatter_rows(tb_ref, 1, push_ref, blocks)
+    own_buf[...] = scatter_rows(tb_ref, 0, push_ref, blocks)
+    vn_send[0] = vfree_ref[mine]
+    vn_send[1] = imass_ref[mine]
     pl.semaphore_wait(barrier, len(greet))
 
     def remote(src, dst, send, recv, dev):
@@ -238,10 +244,7 @@
             device_id=dev, device_id_type=MESH,
         )
 
-    mine = pl.ds(pl.multiple_of(core * half, half), half)
-    theirs = pl.ds(pl.multiple_of((1 - core) * half, half), half)
     sent = []
-    later_buf[...] = scatter_rows(tb_ref, 1, push_ref, blocks)
     plan = (
         (later_buf.at[mine], (c, up)),
         (later_buf.at[theirs], (mate, up)),
@@ -251,7 +254,6 @@
         cp = remote(src, recv6.at[k], s_sem.at[k], r_sem.at[k], dev)
         cp.start()
         sent.append(cp)
-    own_buf[...] = scatter_rows(tb_ref, 0, push_ref, blocks)
     plan = (
         (own_buf.at[mine], (c, down)),
         (own_buf.at[theirs], (mate, down)),
@@ -261,8 +263,6 @@
         cp = remote(src, recv6.at[3 + k], s_sem.at[3 + k], r_sem.at[3 + k], dev)
         cp.start()
         sent.append(cp)
-    vn_send[0] = vfree_ref[mine]
-    vn_send[1] = imass_ref[mine]
     vcp = remote(vn_send, vnext_ref, s_sem.at[8], r_sem.at[8], (c, down))
     vcp.start()
     sent.append(vcp)

time: 93 us -> 92.7 us (level)
  no operation moved by 1% of the time
where the time goes in v11:
time: 92.7 us; the launch traced here: 92.2 us
  Pallas kernels  56.8 us (61%)
  matrix products  28.8 us (31%)
  other arithmetic  3.21 us (3%)
  local copies, waits for them, and re-layouts  1.97 us (2%)
  between operations  1.4 us (2%)
    pallas_call x2, Pallas kernels, dual_exchange(): pl.pallas_call(functools.partial(dual_kernel, n_contact, n_body), out_sha...  41.1 us
    dot_general x3, matrix products, pushes(): jnp.einsum('tkbc,tc->ktb', jacobian, lamb, preferred_element_type=jnp.flo...  18.7 us
    pallas_call x1, Pallas kernels, sweep_exchange(): pl.pallas_call(functools.partial(sweep_kernel, n_contact, n_body, last),...  15.7 us
    dot_general x2, matrix products, per_device(): jnp.einsum('tkbc,ktb->tc', jacobian, rows, preferred_element_type=jnp.flo...  10.2 us
    dot_general x3, local copies, waits for them, and re-layouts, pushes(): jnp.einsum('tkbc,tc->ktb', jacobian, lamb, preferred_element_type=jnp.flo...  1.94 us

profile of v11, /device:TPU:1, one launch (start us, length us, event | category | flops | bytes accessed | tf_op | source)
XLA Modules:
  0.0 92.2 jit_solution(4284121128896977555)
XLA Ops:
  1.3 0.8 fusion.16
  2.1 0.0 copy-start.2
  2.1 0.0 copy-start.3
  2.1 0.0 copy-start.4
  2.1 0.0 copy-start.5
  2.1 6.2 %fusion.12 = f32[16,1,2,384]{3,1,2,0:T(1,128)S(1)} fusion(bf16[16,2,384,384]{3,2,1,0:T(8,128)(2,1)} %param.9, bf16[16,384,1,1]{1,0,2,3:T(8,128)(2,1)S(1)} %fusion.16), kind=kOutput, calls=%fused_computation.20 | convolution fusion | flops 9437184 | bytes 9498624 | tf_op jit(solution)/shard_map/tkbc,tc->ktb/dot_general | solution.py:363
  8.4 0.6 copy.38
  9.0 24.5 %shard_map.104 = bf16[2,16,384]{2,1,0:T(8,128)(2,1)} custom-call(s32[2,16]{1,0:T(2,128)} %bitcast.48, f32[2,16,384]{2,1,0:T(8,128)} %bitcast.46, f32[32,384]{1,0:T(8,128)} %refs_2_.3, f32[32,384]{1,0:T(8,128)} %refs_3_.3), custom_call_target="tpu_custom_call" | custom-call | tf_op jit(solution)/shard_map/pallas_call | solution.py:342
  33.5 5.1 %fusion.2 = f32[16,1,384,1]{2,1,3,0:T(1,128)S(1)} fusion(bf16[16,2,384,384]{3,2,1,0:T(8,128)(2,1)} %param.9, bf16[2,16,384,1]{2,1,0,3:T(8,128)(2,1)} %bitcast.43), kind=kOutput, calls=%fused_computation.4 | convolution fusion | flops 9437184 | bytes 9486336 | tf_op jit(solution)/shard_map/tkbc,ktb->tc/dot_general | solution.py:368
  38.6 0.0 copy-done.2
  38.6 0.0 copy-done.3
  38.6 0.0 copy-done.4
  38.6 0.1 fusion.7
  38.7 0.0 copy-done.5
  38.8 0.1 fusion.15
  38.8 6.2 %fusion.10 = f32[16,1,2,384]{3,1,2,0:T(1,128)S(1)} fusion(bf16[16,2,384,384]{3,2,1,0:T(8,128)(2,1)} %param.9, bf16[16,384,1,1]{1,0,2,3:T(8,128)(2,1)S(1)} %fusion.15), kind=kOutput, calls=%fused_computation.18 | convolution fusion | flops 9437184 | bytes 9498624 | tf_op jit(solution)/shard_map/tkbc,tc->ktb/dot_general | solution.py:363
  45.0 0.6 copy.37
  45.7 16.6 %shard_map.105 = bf16[2,16,384]{2,1,0:T(8,128)(2,1)} custom-call(s32[2,16]{1,0:T(2,128)} %bitcast.49, f32[2,16,384]{2,1,0:T(8,128)} %bitcast.47, f32[32,384]{1,0:T(8,128)} %refs_2_.3, f32[32,384]{1,0:T(8,128)} %refs_3_.3), custom_call_target="tpu_custom_call" | custom-call | tf_op jit(solution)/shard_map/pallas_call | solution.py:342
  62.3 0.0 copy-start
  62.3 0.0 copy-start.1
  62.3 5.1 %fusion = f32[16,1,384,1]{2,1,3,0:T(1,128)S(1)} fusion(bf16[16,2,384,384]{3,2,1,0:T(8,128)(2,1)} %param.9, bf16[2,16,384,1]{2,1,0,3:T(8,128)(2,1)} %bitcast.44), kind=kOutput, calls=%fused_computation.1 | convolution fusion | flops 9437184 | bytes 9486336 | tf_op jit(solution)/shard_map/tkbc,ktb->tc/dot_general | solution.py:368
  67.4 0.1 fusion.5
  67.5 0.7 convert_bitcast_fusion
  68.2 6.2 %fusion.8 = f32[16,1,2,384]{3,1,2,0:T(1,128)S(1)} fusion(bf16[16,2,384,384]{3,2,1,0:T(8,128)(2,1)} %param.9, bf16[16,384,1,1]{1,0,2,3:T(8,128)(2,1)S(1)} %get-tuple-element.2), kind=kOutput, calls=%fused_computation.16 | convolution fusion | flops 9437184 | bytes 9498624 | tf_op jit(solution)/shard_map/tkbc,tc->ktb/dot_general | solution.py:363
  74.4 0.6 copy.36
  75.1 15.7 %shard_map.106 = f32[32,384]{1,0:T(8,128)} custom-call(s32[2,16]{1,0:T(2,128)} %bitcast.50, f32[2,16,384]{2,1,0:T(8,128)} %bitcast.45), custom_call_target="tpu_custom_call" | custom-call | tf_op jit(solution)/shard_map/pallas_call | solution.py:196
  90.7 0.0 copy-done
  90.7 0.0 copy-done.1
  90.7 1.4 %multiply_add_fusion = f32[32,384]{1,0:T(8,128)} fusion(f32[32,384]{1,0:T(8,128)S(1)} %copy-done, f32[32,384]{1,0:T(8,128)S(1)} %copy-done.1, f32[32,384]{1,0:T(8,128)} %shard_map.106), kind=kLoop, calls=%fused_computation.7 | loop fusion | flops 24576 | bytes 196608 | tf_op jit(solution)/shard_map/add | solution.py:371
  (5 shorter events, 0.1 us)
Async XLA Ops:
  2.1 36.5 %copy-start.2 = (f32[16,384]{1,0:T(8,128)S(1)}, f32[16,384]{1,0:T(8,128)}, u32[]{:S(2)}) copy-start(f32[16,384]{1,0:T(8,128)} %param.17) | copy-start | bytes 73732
  2.1 36.5 %copy-start.3 = (f32[16,384]{1,0:T(8,128)S(1)}, f32[16,384]{1,0:T(8,128)}, u32[]{:S(2)}) copy-start(f32[16,384]{1,0:T(8,128)} %param.15) | copy-start | bytes 73732
  2.1 36.5 %copy-start.4 = (f32[16,384]{1,0:T(8,128)S(1)}, f32[16,384]{1,0:T(8,128)}, u32[]{:S(2)}) copy-start(f32[16,384]{1,0:T(8,128)} %param.14) | copy-start | bytes 73732
  2.1 36.6 %copy-start.5 = (f32[16,128]{1,0:T(8,128)S(1)}, f32[16,128]{1,0:T(8,128)}, u32[]{:S(2)}) copy-start(f32[16,128]{1,0:T(8,128)} %param.16) | copy-start | bytes 24580
  62.3 28.4 %copy-start = (f32[32,384]{1,0:T(8,128)S(1)}, f32[32,384]{1,0:T(8,128)}, u32[]{:S(2)}) copy-start(f32[32,384]{1,0:T(8,128)} %refs_2_.3) | copy-start | bytes 147460
  62.3 28.4 %copy-start.1 = (f32[32,384]{1,0:T(8,128)S(1)}, f32[32,384]{1,0:T(8,128)}, u32[]{:S(2)}) copy-start(f32[32,384]{1,0:T(8,128)} %refs_3_.3) | copy-start | bytes 147460

commit v12 on v11

--- a/solution.py
+++ b/solution.py
@@ -349,6 +349,131 @@
     )(tile_block, push, vel_free, inv_mass)
 
 
+def final_kernel(n_contact, n_body, *refs):
+    gx, gy = contact_groups(n_contact)
+    (tb_ref, push_ref,
+     tot_out,
+     own_buf, later_buf, recv2, fbuf, lsend, sbuf, tot_buf,
+     s_sem, r_sem, fs_sem, fr_sem, ss_sem, sr_sem) = refs
+    blocks = own_buf.shape[0]
+    half = blocks // 2
+    c = lax.axis_index("contact")
+    b = lax.axis_index("body")
+    core = lax.rem(c, 2)
+    x = lax.rem(c // 2, gx)
+    y = c // (2 * gx)
+    mate = c + 1 - 2 * core
+    up = lax.rem(b + 1, n_body)
+    down = lax.rem(b + n_body - 1, n_body)
+    x_peers = [(y * gx + lax.rem(x + j, gx)) * 2 + core for j in range(1, gx)]
+    y_peers = [(lax.rem(y + j, gy) * gx + x) * 2 + core for j in range(1, gy)]
+    pos1, peers1, size1, pos2, peers2, size2 = x, x_peers, gx, y, y_peers, gy
+    if gx == gy:
+        first = [xv * (1 - core) + yv * core for xv, yv in zip([x] + x_peers, [y] + y_peers)]
+        second = [xv * core + yv * (1 - core) for xv, yv in zip([x] + x_peers, [y] + y_peers)]
+        pos1, peers1, pos2, peers2 = first[0], first[1:], second[0], second[1:]
+
+    greet = [(mate, b), (c, up), (c, down)]
+    greet += [(p, b) for p in peers1] + [(p, up) for p in peers1] + [(p, down) for p in peers1]
+    greet += [(p, b) for p in peers2]
+    barrier = pltpu.get_barrier_semaphore()
+    for dev in greet:
+        pl.semaphore_signal(barrier, inc=1, device_id=dev, device_id_type=MESH)
+    later_buf[...] = scatter_rows(tb_ref, 1, push_ref, blocks)
+    own_buf[...] = scatter_rows(tb_ref, 0, push_ref, blocks)
+    pl.semaphore_wait(barrier, len(greet))
+
+    def remote(src, dst, send, recv, dev):
+        return pltpu.make_async_remote_copy(
+            src_ref=src, dst_ref=dst, send_sem=send, recv_sem=recv,
+            device_id=dev, device_id_type=MESH,
+        )
+
+    mine = pl.ds(pl.multiple_of(core * half, half), half)
+    theirs = pl.ds(pl.multiple_of((1 - core) * half, half), half)
+    sent = []
+    for k, src in enumerate((own_buf.at[theirs], later_buf.at[theirs])):
+        cp = remote(src, recv2.at[k], s_sem.at[k], r_sem.at[k], (mate, b))
+        cp.start()
+        sent.append(cp)
+    for k in range(2):
+        remote(own_buf.at[mine], recv2.at[k], s_sem.at[k], r_sem.at[k], (mate, b)).wait_recv()
+    fbuf[pos1] = own_buf[mine] + recv2[0]
+    lsend[...] = later_buf[mine] + recv2[1]
+
+    for j, p in enumerate(peers1):
+        cp = remote(fbuf.at[pos1], fbuf.at[pos1], fs_sem.at[j], fr_sem.at[pos1], (p, b))
+        cp.start()
+        sent.append(cp)
+    for j, p in enumerate([c] + peers1):
+        cp = remote(lsend, fbuf.at[size1 + pos1], fs_sem.at[size1 - 1 + j],
+                    fr_sem.at[size1 + pos1], (p, up))
+        cp.start()
+        sent.append(cp)
+    for j in range(1, size1):
+        q = lax.rem(pos1 + j, size1)
+        remote(lsend, fbuf.at[q], fs_sem.at[0], fr_sem.at[q], (peers1[j - 1], b)).wait_recv()
+    for j, p in enumerate([c] + peers1):
+        q = lax.rem(pos1 + j, size1)
+        remote(lsend, fbuf.at[size1 + q], fs_sem.at[0], fr_sem.at[size1 + q], (p, down)).wait_recv()
+    part = fbuf[0]
+    for g in range(1, 2 * size1):
+        part = part + fbuf[g]
+
+    if size2 > 1:
+        sbuf[pos2] = part
+        for j, p in enumerate(peers2):
+            cp = remote(sbuf.at[pos2], sbuf.at[pos2], ss_sem.at[j], sr_sem.at[pos2], (p, b))
+            cp.start()
+            sent.append(cp)
+        for j in range(1, size2):
+            src_pos = lax.rem(pos2 + size2 - j, size2)
+            remote(sbuf.at[src_pos], sbuf.at[src_pos], ss_sem.at[0], sr_sem.at[src_pos], (peers2[-j], b)).wait_recv()
+        part = sbuf[0]
+        for g in range(1, size2):
+            part = part + sbuf[g]
+
+    tot_buf[mine] = part
+    cp = remote(tot_buf.at[mine], tot_buf.at[mine], s_sem.at[2], r_sem.at[2], (mate, b))
+    cp.start()
+    sent.append(cp)
+    remote(tot_buf.at[theirs], tot_buf.at[theirs], s_sem.at[2], r_sem.at[2], (mate, b)).wait_recv()
+    tot_out[...] = tot_buf[...]
+    for cp in sent:
+        cp.wait_send()
+
+
+def final_exchange(tile_block, push, vel_free, n_contact, n_body):
+    gx, gy = contact_groups(n_contact)
+    blocks, width = vel_free.shape
+    half = blocks // 2
+    vspec = pl.BlockSpec(memory_space=pltpu.VMEM)
+    sspec = pl.BlockSpec(memory_space=pltpu.SMEM)
+    scratch = [
+        pltpu.VMEM((blocks, width), jnp.float32),
+        pltpu.VMEM((blocks, width), jnp.float32),
+        pltpu.VMEM((2, half, width), jnp.float32),
+        pltpu.VMEM((2 * gx, half, width), jnp.float32),
+        pltpu.VMEM((half, width), jnp.float32),
+        pltpu.VMEM((gy, half, width), jnp.float32),
+        pltpu.VMEM((blocks, width), jnp.float32),
+        pltpu.SemaphoreType.DMA((3,)),
+        pltpu.SemaphoreType.DMA((3,)),
+        pltpu.SemaphoreType.DMA((2 * gx,)),
+        pltpu.SemaphoreType.DMA((2 * gx,)),
+        pltpu.SemaphoreType.DMA((max(gy - 1, 1),)),
+        pltpu.SemaphoreType.DMA((gy,)),
+    ]
+    return pl.pallas_call(
+        functools.partial(final_kernel, n_contact, n_body),
+        out_shape=jax.ShapeDtypeStruct((blocks, width), jnp.float32),
+        in_specs=[sspec, vspec],
+        out_specs=vspec,
+        scratch_shapes=scratch,
+        compiler_params=pltpu.CompilerParams(collective_id=1, has_side_effects=True),
+    )(tile_block, push)
+
+
 def per_device(
     n_contact, n_body,
     jacobian, tile_block, tile_count, vel_free, inv_mass, bias, step_scale, friction, impulse_start,
@@ -367,7 +492,7 @@
         rows = dual_exchange(tile_block.T, pushes(lam), vel_free, inv_mass, n_contact, n_body)
         rel = jnp.einsum("tkbc,ktb->tc", jacobian, rows, preferred_element_type=jnp.float32) + bias
         lam = project(lam - step_scale * rel, friction, contacts) * mask
-    total = sweep_exchange(tile_block.T, pushes(lam), vel_free, inv_mass, n_contact, n_body, True)
+    total = final_exchange(tile_block.T, pushes(lam), vel_free, n_contact, n_body)
     velocity = vel_free + inv_mass * total
     return (lam, velocity)
 

time: 92.7 us -> 93.6 us (level)
  no operation moved by 1% of the time
where the time goes in v12:
time: 93.6 us; the launch traced here: 93 us
  Pallas kernels  57.6 us (62%)
  matrix products  28.8 us (31%)
  other arithmetic  3.21 us (3%)
  local copies, waits for them, and re-layouts  1.97 us (2%)
  between operations  1.4 us (1%)
    pallas_call x2, Pallas kernels, dual_exchange(): pl.pallas_call(functools.partial(dual_kernel, n_contact, n_body), out_sha...  41.1 us
    dot_general x3, matrix products, pushes(): jnp.einsum('tkbc,tc->ktb', jacobian, lamb, preferred_element_type=jnp.flo...  18.7 us
    pallas_call x1, Pallas kernels, final_exchange(): pl.pallas_call(functools.partial(final_kernel, n_contact, n_body), out_sh...  16.5 us
    dot_general x2, matrix products, per_device(): jnp.einsum('tkbc,ktb->tc', jacobian, rows, preferred_element_type=jnp.flo...  10.2 us
    dot_general x3, local copies, waits for them, and re-layouts, pushes(): jnp.einsum('tkbc,tc->ktb', jacobian, lamb, preferred_element_type=jnp.flo...  1.94 us

profile of v12, /device:TPU:1, one launch (start us, length us, event | category | flops | bytes accessed | tf_op | source)
XLA Modules:
  0.0 93.0 jit_solution(4364195092027920947)
XLA Ops:
  1.3 0.8 fusion.16
  2.1 0.0 copy-start.2
  2.1 0.0 copy-start.3
  2.1 0.0 copy-start.4
  2.1 0.0 copy-start.5
  2.1 6.2 %fusion.12 = f32[16,1,2,384]{3,1,2,0:T(1,128)S(1)} fusion(bf16[16,2,384,384]{3,2,1,0:T(8,128)(2,1)} %param.9, bf16[16,384,1,1]{1,0,2,3:T(8,128)(2,1)S(1)} %fusion.16), kind=kOutput, calls=%fused_computation.20 | convolution fusion | flops 9437184 | bytes 9498624 | tf_op jit(solution)/shard_map/tkbc,tc->ktb/dot_general | solution.py:488
  8.4 0.6 copy.38
  9.0 24.5 %shard_map.104 = bf16[2,16,384]{2,1,0:T(8,128)(2,1)} custom-call(s32[2,16]{1,0:T(2,128)} %bitcast.48, f32[2,16,384]{2,1,0:T(8,128)} %bitcast.46, f32[32,384]{1,0:T(8,128)} %refs_2_.3, f32[32,384]{1,0:T(8,128)} %refs_3_.3), custom_call_target="tpu_custom_call" | custom-call | tf_op jit(solution)/shard_map/pallas_call | solution.py:342
  33.5 5.1 %fusion.2 = f32[16,1,384,1]{2,1,3,0:T(1,128)S(1)} fusion(bf16[16,2,384,384]{3,2,1,0:T(8,128)(2,1)} %param.9, bf16[2,16,384,1]{2,1,0,3:T(8,128)(2,1)} %bitcast.43), kind=kOutput, calls=%fused_computation.4 | convolution fusion | flops 9437184 | bytes 9486336 | tf_op jit(solution)/shard_map/tkbc,ktb->tc/dot_general | solution.py:493
  38.6 0.0 copy-done.2
  38.6 0.0 copy-done.3
  38.6 0.0 copy-done.4
  38.6 0.1 fusion.7
  38.7 0.0 copy-done.5
  38.8 0.1 fusion.15
  38.8 6.2 %fusion.10 = f32[16,1,2,384]{3,1,2,0:T(1,128)S(1)} fusion(bf16[16,2,384,384]{3,2,1,0:T(8,128)(2,1)} %param.9, bf16[16,384,1,1]{1,0,2,3:T(8,128)(2,1)S(1)} %fusion.15), kind=kOutput, calls=%fused_computation.18 | convolution fusion | flops 9437184 | bytes 9498624 | tf_op jit(solution)/shard_map/tkbc,tc->ktb/dot_general | solution.py:488
  45.0 0.6 copy.37
  45.7 16.6 %shard_map.105 = bf16[2,16,384]{2,1,0:T(8,128)(2,1)} custom-call(s32[2,16]{1,0:T(2,128)} %bitcast.49, f32[2,16,384]{2,1,0:T(8,128)} %bitcast.47, f32[32,384]{1,0:T(8,128)} %refs_2_.3, f32[32,384]{1,0:T(8,128)} %refs_3_.3), custom_call_target="tpu_custom_call" | custom-call | tf_op jit(solution)/shard_map/pallas_call | solution.py:342
  62.3 0.0 copy-start
  62.3 0.0 copy-start.1
  62.3 5.1 %fusion = f32[16,1,384,1]{2,1,3,0:T(1,128)S(1)} fusion(bf16[16,2,384,384]{3,2,1,0:T(8,128)(2,1)} %param.9, bf16[2,16,384,1]{2,1,0,3:T(8,128)(2,1)} %bitcast.44), kind=kOutput, calls=%fused_computation.1 | convolution fusion | flops 9437184 | bytes 9486336 | tf_op jit(solution)/shard_map/tkbc,ktb->tc/dot_general | solution.py:493
  67.4 0.1 fusion.5
  67.5 0.7 convert_bitcast_fusion
  68.2 6.2 %fusion.8 = f32[16,1,2,384]{3,1,2,0:T(1,128)S(1)} fusion(bf16[16,2,384,384]{3,2,1,0:T(8,128)(2,1)} %param.9, bf16[16,384,1,1]{1,0,2,3:T(8,128)(2,1)S(1)} %get-tuple-element.2), kind=kOutput, calls=%fused_computation.16 | convolution fusion | flops 9437184 | bytes 9498624 | tf_op jit(solution)/shard_map/tkbc,tc->ktb/dot_general | solution.py:488
  74.4 0.6 copy.36
  75.1 16.5 %shard_map.106 = f32[32,384]{1,0:T(8,128)} custom-call(s32[2,16]{1,0:T(2,128)} %bitcast.50, f32[2,16,384]{2,1,0:T(8,128)} %bitcast.45), custom_call_target="tpu_custom_call" | custom-call | tf_op jit(solution)/shard_map/pallas_call | solution.py:467
  91.6 0.0 copy-done
  91.6 0.0 copy-done.1
  91.6 1.4 %multiply_add_fusion = f32[32,384]{1,0:T(8,128)} fusion(f32[32,384]{1,0:T(8,128)S(1)} %copy-done, f32[32,384]{1,0:T(8,128)S(1)} %copy-done.1, f32[32,384]{1,0:T(8,128)} %shard_map.106), kind=kLoop, calls=%fused_computation.7 | loop fusion | flops 24576 | bytes 196608 | tf_op jit(solution)/shard_map/add | solution.py:496
  (5 shorter events, 0.1 us)
Async XLA Ops:
  2.1 36.5 %copy-start.2 = (f32[16,384]{1,0:T(8,128)S(1)}, f32[16,384]{1,0:T(8,128)}, u32[]{:S(2)}) copy-start(f32[16,384]{1,0:T(8,128)} %param.17) | copy-start | bytes 73732
  2.1 36.5 %copy-start.3 = (f32[16,384]{1,0:T(8,128)S(1)}, f32[16,384]{1,0:T(8,128)}, u32[]{:S(2)}) copy-start(f32[16,384]{1,0:T(8,128)} %param.15) | copy-start | bytes 73732
  2.1 36.5 %copy-start.4 = (f32[16,384]{1,0:T(8,128)S(1)}, f32[16,384]{1,0:T(8,128)}, u32[]{:S(2)}) copy-start(f32[16,384]{1,0:T(8,128)} %param.14) | copy-start | bytes 73732
  2.1 36.6 %copy-start.5 = (f32[16,128]{1,0:T(8,128)S(1)}, f32[16,128]{1,0:T(8,128)}, u32[]{:S(2)}) copy-start(f32[16,128]{1,0:T(8,128)} %param.16) | copy-start | bytes 24580
  62.3 29.3 %copy-start = (f32[32,384]{1,0:T(8,128)S(1)}, f32[32,384]{1,0:T(8,128)}, u32[]{:S(2)}) copy-start(f32[32,384]{1,0:T(8,128)} %refs_2_.3) | copy-start | bytes 147460
  62.3 29.3 %copy-start.1 = (f32[32,384]{1,0:T(8,128)S(1)}, f32[32,384]{1,0:T(8,128)}, u32[]{:S(2)}) copy-start(f32[32,384]{1,0:T(8,128)} %refs_3_.3) | copy-start | bytes 147460

commit v13 on v11

--- a/solution.py
+++ b/solution.py
@@ -35,13 +35,16 @@
     return rest // gy, gy
 
 
-def scatter_rows(tb_ref, column, push_ref, blocks):
-    tiles = push_ref.shape[1]
+def scatter_rows(tb_ref, column, push_ref, blocks, tile_major=False):
+    tiles = push_ref.shape[0] if tile_major else push_ref.shape[1]
     width = push_ref.shape[2]
     slot = lax.broadcasted_iota(jnp.int32, (blocks, width), 0)
     acc = None
     for t in range(tiles):
-        row = push_ref[column, t : t + 1, :]
+        if tile_major:
+            row = push_ref[t, column : column + 1, :]
+        else:
+            row = push_ref[column, t : t + 1, :]
         term = jnp.where(slot == tb_ref[column, t], row, 0.0)
         acc = term if acc is None else acc + term
     return acc
@@ -78,8 +81,8 @@
     barrier = pltpu.get_barrier_semaphore()
     for dev in greet:
         pl.semaphore_signal(barrier, inc=1, device_id=dev, device_id_type=MESH)
-    later_buf[...] = scatter_rows(tb_ref, 1, push_ref, blocks)
-    own_buf[...] = scatter_rows(tb_ref, 0, push_ref, blocks)
+    later_buf[...] = scatter_rows(tb_ref, 1, push_ref, blocks, last)
+    own_buf[...] = scatter_rows(tb_ref, 0, push_ref, blocks, last)
     pl.semaphore_wait(barrier, len(greet))
 
     def remote(src, dst, send, recv, dev):
@@ -162,7 +165,7 @@
 def sweep_exchange(tile_block, push, vel_free, inv_mass, n_contact, n_body, last):
     gx, gy = contact_groups(n_contact)
     blocks, width = vel_free.shape
-    tiles = push.shape[1]
+    tiles = push.shape[0] if last else push.shape[1]
     half = blocks // 2
     vspec = pl.BlockSpec(memory_space=pltpu.VMEM)
     sspec = pl.BlockSpec(memory_space=pltpu.SMEM)
@@ -367,7 +370,9 @@
         rows = dual_exchange(tile_block.T, pushes(lam), vel_free, inv_mass, n_contact, n_body)
         rel = jnp.einsum("tkbc,ktb->tc", jacobian, rows, preferred_element_type=jnp.float32) + bias
         lam = project(lam - step_scale * rel, friction, contacts) * mask
-    total = sweep_exchange(tile_block.T, pushes(lam), vel_free, inv_mass, n_contact, n_body, True)
+    lamb = lam.astype(jnp.bfloat16).astype(jnp.float32)
+    push = jnp.sum(jacobian.astype(jnp.float32) * lamb[:, None, None, :], axis=-1)
+    total = sweep_exchange(tile_block.T, push, vel_free, inv_mass, n_contact, n_body, True)
     velocity = vel_free + inv_mass * total
     return (lam, velocity)
 

time: 92.7 us -> 92.1 us (level)
  other arithmetic: 3.21 us -> 9.5 us
  matrix products: 28.8 us -> 22.6 us
    reduce_sum x0 -> x1, other arithmetic: none -> 6.29 us  [per_device(): jnp.sum(jacobian.astype(jnp.float32) * lamb[:, None, None, :], axis=-1)]
    dot_general x3 -> x2, matrix products: 18.7 us -> 12.4 us  [pushes(): jnp.einsum('tkbc,tc->ktb', jacobian, lamb, preferred_element_type=jnp.flo...]
    dot_general x3 -> x2, local copies, waits for them, and re-layouts: 1.94 us -> 1.29 us  [pushes(): jnp.einsum('tkbc,tc->ktb', jacobian, lamb, preferred_element_type=jnp.flo...]
where the time goes in v13:
time: 92.1 us; the launch traced here: 91.6 us
  Pallas kernels  56.8 us (62%)
  matrix products  22.6 us (25%)
  other arithmetic  9.5 us (10%)
  between operations  1.4 us (2%)
  local copies, waits for them, and re-layouts  1.32 us (1%)
    pallas_call x2, Pallas kernels, dual_exchange(): pl.pallas_call(functools.partial(dual_kernel, n_contact, n_body), out_sha...  41.2 us
    pallas_call x1, Pallas kernels, sweep_exchange(): pl.pallas_call(functools.partial(sweep_kernel, n_contact, n_body, last),...  15.6 us
    dot_general x2, matrix products, pushes(): jnp.einsum('tkbc,tc->ktb', jacobian, lamb, preferred_element_type=jnp.flo...  12.4 us
    dot_general x2, matrix products, per_device(): jnp.einsum('tkbc,ktb->tc', jacobian, rows, preferred_element_type=jnp.flo...  10.2 us
    reduce_sum x1, other arithmetic, per_device(): jnp.sum(jacobian.astype(jnp.float32) * lamb[:, None, None, :], axis=-1)  6.29 us

profile of v13, /device:TPU:1, one launch (start us, length us, event | category | flops | bytes accessed | tf_op | source)
XLA Modules:
  0.0 91.6 jit_solution(7684565901965833230)
XLA Ops:
  1.3 0.8 fusion.14
  2.1 0.0 copy-start.2
  2.1 0.0 copy-start.3
  2.1 0.0 copy-start.4
  2.1 0.0 copy-start.5
  2.1 6.2 %fusion.10 = f32[16,1,2,384]{3,1,2,0:T(1,128)S(1)} fusion(bf16[16,2,384,384]{3,2,1,0:T(8,128)(2,1)} %param.9, bf16[16,384,1,1]{1,0,2,3:T(8,128)(2,1)S(1)} %fusion.14), kind=kOutput, calls=%fused_computation.18 | convolution fusion | flops 9437184 | bytes 9498624 | tf_op jit(solution)/shard_map/tkbc,tc->ktb/dot_general | solution.py:366
  8.4 0.6 copy.32
  9.0 24.5 %shard_map.104 = bf16[2,16,384]{2,1,0:T(8,128)(2,1)} custom-call(s32[2,16]{1,0:T(2,128)} %bitcast.39, f32[2,16,384]{2,1,0:T(8,128)} %bitcast.37, f32[32,384]{1,0:T(8,128)} %refs_2_.3, f32[32,384]{1,0:T(8,128)} %refs_3_.3), custom_call_target="tpu_custom_call" | custom-call | tf_op jit(solution)/shard_map/pallas_call | solution.py:345
  33.6 5.1 %fusion.2 = f32[16,1,384,1]{2,1,3,0:T(1,128)S(1)} fusion(bf16[16,2,384,384]{3,2,1,0:T(8,128)(2,1)} %param.9, bf16[2,16,384,1]{2,1,0,3:T(8,128)(2,1)} %bitcast.35), kind=kOutput, calls=%fused_computation.4 | convolution fusion | flops 9437184 | bytes 9486336 | tf_op jit(solution)/shard_map/tkbc,ktb->tc/dot_general | solution.py:371
  38.6 0.0 copy-done.2
  38.6 0.0 copy-done.3
  38.6 0.0 copy-done.4
  38.6 0.1 fusion.7
  38.7 0.0 copy-done.5
  38.8 0.1 fusion.13
  38.8 6.2 %fusion.8 = f32[16,1,2,384]{3,1,2,0:T(1,128)S(1)} fusion(bf16[16,2,384,384]{3,2,1,0:T(8,128)(2,1)} %param.9, bf16[16,384,1,1]{1,0,2,3:T(8,128)(2,1)S(1)} %fusion.13), kind=kOutput, calls=%fused_computation.16 | convolution fusion | flops 9437184 | bytes 9498624 | tf_op jit(solution)/shard_map/tkbc,tc->ktb/dot_general | solution.py:366
  45.0 0.6 copy.31
  45.7 16.6 %shard_map.105 = bf16[2,16,384]{2,1,0:T(8,128)(2,1)} custom-call(s32[2,16]{1,0:T(2,128)} %bitcast.40, f32[2,16,384]{2,1,0:T(8,128)} %bitcast.38, f32[32,384]{1,0:T(8,128)} %refs_2_.3, f32[32,384]{1,0:T(8,128)} %refs_3_.3), custom_call_target="tpu_custom_call" | custom-call | tf_op jit(solution)/shard_map/pallas_call | solution.py:345
  62.3 0.0 copy-start
  62.3 0.0 copy-start.1
  62.3 5.1 %fusion = f32[16,1,384,1]{2,1,3,0:T(1,128)S(1)} fusion(bf16[16,2,384,384]{3,2,1,0:T(8,128)(2,1)} %param.9, bf16[2,16,384,1]{2,1,0,3:T(8,128)(2,1)} %bitcast.36), kind=kOutput, calls=%fused_computation.1 | convolution fusion | flops 9437184 | bytes 9486336 | tf_op jit(solution)/shard_map/tkbc,ktb->tc/dot_general | solution.py:371
  67.4 0.1 fusion.5
  67.6 0.7 convert_convert_fusion
  68.2 6.3 %multiply_reduce_fusion.refs_1_ = f32[16,2,384]{2,1,0:T(2,128)} fusion(bf16[16,2,384,384]{3,2,1,0:T(8,128)(2,1)} %param.9, f32[16,384]{1,0:T(8,128)S(1)} %get-tuple-element.2), kind=kLoop, calls=%fused_computation | loop fusion | flops 14143488 | bytes 9510912 | tf_op jit(solution)/shard_map/reduce_sum | solution.py:374
  74.5 15.6 %shard_map.106 = f32[32,384]{1,0:T(8,128)} custom-call(s32[2,16]{1,0:T(2,128)} %bitcast.41, f32[16,2,384]{2,1,0:T(2,128)} %multiply_reduce_fusion.refs_1_), custom_call_target="tpu_custom_call" | custom-call | tf_op jit(solution)/shard_map/pallas_call | solution.py:199
  90.2 0.0 copy-done
  90.2 0.0 copy-done.1
  90.2 1.4 %multiply_add_fusion = f32[32,384]{1,0:T(8,128)} fusion(f32[32,384]{1,0:T(8,128)S(1)} %copy-done, f32[32,384]{1,0:T(8,128)S(1)} %copy-done.1, f32[32,384]{1,0:T(8,128)} %shard_map.106), kind=kLoop, calls=%fused_computation.7 | loop fusion | flops 24576 | bytes 196608 | tf_op jit(solution)/shard_map/add | solution.py:376
  (5 shorter events, 0.1 us)
Async XLA Ops:
  2.1 36.5 %copy-start.2 = (f32[16,384]{1,0:T(8,128)S(1)}, f32[16,384]{1,0:T(8,128)}, u32[]{:S(2)}) copy-start(f32[16,384]{1,0:T(8,128)} %param.17) | copy-start | bytes 73732
  2.1 36.5 %copy-start.3 = (f32[16,384]{1,0:T(8,128)S(1)}, f32[16,384]{1,0:T(8,128)}, u32[]{:S(2)}) copy-start(f32[16,384]{1,0:T(8,128)} %param.15) | copy-start | bytes 73732
  2.1 36.5 %copy-start.4 = (f32[16,384]{1,0:T(8,128)S(1)}, f32[16,384]{1,0:T(8,128)}, u32[]{:S(2)}) copy-start(f32[16,384]{1,0:T(8,128)} %param.14) | copy-start | bytes 73732
  2.1 36.6 %copy-start.5 = (f32[16,128]{1,0:T(8,128)S(1)}, f32[16,128]{1,0:T(8,128)}, u32[]{:S(2)}) copy-start(f32[16,128]{1,0:T(8,128)} %param.16) | copy-start | bytes 24580
  62.3 27.9 %copy-start = (f32[32,384]{1,0:T(8,128)S(1)}, f32[32,384]{1,0:T(8,128)}, u32[]{:S(2)}) copy-start(f32[32,384]{1,0:T(8,128)} %refs_2_.3) | copy-start | bytes 147460
  62.3 27.9 %copy-start.1 = (f32[32,384]{1,0:T(8,128)S(1)}, f32[32,384]{1,0:T(8,128)}, u32[]{:S(2)}) copy-start(f32[32,384]{1,0:T(8,128)} %refs_3_.3) | copy-start | bytes 147460

commit v14 on v13

--- a/solution.py
+++ b/solution.py
@@ -115,7 +115,8 @@
         if size == 1:
             continue
         buf[pos] = part
-        for j, p in enumerate(peers):
+        for j in sorted(range(size - 1), key=lambda j: -min(j + 1, size - 1 - j)):
+            p = peers[j]
             cp = remote(buf.at[pos], buf.at[pos], ssem.at[j], rsem.at[pos], (p, b))
             cp.start()
             sent.append(cp)
@@ -287,7 +288,8 @@
         if size == 1:
             continue
         buf[pos] = part
-        for j, p in enumerate(peers):
+        for j in sorted(range(size - 1), key=lambda j: -min(j + 1, size - 1 - j)):
+            p = peers[j]
             cp = remote(buf.at[pos], buf.at[pos], ssem.at[j], rsem.at[pos], (p, b))
             cp.start()
             sent.append(cp)

time: 92.1 us -> 91.3 us (level)
  no operation moved by 1% of the time
where the time goes in v14:
time: 91.3 us; the launch traced here: 90.7 us
  Pallas kernels  55.9 us (61%)
  matrix products  22.6 us (25%)
  other arithmetic  9.5 us (10%)
  between operations  1.4 us (2%)
  local copies, waits for them, and re-layouts  1.32 us (1%)
    pallas_call x2, Pallas kernels, dual_exchange(): pl.pallas_call(functools.partial(dual_kernel, n_contact, n_body), out_sha...  40.3 us
    pallas_call x1, Pallas kernels, sweep_exchange(): pl.pallas_call(functools.partial(sweep_kernel, n_contact, n_body, last),...  15.6 us
    dot_general x2, matrix products, pushes(): jnp.einsum('tkbc,tc->ktb', jacobian, lamb, preferred_element_type=jnp.flo...  12.4 us
    dot_general x2, matrix products, per_device(): jnp.einsum('tkbc,ktb->tc', jacobian, rows, preferred_element_type=jnp.flo...  10.2 us
    reduce_sum x1, other arithmetic, per_device(): jnp.sum(jacobian.astype(jnp.float32) * lamb[:, None, None, :], axis=-1)  6.29 us

profile of v14, /device:TPU:1, one launch (start us, length us, event | category | flops | bytes accessed | tf_op | source)
XLA Modules:
  0.0 90.7 jit_solution(10582048035667119038)
XLA Ops:
  1.3 0.8 fusion.14
  2.1 0.0 copy-start.2
  2.1 0.0 copy-start.3
  2.1 0.0 copy-start.4
  2.1 0.0 copy-start.5
  2.1 6.2 %fusion.10 = f32[16,1,2,384]{3,1,2,0:T(1,128)S(1)} fusion(bf16[16,2,384,384]{3,2,1,0:T(8,128)(2,1)} %param.9, bf16[16,384,1,1]{1,0,2,3:T(8,128)(2,1)S(1)} %fusion.14), kind=kOutput, calls=%fused_computation.18 | convolution fusion | flops 9437184 | bytes 9498624 | tf_op jit(solution)/shard_map/tkbc,tc->ktb/dot_general | solution.py:368
  8.4 0.6 copy.32
  9.0 24.2 %shard_map.104 = bf16[2,16,384]{2,1,0:T(8,128)(2,1)} custom-call(s32[2,16]{1,0:T(2,128)} %bitcast.39, f32[2,16,384]{2,1,0:T(8,128)} %bitcast.37, f32[32,384]{1,0:T(8,128)} %refs_2_.3, f32[32,384]{1,0:T(8,128)} %refs_3_.3), custom_call_target="tpu_custom_call" | custom-call | tf_op jit(solution)/shard_map/pallas_call | solution.py:347
  33.2 5.1 %fusion.2 = f32[16,1,384,1]{2,1,3,0:T(1,128)S(1)} fusion(bf16[16,2,384,384]{3,2,1,0:T(8,128)(2,1)} %param.9, bf16[2,16,384,1]{2,1,0,3:T(8,128)(2,1)} %bitcast.35), kind=kOutput, calls=%fused_computation.4 | convolution fusion | flops 9437184 | bytes 9486336 | tf_op jit(solution)/shard_map/tkbc,ktb->tc/dot_general | solution.py:373
  38.3 0.0 copy-done.2
  38.3 0.0 copy-done.3
  38.3 0.0 copy-done.4
  38.3 0.1 fusion.7
  38.4 0.0 copy-done.5
  38.4 0.1 fusion.13
  38.5 6.2 %fusion.8 = f32[16,1,2,384]{3,1,2,0:T(1,128)S(1)} fusion(bf16[16,2,384,384]{3,2,1,0:T(8,128)(2,1)} %param.9, bf16[16,384,1,1]{1,0,2,3:T(8,128)(2,1)S(1)} %fusion.13), kind=kOutput, calls=%fused_computation.16 | convolution fusion | flops 9437184 | bytes 9498624 | tf_op jit(solution)/shard_map/tkbc,tc->ktb/dot_general | solution.py:368
  44.7 0.6 copy.31
  45.3 16.1 %shard_map.105 = bf16[2,16,384]{2,1,0:T(8,128)(2,1)} custom-call(s32[2,16]{1,0:T(2,128)} %bitcast.40, f32[2,16,384]{2,1,0:T(8,128)} %bitcast.38, f32[32,384]{1,0:T(8,128)} %refs_2_.3, f32[32,384]{1,0:T(8,128)} %refs_3_.3), custom_call_target="tpu_custom_call" | custom-call | tf_op jit(solution)/shard_map/pallas_call | solution.py:347
  61.5 0.0 copy-start
  61.5 0.0 copy-start.1
  61.5 5.1 %fusion = f32[16,1,384,1]{2,1,3,0:T(1,128)S(1)} fusion(bf16[16,2,384,384]{3,2,1,0:T(8,128)(2,1)} %param.9, bf16[2,16,384,1]{2,1,0,3:T(8,128)(2,1)} %bitcast.36), kind=kOutput, calls=%fused_computation.1 | convolution fusion | flops 9437184 | bytes 9486336 | tf_op jit(solution)/shard_map/tkbc,ktb->tc/dot_general | solution.py:373
  66.6 0.1 fusion.5
  66.7 0.7 convert_convert_fusion
  67.4 6.3 %multiply_reduce_fusion.refs_1_ = f32[16,2,384]{2,1,0:T(2,128)} fusion(bf16[16,2,384,384]{3,2,1,0:T(8,128)(2,1)} %param.9, f32[16,384]{1,0:T(8,128)S(1)} %get-tuple-element.2), kind=kLoop, calls=%fused_computation | loop fusion | flops 14143488 | bytes 9510912 | tf_op jit(solution)/shard_map/reduce_sum | solution.py:376
  73.7 15.6 %shard_map.106 = f32[32,384]{1,0:T(8,128)} custom-call(s32[2,16]{1,0:T(2,128)} %bitcast.41, f32[16,2,384]{2,1,0:T(2,128)} %multiply_reduce_fusion.refs_1_), custom_call_target="tpu_custom_call" | custom-call | tf_op jit(solution)/shard_map/pallas_call | solution.py:200
  89.3 0.0 copy-done
  89.3 0.0 copy-done.1
  89.3 1.4 %multiply_add_fusion = f32[32,384]{1,0:T(8,128)} fusion(f32[32,384]{1,0:T(8,128)S(1)} %copy-done, f32[32,384]{1,0:T(8,128)S(1)} %copy-done.1, f32[32,384]{1,0:T(8,128)} %shard_map.106), kind=kLoop, calls=%fused_computation.7 | loop fusion | flops 24576 | bytes 196608 | tf_op jit(solution)/shard_map/add | solution.py:378
  (5 shorter events, 0.1 us)
Async XLA Ops:
  2.1 36.2 %copy-start.2 = (f32[16,384]{1,0:T(8,128)S(1)}, f32[16,384]{1,0:T(8,128)}, u32[]{:S(2)}) copy-start(f32[16,384]{1,0:T(8,128)} %param.17) | copy-start | bytes 73732
  2.1 36.2 %copy-start.3 = (f32[16,384]{1,0:T(8,128)S(1)}, f32[16,384]{1,0:T(8,128)}, u32[]{:S(2)}) copy-start(f32[16,384]{1,0:T(8,128)} %param.15) | copy-start | bytes 73732
  2.1 36.2 %copy-start.4 = (f32[16,384]{1,0:T(8,128)S(1)}, f32[16,384]{1,0:T(8,128)}, u32[]{:S(2)}) copy-start(f32[16,384]{1,0:T(8,128)} %param.14) | copy-start | bytes 73732
  2.1 36.3 %copy-start.5 = (f32[16,128]{1,0:T(8,128)S(1)}, f32[16,128]{1,0:T(8,128)}, u32[]{:S(2)}) copy-start(f32[16,128]{1,0:T(8,128)} %param.16) | copy-start | bytes 24580
  61.5 27.8 %copy-start = (f32[32,384]{1,0:T(8,128)S(1)}, f32[32,384]{1,0:T(8,128)}, u32[]{:S(2)}) copy-start(f32[32,384]{1,0:T(8,128)} %refs_2_.3) | copy-start | bytes 147460
  61.5 27.8 %copy-start.1 = (f32[32,384]{1,0:T(8,128)S(1)}, f32[32,384]{1,0:T(8,128)}, u32[]{:S(2)}) copy-start(f32[32,384]{1,0:T(8,128)} %refs_3_.3) | copy-start | bytes 147460

commit v15 on v14

--- a/solution.py
+++ b/solution.py
@@ -253,18 +253,13 @@
         (later_buf.at[mine], (c, up)),
         (later_buf.at[theirs], (mate, up)),
         (later_buf.at[theirs], (mate, b)),
-    )
-    for k, (src, dev) in enumerate(plan):
-        cp = remote(src, recv6.at[k], s_sem.at[k], r_sem.at[k], dev)
-        cp.start()
-        sent.append(cp)
-    plan = (
         (own_buf.at[mine], (c, down)),
         (own_buf.at[theirs], (mate, down)),
         (own_buf.at[theirs], (mate, b)),
     )
-    for k, (src, dev) in enumerate(plan):
-        cp = remote(src, recv6.at[3 + k], s_sem.at[3 + k], r_sem.at[3 + k], dev)
+    for k in (0, 1, 3, 4, 2, 5):
+        src, dev = plan[k]
+        cp = remote(src, recv6.at[k], s_sem.at[k], r_sem.at[k], dev)
         cp.start()
         sent.append(cp)
     vcp = remote(vn_send, vnext_ref, s_sem.at[8], r_sem.at[8], (c, down))

time: 91.3 us -> 91.3 us (level)
  no operation moved by 1% of the time
where the time goes in v15:
time: 91.3 us; the launch traced here: 90.7 us
  Pallas kernels  55.9 us (61%)
  matrix products  22.6 us (25%)
  other arithmetic  9.5 us (10%)
  between operations  1.4 us (2%)
  local copies, waits for them, and re-layouts  1.32 us (1%)
    pallas_call x2, Pallas kernels, dual_exchange(): pl.pallas_call(functools.partial(dual_kernel, n_contact, n_body), out_sha...  40.3 us
    pallas_call x1, Pallas kernels, sweep_exchange(): pl.pallas_call(functools.partial(sweep_kernel, n_contact, n_body, last),...  15.6 us
    dot_general x2, matrix products, pushes(): jnp.einsum('tkbc,tc->ktb', jacobian, lamb, preferred_element_type=jnp.flo...  12.4 us
    dot_general x2, matrix products, per_device(): jnp.einsum('tkbc,ktb->tc', jacobian, rows, preferred_element_type=jnp.flo...  10.2 us
    reduce_sum x1, other arithmetic, per_device(): jnp.sum(jacobian.astype(jnp.float32) * lamb[:, None, None, :], axis=-1)  6.29 us

profile of v15, /device:TPU:1, one launch (start us, length us, event | category | flops | bytes accessed | tf_op | source)
XLA Modules:
  0.0 90.7 jit_solution(5328897633345246549)
XLA Ops:
  1.3 0.8 fusion.14
  2.1 0.0 copy-start.2
  2.1 0.0 copy-start.3
  2.1 0.0 copy-start.4
  2.1 0.0 copy-start.5
  2.1 6.2 %fusion.10 = f32[16,1,2,384]{3,1,2,0:T(1,128)S(1)} fusion(bf16[16,2,384,384]{3,2,1,0:T(8,128)(2,1)} %param.9, bf16[16,384,1,1]{1,0,2,3:T(8,128)(2,1)S(1)} %fusion.14), kind=kOutput, calls=%fused_computation.18 | convolution fusion | flops 9437184 | bytes 9498624 | tf_op jit(solution)/shard_map/tkbc,tc->ktb/dot_general | solution.py:363
  8.4 0.6 copy.32
  9.0 24.2 %shard_map.104 = bf16[2,16,384]{2,1,0:T(8,128)(2,1)} custom-call(s32[2,16]{1,0:T(2,128)} %bitcast.39, f32[2,16,384]{2,1,0:T(8,128)} %bitcast.37, f32[32,384]{1,0:T(8,128)} %refs_2_.3, f32[32,384]{1,0:T(8,128)} %refs_3_.3), custom_call_target="tpu_custom_call" | custom-call | tf_op jit(solution)/shard_map/pallas_call | solution.py:342
  33.2 5.1 %fusion.2 = f32[16,1,384,1]{2,1,3,0:T(1,128)S(1)} fusion(bf16[16,2,384,384]{3,2,1,0:T(8,128)(2,1)} %param.9, bf16[2,16,384,1]{2,1,0,3:T(8,128)(2,1)} %bitcast.35), kind=kOutput, calls=%fused_computation.4 | convolution fusion | flops 9437184 | bytes 9486336 | tf_op jit(solution)/shard_map/tkbc,ktb->tc/dot_general | solution.py:368
  38.3 0.0 copy-done.2
  38.3 0.0 copy-done.3
  38.3 0.0 copy-done.4
  38.3 0.1 fusion.7
  38.4 0.0 copy-done.5
  38.4 0.1 fusion.13
  38.5 6.2 %fusion.8 = f32[16,1,2,384]{3,1,2,0:T(1,128)S(1)} fusion(bf16[16,2,384,384]{3,2,1,0:T(8,128)(2,1)} %param.9, bf16[16,384,1,1]{1,0,2,3:T(8,128)(2,1)S(1)} %fusion.13), kind=kOutput, calls=%fused_computation.16 | convolution fusion | flops 9437184 | bytes 9498624 | tf_op jit(solution)/shard_map/tkbc,tc->ktb/dot_general | solution.py:363
  44.7 0.6 copy.31
  45.3 16.1 %shard_map.105 = bf16[2,16,384]{2,1,0:T(8,128)(2,1)} custom-call(s32[2,16]{1,0:T(2,128)} %bitcast.40, f32[2,16,384]{2,1,0:T(8,128)} %bitcast.38, f32[32,384]{1,0:T(8,128)} %refs_2_.3, f32[32,384]{1,0:T(8,128)} %refs_3_.3), custom_call_target="tpu_custom_call" | custom-call | tf_op jit(solution)/shard_map/pallas_call | solution.py:342
  61.5 0.0 copy-start
  61.5 0.0 copy-start.1
  61.5 5.1 %fusion = f32[16,1,384,1]{2,1,3,0:T(1,128)S(1)} fusion(bf16[16,2,384,384]{3,2,1,0:T(8,128)(2,1)} %param.9, bf16[2,16,384,1]{2,1,0,3:T(8,128)(2,1)} %bitcast.36), kind=kOutput, calls=%fused_computation.1 | convolution fusion | flops 9437184 | bytes 9486336 | tf_op jit(solution)/shard_map/tkbc,ktb->tc/dot_general | solution.py:368
  66.6 0.1 fusion.5
  66.7 0.7 convert_convert_fusion
  67.4 6.3 %multiply_reduce_fusion.refs_1_ = f32[16,2,384]{2,1,0:T(2,128)} fusion(bf16[16,2,384,384]{3,2,1,0:T(8,128)(2,1)} %param.9, f32[16,384]{1,0:T(8,128)S(1)} %get-tuple-element.2), kind=kLoop, calls=%fused_computation | loop fusion | flops 14143488 | bytes 9510912 | tf_op jit(solution)/shard_map/reduce_sum | solution.py:371
  73.7 15.6 %shard_map.106 = f32[32,384]{1,0:T(8,128)} custom-call(s32[2,16]{1,0:T(2,128)} %bitcast.41, f32[16,2,384]{2,1,0:T(2,128)} %multiply_reduce_fusion.refs_1_), custom_call_target="tpu_custom_call" | custom-call | tf_op jit(solution)/shard_map/pallas_call | solution.py:200
  89.3 0.0 copy-done
  89.3 0.0 copy-done.1
  89.3 1.4 %multiply_add_fusion = f32[32,384]{1,0:T(8,128)} fusion(f32[32,384]{1,0:T(8,128)S(1)} %copy-done, f32[32,384]{1,0:T(8,128)S(1)} %copy-done.1, f32[32,384]{1,0:T(8,128)} %shard_map.106), kind=kLoop, calls=%fused_computation.7 | loop fusion | flops 24576 | bytes 196608 | tf_op jit(solution)/shard_map/add | solution.py:373
  (5 shorter events, 0.1 us)
Async XLA Ops:
  2.1 36.2 %copy-start.2 = (f32[16,384]{1,0:T(8,128)S(1)}, f32[16,384]{1,0:T(8,128)}, u32[]{:S(2)}) copy-start(f32[16,384]{1,0:T(8,128)} %param.17) | copy-start | bytes 73732
  2.1 36.2 %copy-start.3 = (f32[16,384]{1,0:T(8,128)S(1)}, f32[16,384]{1,0:T(8,128)}, u32[]{:S(2)}) copy-start(f32[16,384]{1,0:T(8,128)} %param.15) | copy-start | bytes 73732
  2.1 36.2 %copy-start.4 = (f32[16,384]{1,0:T(8,128)S(1)}, f32[16,384]{1,0:T(8,128)}, u32[]{:S(2)}) copy-start(f32[16,384]{1,0:T(8,128)} %param.14) | copy-start | bytes 73732
  2.1 36.3 %copy-start.5 = (f32[16,128]{1,0:T(8,128)S(1)}, f32[16,128]{1,0:T(8,128)}, u32[]{:S(2)}) copy-start(f32[16,128]{1,0:T(8,128)} %param.16) | copy-start | bytes 24580
  61.5 27.8 %copy-start = (f32[32,384]{1,0:T(8,128)S(1)}, f32[32,384]{1,0:T(8,128)}, u32[]{:S(2)}) copy-start(f32[32,384]{1,0:T(8,128)} %refs_2_.3) | copy-start | bytes 147460
  61.5 27.8 %copy-start.1 = (f32[32,384]{1,0:T(8,128)S(1)}, f32[32,384]{1,0:T(8,128)}, u32[]{:S(2)}) copy-start(f32[32,384]{1,0:T(8,128)} %refs_3_.3) | copy-start | bytes 147460
